TPU v7x, 32 devices: a whole 2x2x4 slice. The times are simulated.
32 devices in a mesh: morton: 8 (over y, x, core), lane: 4 (over z).
Axes of the slice: x: 2, y: 2, z: 4, core: 2. Of those that a mesh axis runs over, the one named last changes fastest.
Arguments:
- multipoles: bfloat16 [8, 512, 296], P('morton', 'lane'), may hold values from -6 to 6
- counts: int32 [8, 512], P('morton', 'lane'), may hold values from 1 to 12
- sources: int32 [8, 512, 12], P('morton', 'lane'), may hold values from 0 to 1151, as said below
- relpos: int32 [8, 512, 12], P('morton', 'lane'), may hold values from 0 to 11, as said below
- operators: bfloat16 [12, 296, 296], P('lane'), may hold values from -0.375 to 0.375
- c2e: bfloat16 [296, 296], replicated, may hold values from -0.375 to 0.375
Outputs:
- local_density: float32 [8, 512, 296], P('morton', 'lane')
Inputs may be any that keep to these rules, and one draw needn't show every extreme that they name: `sources`: every live slot names a source box inside the grid of 8 x 4 devices' boxes. `relpos`: the ids of one box's slots are all different.
All inputs are finite; a program needn't handle non-finite values.
Results may differ from a plain program's by a relative error of at most 0.0029.
Values may be sent and summed in bfloat16 or wider, within the bound.
No kernel may reach another device: no remote copies, remote signals or barrier semaphores. Data moves between devices by JAX's collectives and lax.ppermute only.
A program may use at most 64 MiB of HBM per device.

v0:
```python
import functools

import jax
import jax.numpy as jnp
from jax import lax
from jax.experimental import pallas as pl
from jax.experimental.pallas import tpu as pltpu
from jax.sharding import PartitionSpec as P


def pairs_xor(count, mask):
    return [(i, i ^ mask) for i in range(count)]


def pairs_odd(count):
    out = []
    for i in range(1, count - 1, 2):
        out += [(i, i + 1), (i + 1, i)]
    return out


def part_rows(rows, parts):
    return 8 * -(-rows // (8 * parts))


def part_start(rows, size, index):
    return jnp.minimum(index * size, rows - size)


def gather_kernel(boxes, per, lanes, ids, counts, sources, relpos, column, twin, other, own_hbm, c2e_hbm, out, before, c2e_out, own, sems):
    own_copy = pltpu.make_async_copy(own_hbm, own, sems.at[0])
    c2e_copy = pltpu.make_async_copy(c2e_hbm, c2e_out, sems.at[1])
    own_copy.start()
    c2e_copy.start()
    lane_id, seg_id = ids[0], ids[1]
    code = sources[:, 0, :]
    rel = relpos[:, 0, :]
    width = out.shape[2]
    slot = lax.broadcasted_iota(jnp.int32, rel.shape, 0)
    live = slot < counts[...]
    nb = jnp.zeros_like(code)
    for k in range(1, 9):
        nb = nb + (code >= k * boxes).astype(jnp.int32)
    a = (nb >= 3).astype(jnp.int32) + (nb >= 6).astype(jnp.int32)
    b = nb - 3 * a
    offset = code - nb * boxes

    def place(v, odd):
        return jnp.where(v == 1, 0, jnp.where(v == 2 - 2 * odd, 1, 2))

    mapped = (place(a, seg_id % 2) * 3 + place(b, lane_id % 2)) * boxes + offset + 1
    mapped = jnp.where(live, mapped, 0)
    rows = []
    for g in range(lanes):
        for i in range(per):
            wanted = (lane_id ^ g) * per + i
            rows.append(jnp.sum(jnp.where(rel == wanted, mapped, 0), axis=0, keepdims=True) - 1)
    fill = jnp.full((boxes - len(rows), boxes), -1, jnp.int32)
    index = jnp.concatenate(rows + [fill], axis=0).T
    parts = []
    for ref in (column, twin, other):
        for j in range(3):
            parts.append(ref[pl.ds(j * width, width), :])
    table = jnp.concatenate(parts, axis=1)
    spot = lax.broadcasted_iota(jnp.int32, (boxes, 9 * boxes), 1)
    for g in range(lanes):
        picks = []
        for i in range(per):
            at = g * per + i
            picks.append((index[:, at : at + 1] == spot).astype(jnp.float32).astype(jnp.bfloat16))
        picks = jnp.concatenate(picks, axis=0)
        found = lax.dot_general(picks, table, (((1,), (1,)), ((), ())), preferred_element_type=jnp.float32)
        out[g * per : (g + 1) * per] = found.astype(jnp.bfloat16).reshape(per, boxes, width)
    own_copy.wait()
    total = None
    for i in range(per):
        term = jnp.dot(out[i], own[i], preferred_element_type=jnp.float32)
        total = term if total is None else total + term
    before[...] = total
    c2e_copy.wait()


def accumulate(total, picked, group, buffer, per, width):
    for i in range(per):
        term = jnp.dot(picked[group * per + i], buffer[pl.ds(i * width, width), :], preferred_element_type=jnp.float32)
        total = total + term
    return total


def place_part(buffer, rows, size, index, part):
    buffer[pl.ds(pl.multiple_of(part_start(rows, size, index), 8), size), :] = part


def near_kernel(per, width, ids, picked, before, mine, twin, out, buffer):
    rows, size = per * width, mine.shape[0]
    core = ids[1] % 2
    place_part(buffer, rows, size, core, mine[...])
    place_part(buffer, rows, size, 1 - core, twin[...])
    out[...] = accumulate(before[...], picked, 1, buffer, per, width)


def far_kernel(per, width, count, ids, picked, before, c2e, *refs):
    pieces, twins, out, buffer = refs[:count], refs[count : 2 * count], refs[-2], refs[-1]
    rows = per * width
    groups, size = pieces[0].shape[:2]
    total = before[...]
    for k in range(groups):
        view = buffer.at[k]
        for j in range(count):
            place_part(view, rows, size, ids[1] ^ (2 * j), pieces[j][k])
            place_part(view, rows, size, ids[1] ^ (2 * j + 1), twins[j][k])
        total = accumulate(total, picked, k + 2, view, per, width)
    check = total.astype(jnp.bfloat16)
    out[...] = jnp.dot(check, c2e[...], preferred_element_type=jnp.float32).T


def per_device(multipoles, counts, sources, relpos, operators, c2e):
    segs, lanes = lax.axis_size("morton"), lax.axis_size("lane")
    seg_id, lane_id = lax.axis_index("morton"), lax.axis_index("lane")
    boxes, width = multipoles.shape[1:]
    per = operators.shape[0]
    rows = per * width

    block = multipoles[0].T
    flat = operators.reshape(rows, width)
    half, eighth = part_rows(rows, 2), part_rows(rows, segs)
    near = lax.ppermute(block, "lane", pairs_xor(lanes, 1))
    far = lax.ppermute(block, "lane", pairs_odd(lanes))
    small = lax.dynamic_slice_in_dim(flat, part_start(rows, eighth, seg_id), eighth, 0)[None]
    big = lax.dynamic_slice_in_dim(flat, part_start(rows, half, seg_id % 2), half, 0)
    landed = [lax.ppermute(small, "lane", pairs_xor(lanes, k)) for k in range(2, lanes)]
    mine = lax.ppermute(big, "lane", pairs_xor(lanes, 1))

    column = jnp.concatenate([block, near, far], axis=0)
    twin = lax.ppermute(column, "morton", pairs_xor(segs, 1))
    other = lax.ppermute(column, "morton", pairs_odd(segs))

    landed = jnp.concatenate(landed, axis=0)
    pieces = [landed] + [lax.ppermute(landed, "morton", pairs_xor(segs, 2 * j)) for j in range(1, segs // 2)]
    mine_twin = lax.ppermute(mine, "morton", pairs_xor(segs, 1))
    twins = [lax.ppermute(piece, "morton", pairs_xor(segs, 1)) for piece in pieces]

    smem = pl.BlockSpec(memory_space=pltpu.SMEM)
    vmem = pl.BlockSpec(memory_space=pltpu.VMEM)
    anywhere = pl.BlockSpec(memory_space=pl.ANY)

    def call(kernel, out, args, specs=None, scratch=(), flops=0, limit=24 << 20):
        return pl.pallas_call(
            kernel,
            out_shape=out,
            in_specs=[smem] + (specs or [vmem] * (len(args) - 1)),
            out_specs=jax.tree.map(lambda _: vmem, out),
            scratch_shapes=list(scratch),
            compiler_params=pltpu.CompilerParams(vmem_limit_bytes=limit),
            cost_estimate=pl.CostEstimate(flops=flops, bytes_accessed=1 << 20, transcendentals=0),
        )(*args)

    vec = jnp.stack([lane_id, seg_id]).astype(jnp.int32)
    sums = jax.ShapeDtypeStruct((boxes, width), jnp.float32)
    picked, before, c2e_near = call(
        functools.partial(gather_kernel, boxes, per, lanes),
        (
            jax.ShapeDtypeStruct((lanes * per, boxes, width), jnp.bfloat16),
            sums,
            jax.ShapeDtypeStruct(c2e.shape, c2e.dtype),
        ),
        (vec, counts, jnp.transpose(sources, (2, 0, 1)), jnp.transpose(relpos, (2, 0, 1)), column, twin, other, operators, c2e),
        specs=[vmem] * 6 + [anywhere] * 2,
        scratch=[pltpu.VMEM(operators.shape, operators.dtype), pltpu.SemaphoreType.DMA((2,))],
        flops=2 * lanes * per * boxes * boxes * 9 * width,
    )
    before = call(
        functools.partial(near_kernel, per, width),
        sums,
        (vec, picked, before, mine, mine_twin),
        scratch=[pltpu.VMEM((rows, width), jnp.bfloat16)],
        flops=2 * boxes * rows * width,
    )
    density = call(
        functools.partial(far_kernel, per, width, len(pieces)),
        jax.ShapeDtypeStruct((width, boxes), jnp.float32),
        (vec, picked, before, c2e_near, *pieces, *twins),
        scratch=[pltpu.VMEM((lanes - 2, rows, width), jnp.bfloat16)],
        flops=2 * boxes * rows * width,
    )
    return density.T.reshape(1, boxes, width)


def solution(mesh):
    return jax.shard_map(
        per_device,
        mesh=mesh,
        in_specs=(
            P("morton", "lane", None),
            P("morton", "lane"),
            P("morton", "lane", None),
            P("morton", "lane", None),
            P("lane", None, None),
            P(),
        ),
        out_specs=P("morton", "lane", None),
        check_vma=False,
    )
```

profile of v0, /device:TPU:0, one launch (start us, length us, event | category | flops | bytes accessed | tf_op | source)
XLA Modules:
  0.0 41.0 jit_solution(2616436417271779896)
XLA Ops:
  0.0 0.0 copy-start.5
  0.0 0.0 copy-start
  0.0 0.0 copy-start.2
  0.0 0.0 copy-start.3
  0.0 0.0 copy-start.1
  0.0 0.0 copy-start.4
  0.0 3.1 %collective-permute-start = (bf16[296,128]{1,0:T(8,128)(2,1)}, bf16[296,128]{1,0:T(8,128)(2,1)S(1)}, u32[]{:S(2)}, u32[]{:S(2)}) collective-permute-start(bf16[296,128]{1,0:T(8,128)(2,1)} %bitcast.17), channel_id=1, source_target_pairs={{0,1},{1,0},{2,3},{3,2},{4,5},{5,4},{6,7},{7,6},{8,9},{9,8},{10,11... | collective-permute-start | bytes 227336 | tf_op jit(solution)/shard_map/ppermute | solution.py:127
  3.2 0.7 %collective-permute-start.1 = (bf16[296,128]{1,0:T(8,128)(2,1)}, bf16[296,128]{1,0:T(8,128)(2,1)S(1)}, u32[]{:S(2)}, u32[]{:S(2)}) collective-permute-start(bf16[296,128]{1,0:T(8,128)(2,1)} %bitcast.18), channel_id=1, source_target_pairs={{1,2},{2,1},{5,6},{6,5},{9,10},{10,9},{13,14},{14,13},{17,18},{18,... | collective-permute-start | bytes 227336 | tf_op jit(solution)/shard_map/ppermute | solution.py:128
  3.8 0.9 %dynamic-slice_bitcast_fusion = bf16[1,112,296]{2,1,0:T(8,128)(2,1)S(1)} fusion(bf16[888,296]{1,0:T(8,128)(2,1)} %bitcast.13, s32[]{:T(128)S(6)} %select_n.15), kind=kLoop, calls=%fused_computation.1 | loop fusion | bytes 132612 | tf_op jit(solution)/shard_map/broadcast_in_dim | solution.py:129
  4.8 3.9 %collective-permute-start.6 = (bf16[1,112,296]{2,1,0:T(8,128)(2,1)S(1)}, bf16[1,112,296]{2,1,0:T(8,128)(2,1)S(1)}, u32[]{:S(2)}, u32[]{:S(2)}) collective-permute-start(bf16[1,112,296]{2,1,0:T(8,128)(2,1)S(1)} %dynamic-slice_bitcast_fusion), channel_id=1, source_target_pairs={{0,2},{1,3},{2,0},{3,1},{4,6},{5,7},{6,4},{7,5},{8,10},{9,11},{10,... | collective-permute-start | bytes 198920 | tf_op jit(solution)/shard_map/ppermute | solution.py:131
  8.7 2.9 %collective-permute-start.7 = (bf16[1,112,296]{2,1,0:T(8,128)(2,1)S(1)}, bf16[1,112,296]{2,1,0:T(8,128)(2,1)S(1)}, u32[]{:S(2)}, u32[]{:S(2)}) collective-permute-start(bf16[1,112,296]{2,1,0:T(8,128)(2,1)S(1)} %dynamic-slice_bitcast_fusion), channel_id=1, source_target_pairs={{0,3},{1,2},{2,1},{3,0},{4,7},{5,6},{6,5},{7,4},{8,11},{9,10},{10,... | collective-permute-start | bytes 198920 | tf_op jit(solution)/shard_map/ppermute | solution.py:131
  11.6 1.1 %constant_dynamic-slice_fusion = bf16[448,296]{1,0:T(8,128)(2,1)S(1)} fusion(bf16[888,296]{1,0:T(8,128)(2,1)} %bitcast.14, s32[]{:T(128)S(6)} %select_n.14), kind=kLoop, calls=%fused_computation.5 | loop fusion | bytes 530436 | tf_op jit(solution)/shard_map/dynamic_slice | solution.py:130
  12.6 0.1 collective-permute-start.4
  12.7 3.1 %collective-permute-done.6 = bf16[1,112,296]{2,1,0:T(8,128)(2,1)S(1)} collective-permute-done((bf16[1,112,296]{2,1,0:T(8,128)(2,1)S(1)}, bf16[1,112,296]{2,1,0:T(8,128)(2,1)S(1)}, u32[]{:S(2)}, u32[]{:S(2)}) %collective-permute-start.6) | collective-permute-done | bytes 66336 | tf_op jit(solution)/shard_map/ppermute | solution.py:131
  15.9 0.9 %collective-permute-done.7 = bf16[1,112,296]{2,1,0:T(8,128)(2,1)S(1)} collective-permute-done((bf16[1,112,296]{2,1,0:T(8,128)(2,1)S(1)}, bf16[1,112,296]{2,1,0:T(8,128)(2,1)S(1)}, u32[]{:S(2)}, u32[]{:S(2)}) %collective-permute-start.7) | collective-permute-done | bytes 66336 | tf_op jit(solution)/shard_map/ppermute | solution.py:131
  16.8 1.6 %collective-permute-start.8 = (bf16[2,112,296]{2,1,0:T(8,128)(2,1)S(1)}, bf16[2,112,296]{2,1,0:T(8,128)(2,1)S(1)}, u32[]{:S(2)}, u32[]{:S(2)}) collective-permute-start(bf16[2,112,296]{2,1,0:T(8,128)(2,1)S(1)} %constant_dynamic-update-slice_fusion.refs_0_), channel_id=1, source_target_pairs={{0,8},{4,12},{8,0},{12,4},{16,24},{20,28},{24,16},{28,20},{1,9},{5... | collective-permute-start | bytes 397832 | tf_op jit(solution)/shard_map/ppermute | solution.py:139
  18.4 0.0 collective-permute-done
  18.4 0.0 collective-permute-done.1
  18.4 0.0 copy-done.5
  18.4 0.1 collective-permute-start.2
  18.5 0.7 %collective-permute-start.3 = (bf16[888,128]{1,0:T(8,128)(2,1)S(1)}, bf16[888,128]{1,0:T(8,128)(2,1)S(1)}, u32[]{:S(2)}, u32[]{:S(2)}) collective-permute-start(bf16[888,128]{1,0:T(8,128)(2,1)S(1)} %pad_maximum_fusion.column), channel_id=1, source_target_pairs={{4,8},{8,4},{12,16},{16,12},{20,24},{24,20},{5,9},{9,5},{13,17},{1... | collective-permute-start | bytes 681992 | tf_op jit(solution)/shard_map/ppermute | solution.py:136
  19.2 3.4 %collective-permute-start.9 = (bf16[2,112,296]{2,1,0:T(8,128)(2,1)S(1)}, bf16[2,112,296]{2,1,0:T(8,128)(2,1)S(1)}, u32[]{:S(2)}, u32[]{:S(2)}) collective-permute-start(bf16[2,112,296]{2,1,0:T(8,128)(2,1)S(1)} %constant_dynamic-update-slice_fusion.refs_0_), channel_id=1, source_target_pairs={{0,16},{4,20},{8,24},{12,28},{16,0},{20,4},{24,8},{28,12},{1,17},{... | collective-permute-start | bytes 397832 | tf_op jit(solution)/shard_map/ppermute | solution.py:139
  22.6 0.0 collective-permute-done.8.refs_1_
  22.6 2.2 %collective-permute-start.10 = (bf16[2,112,296]{2,1,0:T(8,128)(2,1)S(1)}, bf16[2,112,296]{2,1,0:T(8,128)(2,1)S(1)}, u32[]{:S(2)}, u32[]{:S(2)}) collective-permute-start(bf16[2,112,296]{2,1,0:T(8,128)(2,1)S(1)} %constant_dynamic-update-slice_fusion.refs_0_), channel_id=1, source_target_pairs={{0,24},{4,28},{8,16},{12,20},{16,8},{20,12},{24,0},{28,4},{1,25},{... | collective-permute-start | bytes 397832 | tf_op jit(solution)/shard_map/ppermute | solution.py:139
  24.7 0.0 collective-permute-done.4.mine
  24.7 0.0 collective-permute-start.5
  24.7 7.8 %collective-permute-done.9.refs_2_ = bf16[2,112,296]{2,1,0:T(8,128)(2,1)S(1)} collective-permute-done((bf16[2,112,296]{2,1,0:T(8,128)(2,1)S(1)}, bf16[2,112,296]{2,1,0:T(8,128)(2,1)S(1)}, u32[]{:S(2)}, u32[]{:S(2)}) %collective-permute-start.9) | collective-permute-done | bytes 132640 | tf_op jit(solution)/shard_map/ppermute | solution.py:139
  32.6 0.0 collective-permute-start.11
  32.6 0.0 collective-permute-done.10.refs_3_
  32.6 0.5 %collective-permute-start.12 = (bf16[2,112,296]{2,1,0:T(8,128)(2,1)S(1)}, bf16[2,112,296]{2,1,0:T(8,128)(2,1)S(1)}, u32[]{:S(2)}, u32[]{:S(2)}) collective-permute-start(bf16[2,112,296]{2,1,0:T(8,128)(2,1)S(1)} %collective-permute-done.8.refs_1_), channel_id=1, source_target_pairs={{0,4},{4,0},{8,12},{12,8},{16,20},{20,16},{24,28},{28,24},{1,5},{5... | collective-permute-start | bytes 397832 | tf_op jit(solution)/shard_map/ppermute | solution.py:141
  33.1 0.0 collective-permute-done.2.twin
  33.1 0.1 collective-permute-start.13
  33.2 0.0 collective-permute-done.3.other
  33.2 0.4 %collective-permute-start.14 = (bf16[2,112,296]{2,1,0:T(8,128)(2,1)S(1)}, bf16[2,112,296]{2,1,0:T(8,128)(2,1)S(1)}, u32[]{:S(2)}, u32[]{:S(2)}) collective-permute-start(bf16[2,112,296]{2,1,0:T(8,128)(2,1)S(1)} %collective-permute-done.10.refs_3_), channel_id=1, source_target_pairs={{0,4},{4,0},{8,12},{12,8},{16,20},{20,16},{24,28},{28,24},{1,5},{5... | collective-permute-start | bytes 397832 | tf_op jit(solution)/shard_map/ppermute | solution.py:141
  33.6 0.1 pad_add_fusion.ids
  33.7 0.0 copy-done
  33.7 0.0 copy-done.2
  33.7 0.0 copy-done.3
  33.7 0.0 copy-done.1
  33.7 0.0 copy-done.4
  33.7 4.1 %shard_map.64 = (bf16[12,128,296]{2,1,0:T(8,128)(2,1)S(1)}, f32[128,296]{1,0:T(8,128)S(1)}, bf16[296,296]{1,0:T(8,128)(2,1)S(1)}) custom-call(s32[2]{0:T(128)S(1)} %pad_add_fusion.ids, s32[1,128]{1,0:T(1,128)S(1)} %copy-done.4, s32[12,1,128]{2,1,0:T(1,128)S(1)} %bitcast.15, s32[12,1,128]{2,1,0:T(1,128)S(1)} %bitcast.16, ...), custom_call_target="tpu_custom_call" | custom-call | flops 1047527424 | bytes 1048576 | tf_op jit(solution)/shard_map/pallas_call | solution.py:148
  37.8 0.0 collective-permute-done.5.twin
  37.8 1.0 %shard_map.65.before = f32[128,296]{1,0:T(8,128)S(1)} custom-call(s32[2]{0:T(128)S(1)} %pad_add_fusion.ids, bf16[12,128,296]{2,1,0:T(8,128)(2,1)S(1)} %get-tuple-element.8.picked, f32[128,296]{1,0:T(8,128)S(1)} %get-tuple-element.9.before, bf16[448,296]{1,0:T(8,128)(2,1)S(1)} %collective-permute-done.4.mine, bf16[448,296]{1,0:T(8,128)(2,1)S(1)} %collective-permute-done.5.twin), custom_call_target="tpu_custom_call" | custom-call | flops 67289088 | bytes 1048576 | tf_op jit(solution)/shard_map/pallas_call | solution.py:148
  38.8 0.0 collective-permute-done.11.refs_4_
  38.8 0.0 collective-permute-done.12.refs_5_
  38.8 0.0 collective-permute-done.13.refs_6_
  38.8 0.0 collective-permute-done.14.refs_7_
  38.9 2.1 %shard_map.66 = f32[296,128]{1,0:T(8,128)} custom-call(s32[2]{0:T(128)S(1)} %pad_add_fusion.ids, bf16[12,128,296]{2,1,0:T(8,128)(2,1)S(1)} %get-tuple-element.8.picked, f32[128,296]{1,0:T(8,128)S(1)} %shard_map.65.before, bf16[296,296]{1,0:T(8,128)(2,1)S(1)} %get-tuple-element.10.c2e, bf16[2,112,296]{2,1,0:T(8,128)(2,1)S(1)} %constant_dynamic-update-slice_fusion.refs_0_, ...), custom_call_target="tpu_custom_call" | custom-call | flops 67289088 | bytes 1048576 | tf_op jit(solution)/shard_map/pallas_call | solution.py:148
  (3 shorter events, 0.0 us)
Async XLA Ops:
  0.0 18.4 %copy-start.5 = (bf16[1,128,296]{1,2,0:T(8,128)(2,1)S(1)}, bf16[1,128,296]{1,2,0:T(8,128)(2,1)}, u32[]{:S(2)}) copy-start(bf16[1,128,296]{1,2,0:T(8,128)(2,1)} %param.6) | copy-start | bytes 227332
  0.0 33.7 %copy-start = (bf16[3,296,296]{2,1,0:T(8,128)(2,1)S(1)}, bf16[3,296,296]{2,1,0:T(8,128)(2,1)}, u32[]{:S(2)}) copy-start(bf16[3,296,296]{2,1,0:T(8,128)(2,1)} %own_hbm.1) | copy-start | bytes 1577092
  0.0 33.7 %copy-start.2 = (s32[1,128,12]{1,0,2:T(1,128)S(1)}, s32[1,128,12]{1,0,2:T(1,128)}, u32[]{:S(2)}) copy-start(s32[1,128,12]{1,0,2:T(1,128)} %param.8) | copy-start | bytes 18436
  0.0 33.7 %copy-start.3 = (s32[1,128,12]{1,0,2:T(1,128)S(1)}, s32[1,128,12]{1,0,2:T(1,128)}, u32[]{:S(2)}) copy-start(s32[1,128,12]{1,0,2:T(1,128)} %param.9) | copy-start | bytes 18436
  0.0 33.7 %copy-start.1 = (bf16[296,296]{1,0:T(8,128)(2,1)S(1)}, bf16[296,296]{1,0:T(8,128)(2,1)}, u32[]{:S(2)}) copy-start(bf16[296,296]{1,0:T(8,128)(2,1)} %c2e_hbm.1) | copy-start | bytes 525700
  0.0 33.7 %copy-start.4 = (s32[1,128]{1,0:T(1,128)S(1)}, s32[1,128]{1,0:T(1,128)}, u32[]{:S(2)}) copy-start(s32[1,128]{1,0:T(1,128)} %counts.1) | copy-start | bytes 1540
  0.0 18.4 %collective-permute-start = (bf16[296,128]{1,0:T(8,128)(2,1)}, bf16[296,128]{1,0:T(8,128)(2,1)S(1)}, u32[]{:S(2)}, u32[]{:S(2)}) collective-permute-start(bf16[296,128]{1,0:T(8,128)(2,1)} %bitcast.17), channel_id=1, source_target_pairs={{0,1},{1,0},{2,3},{3,2},{4,5},{5,4},{6,7},{7,6},{8,9},{9,8},{10,11... | collective-permute-start | bytes 227336 | tf_op jit(solution)/shard_map/ppermute | solution.py:127
  3.2 15.2 %collective-permute-start.1 = (bf16[296,128]{1,0:T(8,128)(2,1)}, bf16[296,128]{1,0:T(8,128)(2,1)S(1)}, u32[]{:S(2)}, u32[]{:S(2)}) collective-permute-start(bf16[296,128]{1,0:T(8,128)(2,1)} %bitcast.18), channel_id=1, source_target_pairs={{1,2},{2,1},{5,6},{6,5},{9,10},{10,9},{13,14},{14,13},{17,18},{18,... | collective-permute-start | bytes 227336 | tf_op jit(solution)/shard_map/ppermute | solution.py:128
  4.8 11.1 %collective-permute-start.6 = (bf16[1,112,296]{2,1,0:T(8,128)(2,1)S(1)}, bf16[1,112,296]{2,1,0:T(8,128)(2,1)S(1)}, u32[]{:S(2)}, u32[]{:S(2)}) collective-permute-start(bf16[1,112,296]{2,1,0:T(8,128)(2,1)S(1)} %dynamic-slice_bitcast_fusion), channel_id=1, source_target_pairs={{0,2},{1,3},{2,0},{3,1},{4,6},{5,7},{6,4},{7,5},{8,10},{9,11},{10,... | collective-permute-start | bytes 198920 | tf_op jit(solution)/shard_map/ppermute | solution.py:131
  8.7 8.1 %collective-permute-start.7 = (bf16[1,112,296]{2,1,0:T(8,128)(2,1)S(1)}, bf16[1,112,296]{2,1,0:T(8,128)(2,1)S(1)}, u32[]{:S(2)}, u32[]{:S(2)}) collective-permute-start(bf16[1,112,296]{2,1,0:T(8,128)(2,1)S(1)} %dynamic-slice_bitcast_fusion), channel_id=1, source_target_pairs={{0,3},{1,2},{2,1},{3,0},{4,7},{5,6},{6,5},{7,4},{8,11},{9,10},{10,... | collective-permute-start | bytes 198920 | tf_op jit(solution)/shard_map/ppermute | solution.py:131
  12.6 12.1 %collective-permute-start.4 = (bf16[448,296]{1,0:T(8,128)(2,1)S(1)}, bf16[448,296]{1,0:T(8,128)(2,1)S(1)}, u32[]{:S(2)}, u32[]{:S(2)}) collective-permute-start(bf16[448,296]{1,0:T(8,128)(2,1)S(1)} %constant_dynamic-slice_fusion), channel_id=1, source_target_pairs={{0,1},{1,0},{2,3},{3,2},{4,5},{5,4},{6,7},{7,6},{8,9},{9,8},{10,11... | collective-permute-start | bytes 795656 | tf_op jit(solution)/shard_map/ppermute | solution.py:132
  16.8 5.7 %collective-permute-start.8 = (bf16[2,112,296]{2,1,0:T(8,128)(2,1)S(1)}, bf16[2,112,296]{2,1,0:T(8,128)(2,1)S(1)}, u32[]{:S(2)}, u32[]{:S(2)}) collective-permute-start(bf16[2,112,296]{2,1,0:T(8,128)(2,1)S(1)} %constant_dynamic-update-slice_fusion.refs_0_), channel_id=1, source_target_pairs={{0,8},{4,12},{8,0},{12,4},{16,24},{20,28},{24,16},{28,20},{1,9},{5... | collective-permute-start | bytes 397832 | tf_op jit(solution)/shard_map/ppermute | solution.py:139
  18.4 14.7 %collective-permute-start.2 = (bf16[888,128]{1,0:T(8,128)(2,1)S(1)}, bf16[888,128]{1,0:T(8,128)(2,1)S(1)}, u32[]{:S(2)}, u32[]{:S(2)}) collective-permute-start(bf16[888,128]{1,0:T(8,128)(2,1)S(1)} %pad_maximum_fusion.column), channel_id=1, source_target_pairs={{0,4},{4,0},{8,12},{12,8},{16,20},{20,16},{24,28},{28,24},{1,5},{5... | collective-permute-start | bytes 681992 | tf_op jit(solution)/shard_map/ppermute | solution.py:135
  18.5 14.7 %collective-permute-start.3 = (bf16[888,128]{1,0:T(8,128)(2,1)S(1)}, bf16[888,128]{1,0:T(8,128)(2,1)S(1)}, u32[]{:S(2)}, u32[]{:S(2)}) collective-permute-start(bf16[888,128]{1,0:T(8,128)(2,1)S(1)} %pad_maximum_fusion.column), channel_id=1, source_target_pairs={{4,8},{8,4},{12,16},{16,12},{20,24},{24,20},{5,9},{9,5},{13,17},{1... | collective-permute-start | bytes 681992 | tf_op jit(solution)/shard_map/ppermute | solution.py:136
  19.2 13.4 %collective-permute-start.9 = (bf16[2,112,296]{2,1,0:T(8,128)(2,1)S(1)}, bf16[2,112,296]{2,1,0:T(8,128)(2,1)S(1)}, u32[]{:S(2)}, u32[]{:S(2)}) collective-permute-start(bf16[2,112,296]{2,1,0:T(8,128)(2,1)S(1)} %constant_dynamic-update-slice_fusion.refs_0_), channel_id=1, source_target_pairs={{0,16},{4,20},{8,24},{12,28},{16,0},{20,4},{24,8},{28,12},{1,17},{... | collective-permute-start | bytes 397832 | tf_op jit(solution)/shard_map/ppermute | solution.py:139
  22.6 10.0 %collective-permute-start.10 = (bf16[2,112,296]{2,1,0:T(8,128)(2,1)S(1)}, bf16[2,112,296]{2,1,0:T(8,128)(2,1)S(1)}, u32[]{:S(2)}, u32[]{:S(2)}) collective-permute-start(bf16[2,112,296]{2,1,0:T(8,128)(2,1)S(1)} %constant_dynamic-update-slice_fusion.refs_0_), channel_id=1, source_target_pairs={{0,24},{4,28},{8,16},{12,20},{16,8},{20,12},{24,0},{28,4},{1,25},{... | collective-permute-start | bytes 397832 | tf_op jit(solution)/shard_map/ppermute | solution.py:139
  24.7 13.0 %collective-permute-start.5 = (bf16[448,296]{1,0:T(8,128)(2,1)S(1)}, bf16[448,296]{1,0:T(8,128)(2,1)S(1)}, u32[]{:S(2)}, u32[]{:S(2)}) collective-permute-start(bf16[448,296]{1,0:T(8,128)(2,1)S(1)} %collective-permute-done.4.mine), channel_id=1, source_target_pairs={{0,4},{4,0},{8,12},{12,8},{16,20},{20,16},{24,28},{28,24},{1,5},{5... | collective-permute-start | bytes 795656 | tf_op jit(solution)/shard_map/ppermute | solution.py:140
  32.6 6.3 %collective-permute-start.11 = (bf16[2,112,296]{2,1,0:T(8,128)(2,1)S(1)}, bf16[2,112,296]{2,1,0:T(8,128)(2,1)S(1)}, u32[]{:S(2)}, u32[]{:S(2)}) collective-permute-start(bf16[2,112,296]{2,1,0:T(8,128)(2,1)S(1)} %constant_dynamic-update-slice_fusion.refs_0_), channel_id=1, source_target_pairs={{0,4},{4,0},{8,12},{12,8},{16,20},{20,16},{24,28},{28,24},{1,5},{5... | collective-permute-start | bytes 397832 | tf_op jit(solution)/shard_map/ppermute | solution.py:141
  32.6 6.3 %collective-permute-start.12 = (bf16[2,112,296]{2,1,0:T(8,128)(2,1)S(1)}, bf16[2,112,296]{2,1,0:T(8,128)(2,1)S(1)}, u32[]{:S(2)}, u32[]{:S(2)}) collective-permute-start(bf16[2,112,296]{2,1,0:T(8,128)(2,1)S(1)} %collective-permute-done.8.refs_1_), channel_id=1, source_target_pairs={{0,4},{4,0},{8,12},{12,8},{16,20},{20,16},{24,28},{28,24},{1,5},{5... | collective-permute-start | bytes 397832 | tf_op jit(solution)/shard_map/ppermute | solution.py:141
  33.1 5.8 %collective-permute-start.13 = (bf16[2,112,296]{2,1,0:T(8,128)(2,1)S(1)}, bf16[2,112,296]{2,1,0:T(8,128)(2,1)S(1)}, u32[]{:S(2)}, u32[]{:S(2)}) collective-permute-start(bf16[2,112,296]{2,1,0:T(8,128)(2,1)S(1)} %collective-permute-done.9.refs_2_), channel_id=1, source_target_pairs={{0,4},{4,0},{8,12},{12,8},{16,20},{20,16},{24,28},{28,24},{1,5},{5... | collective-permute-start | bytes 397832 | tf_op jit(solution)/shard_map/ppermute | solution.py:141
  33.2 5.7 %collective-permute-start.14 = (bf16[2,112,296]{2,1,0:T(8,128)(2,1)S(1)}, bf16[2,112,296]{2,1,0:T(8,128)(2,1)S(1)}, u32[]{:S(2)}, u32[]{:S(2)}) collective-permute-start(bf16[2,112,296]{2,1,0:T(8,128)(2,1)S(1)} %collective-permute-done.10.refs_3_), channel_id=1, source_target_pairs={{0,4},{4,0},{8,12},{12,8},{16,20},{20,16},{24,28},{28,24},{1,5},{5... | collective-permute-start | bytes 397832 | tf_op jit(solution)/shard_map/ppermute | solution.py:141
where the time goes:
time: 41.6 us; the launch traced here: 41 us
  starting transfers between devices  19.6 us (47%)
  waiting for transfers between devices  11.9 us (29%)
  Pallas kernels  7.24 us (17%)
  local copies, waits for them, and re-layouts  2.04 us (5%)
    ppermute x3, waiting for transfers between devices, per_device(): lax.ppermute(landed, 'morton', pairs_xor(segs, 2 * j))  7.82 us
    pallas_call x3, Pallas kernels, call(): pl.pallas_call(kernel, out_shape=out, in_specs=[smem] + (specs or [vmem]...  7.24 us
    ppermute x3, starting transfers between devices, per_device(): lax.ppermute(landed, 'morton', pairs_xor(segs, 2 * j))  7.12 us
    ppermute x2, starting transfers between devices, per_device(): lax.ppermute(small, 'lane', pairs_xor(lanes, k))  6.82 us
    ppermute x2, waiting for transfers between devices, per_device(): lax.ppermute(small, 'lane', pairs_xor(lanes, k))  4.06 us
    ppermute x1, starting transfers between devices, per_device(): near = lax.ppermute(block, 'lane', pairs_xor(lanes, 1))  3.13 us
    dynamic_slice x1, local copies, waits for them, and re-layouts, per_device(): lax.dynamic_slice_in_dim(flat, part_start(rows, half, seg_id % 2), half, 0)  1.07 us
    ppermute x4, starting transfers between devices, per_device(): lax.ppermute(piece, 'morton', pairs_xor(segs, 1))  1.02 us
  transfers between devices with their start and end apart: 15, of which 3 were waited for; matrix products, arithmetic and copies ran while one was open for 5% of the time, Pallas kernels for 12%

commit v1 on v0

v1 whole, which is shorter than its diff:
```python
import functools

import jax
import jax.numpy as jnp
from jax import lax
from jax.experimental import pallas as pl
from jax.experimental.pallas import tpu as pltpu
from jax.sharding import PartitionSpec as P


def pairs_xor(count, mask):
    return [(i, i ^ mask) for i in range(count)]


def pairs_odd(count):
    out = []
    for i in range(1, count - 1, 2):
        out += [(i, i + 1), (i + 1, i)]
    return out


def part_rows(rows, parts):
    return 8 * -(-rows // (8 * parts))


def part_start(rows, size, index):
    return jnp.minimum(index * size, rows - size)


def prep_kernel(rows, ids, flat, block, small, block_out, sems):
    size = small.shape[1]
    start = pl.multiple_of(part_start(rows, size, ids[1]), 8)
    copies = [
        pltpu.make_async_copy(flat.at[pl.ds(start, size), :], small.at[0], sems.at[0]),
        pltpu.make_async_copy(block, block_out, sems.at[1]),
    ]
    for copy in copies:
        copy.start()
    for copy in copies:
        copy.wait()


def side_tables(refs, width):
    parts = []
    for ref in refs:
        for j in range(3):
            parts.append(ref[pl.ds(j * width, width), :])
    return jnp.concatenate(parts, axis=1)


def pick_rows(index, table, first, group, per, boxes):
    spot = lax.broadcasted_iota(jnp.int32, (boxes, table.shape[1]), 1) + first
    picks = []
    for i in range(per):
        at = group * per + i
        picks.append((index[:, at : at + 1] == spot).astype(jnp.float32).astype(jnp.bfloat16))
    picks = jnp.concatenate(picks, axis=0)
    found = lax.dot_general(picks, table, (((1,), (1,)), ((), ())), preferred_element_type=jnp.float32)
    return found.astype(jnp.bfloat16).reshape(per, boxes, table.shape[0])


def first_kernel(boxes, per, lanes, ids, counts, sources, relpos, column, c2e, out, index_out, c2e_out):
    lane_id, seg_id = ids[0], ids[1]
    code = sources[:, 0, :]
    rel = relpos[:, 0, :]
    slot = lax.broadcasted_iota(jnp.int32, rel.shape, 0)
    live = slot < counts[...]
    nb = jnp.zeros_like(code)
    for k in range(1, 9):
        nb = nb + (code >= k * boxes).astype(jnp.int32)
    a = (nb >= 3).astype(jnp.int32) + (nb >= 6).astype(jnp.int32)
    b = nb - 3 * a
    offset = code - nb * boxes

    def place(v, odd):
        return jnp.where(v == 1, 0, jnp.where(v == 2 - 2 * odd, 1, 2))

    mapped = (place(b, lane_id % 2) * 3 + place(a, seg_id % 2)) * boxes + offset + 1
    mapped = jnp.where(live, mapped, 0)
    rows = []
    for g in range(lanes):
        for i in range(per):
            wanted = (lane_id ^ g) * per + i
            rows.append(jnp.sum(jnp.where(rel == wanted, mapped, 0), axis=0, keepdims=True) - 1)
    fill = jnp.full((boxes - len(rows), boxes), -1, jnp.int32)
    index = jnp.concatenate(rows + [fill], axis=0).T
    index_out[...] = index
    table = side_tables((column,), out.shape[2])
    for g in range(lanes):
        out[g * per : (g + 1) * per] = pick_rows(index, table, 0, g, per, boxes)
    c2e_out[...] = c2e[...]


def second_kernel(boxes, per, lanes, index, part, near, far, own, out, before):
    table = side_tables((near, far), out.shape[2])
    values = index[...]
    total = None
    for g in range(lanes):
        at = slice(g * per, (g + 1) * per)
        found = part[at] + pick_rows(values, table, 3 * boxes, g, per, boxes)
        out[at] = found
        if g == 0:
            for i in range(per):
                term = jnp.dot(found[i], own[i], preferred_element_type=jnp.float32)
                total = term if total is None else total + term
    before[...] = total


def accumulate(total, picked, group, buffer, per, width):
    for i in range(per):
        term = jnp.dot(picked[group * per + i], buffer[pl.ds(i * width, width), :], preferred_element_type=jnp.float32)
        total = total + term
    return total


def place_part(buffer, rows, size, index, part):
    buffer[pl.ds(pl.multiple_of(part_start(rows, size, index), 8), size), :] = part


def far_kernel(per, width, count, ids, picked, before, c2e, *refs):
    pieces, twins, out, buffer = refs[:count], refs[count : 2 * count], refs[-2], refs[-1]
    rows = per * width
    groups, size = pieces[0].shape[:2]
    total = before[...]
    for k in range(groups):
        view = buffer.at[k]
        for j in range(count):
            place_part(view, rows, size, ids[1] ^ (2 * j), pieces[j][k])
            place_part(view, rows, size, ids[1] ^ (2 * j + 1), twins[j][k])
        total = accumulate(total, picked, k + 1, view, per, width)
    check = total.astype(jnp.bfloat16)
    out[...] = jnp.dot(check, c2e[...], preferred_element_type=jnp.float32).T


def per_device(multipoles, counts, sources, relpos, operators, c2e):
    segs, lanes = lax.axis_size("morton"), lax.axis_size("lane")
    seg_id, lane_id = lax.axis_index("morton"), lax.axis_index("lane")
    boxes, width = multipoles.shape[1:]
    per = operators.shape[0]
    rows = per * width

    block = multipoles[0].T
    flat = operators.reshape(rows, width)
    eighth = part_rows(rows, segs)
    smem = pl.BlockSpec(memory_space=pltpu.SMEM)
    vmem = pl.BlockSpec(memory_space=pltpu.VMEM)
    hbm = pl.BlockSpec(memory_space=pltpu.HBM)

    def call(kernel, out, args, specs=None, scratch=(), flops=0, limit=24 << 20):
        return pl.pallas_call(
            kernel,
            out_shape=out,
            in_specs=specs or [smem] + [vmem] * (len(args) - 1),
            out_specs=jax.tree.map(lambda _: vmem, out),
            scratch_shapes=list(scratch),
            compiler_params=pltpu.CompilerParams(vmem_limit_bytes=limit),
            cost_estimate=pl.CostEstimate(flops=flops, bytes_accessed=1 << 20, transcendentals=0),
        )(*args)

    vec = jnp.stack([lane_id, seg_id]).astype(jnp.int32)
    small, block_near = call(
        functools.partial(prep_kernel, rows),
        (
            jax.ShapeDtypeStruct((1, eighth, width), operators.dtype),
            jax.ShapeDtypeStruct(block.shape, block.dtype),
        ),
        (vec, pltpu.with_memory_space_constraint(flat, pltpu.HBM), pltpu.with_memory_space_constraint(block, pltpu.HBM)),
        specs=[smem, hbm, hbm],
        scratch=[pltpu.SemaphoreType.DMA((2,))],
    )
    twin = lax.ppermute(block, "morton", pairs_xor(segs, 1))
    other = lax.ppermute(block, "morton", pairs_odd(segs))
    column = jnp.concatenate([block_near, twin, other], axis=0)
    near = lax.ppermute(column, "lane", pairs_xor(lanes, 1))
    far = lax.ppermute(column, "lane", pairs_odd(lanes))
    landed = [lax.ppermute(small, "lane", pairs_xor(lanes, k)) for k in range(1, lanes)]

    landed = jnp.concatenate(landed, axis=0)
    pieces = [landed]
    while len(pieces) < segs // 2:
        step = len(pieces)
        pieces += [lax.ppermute(piece, "morton", pairs_xor(segs, 2 * step)) for piece in pieces]
    twins = [lax.ppermute(piece, "morton", pairs_xor(segs, 1)) for piece in pieces]

    sums = jax.ShapeDtypeStruct((boxes, width), jnp.float32)
    table = jax.ShapeDtypeStruct((lanes * per, boxes, width), jnp.bfloat16)
    part, index, c2e_near = call(
        functools.partial(first_kernel, boxes, per, lanes),
        (table, jax.ShapeDtypeStruct((boxes, boxes), jnp.int32), jax.ShapeDtypeStruct(c2e.shape, c2e.dtype)),
        (vec, counts, jnp.transpose(sources, (2, 0, 1)), jnp.transpose(relpos, (2, 0, 1)), column, c2e),
        flops=2 * lanes * per * boxes * boxes * 3 * width,
    )
    picked, before = call(
        functools.partial(second_kernel, boxes, per, lanes),
        (table, sums),
        (index, part, near, far, operators),
        specs=[vmem] * 5,
        flops=2 * lanes * per * boxes * boxes * 6 * width,
    )
    density = call(
        functools.partial(far_kernel, per, width, len(pieces)),
        jax.ShapeDtypeStruct((width, boxes), jnp.float32),
        (vec, picked, before, c2e_near, *pieces, *twins),
        scratch=[pltpu.VMEM((lanes - 1, rows, width), jnp.bfloat16)],
        flops=2 * lanes * boxes * rows * width,
    )
    return density.T.reshape(1, boxes, width)


def solution(mesh):
    return jax.shard_map(
        per_device,
        mesh=mesh,
        in_specs=(
            P("morton", "lane", None),
            P("morton", "lane"),
            P("morton", "lane", None),
            P("morton", "lane", None),
            P("lane", None, None),
            P(),
        ),
        out_specs=P("morton", "lane", None),
        check_vma=False,
    )
```

time: 41.6 us -> 40.6 us (0.976); the launches traced: 41 us -> 40.5 us
  waiting for transfers between devices: 11.9 us -> 17.1 us
  starting transfers between devices: 19.6 us -> 15.5 us
  local copies, waits for them, and re-layouts: 2.04 us -> 0.1 us
    ppermute x9 -> x7, waiting for transfers between devices: 7.84 us -> 10.9 us  [the longest x3 10.9 us: per_device(): lax.ppermute(piece, 'morton', pairs_xor(segs, 2 * step))]
    ppermute x2 -> x3, waiting for transfers between devices: 4.06 us -> 6.23 us  [per_device(): lax.ppermute(small, 'lane', pairs_xor(lanes, k))]
    ppermute x9 -> x7, starting transfers between devices: 11.7 us -> 9.58 us  [the longest x3 5.39 us: per_device(): lax.ppermute(piece, 'morton', pairs_xor(segs, 2 * step))]
    ppermute x2 -> x3, starting transfers between devices: 6.82 us -> 5.38 us  [per_device(): lax.ppermute(small, 'lane', pairs_xor(lanes, k))]
    dynamic_slice x1 -> x0, local copies, waits for them, and re-layouts: 1.07 us -> none  [per_device(): lax.dynamic_slice_in_dim(flat, part_start(rows, half, seg_id % 2), half, 0)]
    broadcast_in_dim x1 -> x0, local copies, waits for them, and re-layouts: 0.92 us -> none  [per_device(): lax.dynamic_slice_in_dim(flat, part_start(rows, eighth, seg_id), eighth, 0)]
    ppermute x4, starting transfers between devices: 1.02 us -> 0.58 us  [per_device(): lax.ppermute(piece, 'morton', pairs_xor(segs, 1))]
    pallas_call x3 -> x4, Pallas kernels: 7.24 us -> 7.47 us  [call(): pl.pallas_call(kernel, out_shape=out, in_specs=specs or [smem] + [vmem] *...]
  transfers between devices with their start and end apart: 15 -> 14, of which waited for: 3 -> 5; matrix products, arithmetic and copies ran while one was open for 5% -> 0% of each run, Pallas kernels for 12% -> 12%
where the time goes in v1:
time: 40.6 us; the launch traced here: 40.5 us
  waiting for transfers between devices  17.1 us (42%)
  starting transfers between devices  15.5 us (38%)
  Pallas kernels  7.47 us (18%)
    ppermute x3, waiting for transfers between devices, per_device(): lax.ppermute(piece, 'morton', pairs_xor(segs, 2 * step))  10.9 us
    pallas_call x4, Pallas kernels, call(): pl.pallas_call(kernel, out_shape=out, in_specs=specs or [smem] + [vmem] *...  7.47 us
    ppermute x3, waiting for transfers between devices, per_device(): lax.ppermute(small, 'lane', pairs_xor(lanes, k))  6.23 us
    ppermute x3, starting transfers between devices, per_device(): lax.ppermute(piece, 'morton', pairs_xor(segs, 2 * step))  5.39 us
    ppermute x3, starting transfers between devices, per_device(): lax.ppermute(small, 'lane', pairs_xor(lanes, k))  5.38 us
    ppermute x1, starting transfers between devices, per_device(): near = lax.ppermute(column, 'lane', pairs_xor(lanes, 1))  2.31 us
  transfers between devices with their start and end apart: 14, of which 5 were waited for; matrix products, arithmetic and copies ran while one was open for 0% of the time, Pallas kernels for 12%

profile of v1, /device:TPU:0, one launch (start us, length us, event | category | flops | bytes accessed | tf_op | source)
XLA Modules:
  0.0 40.5 jit_solution(4553541883871493789)
XLA Ops:
  0.0 0.0 copy-start.2
  0.0 0.0 copy-start.3
  0.0 0.0 copy-start.1
  0.0 0.0 copy-start.4
  0.0 0.6 %collective-permute-start = (bf16[296,128]{1,0:T(8,128)(2,1)}, bf16[296,128]{1,0:T(8,128)(2,1)S(1)}, u32[]{:S(2)}, u32[]{:S(2)}) collective-permute-start(bf16[296,128]{1,0:T(8,128)(2,1)} %bitcast.14), channel_id=1, source_target_pairs={{0,4},{4,0},{8,12},{12,8},{16,20},{20,16},{24,28},{28,24},{1,5},{5... | collective-permute-start | bytes 227336 | tf_op jit(solution)/shard_map/ppermute | solution.py:171
  0.6 0.7 %collective-permute-start.1 = (bf16[296,128]{1,0:T(8,128)(2,1)}, bf16[296,128]{1,0:T(8,128)(2,1)S(1)}, u32[]{:S(2)}, u32[]{:S(2)}) collective-permute-start(bf16[296,128]{1,0:T(8,128)(2,1)} %bitcast.15), channel_id=1, source_target_pairs={{4,8},{8,4},{12,16},{16,12},{20,24},{24,20},{5,9},{9,5},{13,17},{1... | collective-permute-start | bytes 227336 | tf_op jit(solution)/shard_map/ppermute | solution.py:172
  1.2 0.1 pad_add_fusion.ids
  1.3 1.5 %shard_map.64 = (bf16[1,112,296]{2,1,0:T(8,128)(2,1)S(1)}, bf16[296,128]{1,0:T(8,128)(2,1)S(1)}) custom-call(s32[2]{0:T(128)S(1)} %pad_add_fusion.ids, bf16[888,296]{1,0:T(8,128)(2,1)} %bitcast.11, bf16[296,128]{1,0:T(8,128)(2,1)} %bitcast.16), custom_call_target="tpu_custom_call" | custom-call | bytes 1048576 | tf_op jit(solution)/shard_map/pallas_call | solution.py:150
  2.8 0.0 copy-start
  2.8 2.8 %collective-permute-start.4 = (bf16[1,112,296]{2,1,0:T(8,128)(2,1)S(1)}, bf16[1,112,296]{2,1,0:T(8,128)(2,1)S(1)}, u32[]{:S(2)}, u32[]{:S(2)}) collective-permute-start(bf16[1,112,296]{2,1,0:T(8,128)(2,1)S(1)} %get-tuple-element.18), channel_id=1, source_target_pairs={{0,1},{1,0},{2,3},{3,2},{4,5},{5,4},{6,7},{7,6},{8,9},{9,8},{10,11... | collective-permute-start | bytes 198920 | tf_op jit(solution)/shard_map/ppermute | solution.py:176
  5.6 2.6 %collective-permute-start.5 = (bf16[1,112,296]{2,1,0:T(8,128)(2,1)S(1)}, bf16[1,112,296]{2,1,0:T(8,128)(2,1)S(1)}, u32[]{:S(2)}, u32[]{:S(2)}) collective-permute-start(bf16[1,112,296]{2,1,0:T(8,128)(2,1)S(1)} %get-tuple-element.18), channel_id=1, source_target_pairs={{0,2},{1,3},{2,0},{3,1},{4,6},{5,7},{6,4},{7,5},{8,10},{9,11},{10,... | collective-permute-start | bytes 198920 | tf_op jit(solution)/shard_map/ppermute | solution.py:176
  8.2 0.0 collective-permute-start.6
  8.2 0.0 collective-permute-done.4
  8.2 3.9 %collective-permute-done.5 = bf16[1,112,296]{2,1,0:T(8,128)(2,1)S(1)} collective-permute-done((bf16[1,112,296]{2,1,0:T(8,128)(2,1)S(1)}, bf16[1,112,296]{2,1,0:T(8,128)(2,1)S(1)}, u32[]{:S(2)}, u32[]{:S(2)}) %collective-permute-start.5) | collective-permute-done | bytes 66336 | tf_op jit(solution)/shard_map/ppermute | solution.py:176
  12.2 2.3 %collective-permute-done.6 = bf16[1,112,296]{2,1,0:T(8,128)(2,1)S(1)} collective-permute-done((bf16[1,112,296]{2,1,0:T(8,128)(2,1)S(1)}, bf16[1,112,296]{2,1,0:T(8,128)(2,1)S(1)}, u32[]{:S(2)}, u32[]{:S(2)}) %collective-permute-start.6) | collective-permute-done | bytes 66336 | tf_op jit(solution)/shard_map/ppermute | solution.py:176
  14.5 4.4 %collective-permute-start.7 = (bf16[3,112,296]{2,1,0:T(8,128)(2,1)S(1)}, bf16[3,112,296]{2,1,0:T(8,128)(2,1)S(1)}, u32[]{:S(2)}, u32[]{:S(2)}) collective-permute-start(bf16[3,112,296]{2,1,0:T(8,128)(2,1)S(1)} %constant_dynamic-update-slice_fusion.3.refs_0_), channel_id=1, source_target_pairs={{0,8},{4,12},{8,0},{12,4},{16,24},{20,28},{24,16},{28,20},{1,9},{5... | collective-permute-start | bytes 596744 | tf_op jit(solution)/shard_map/ppermute | solution.py:182
  18.9 0.0 collective-permute-done
  19.0 0.0 collective-permute-done.1
  19.0 2.3 %collective-permute-start.2 = (bf16[888,128]{1,0:T(8,128)(2,1)S(1)}, bf16[888,128]{1,0:T(8,128)(2,1)S(1)}, u32[]{:S(2)}, u32[]{:S(2)}) collective-permute-start(bf16[888,128]{1,0:T(8,128)(2,1)S(1)} %constant_dynamic-update-slice_fusion.column), channel_id=1, source_target_pairs={{0,1},{1,0},{2,3},{3,2},{4,5},{5,4},{6,7},{7,6},{8,9},{9,8},{10,11... | collective-permute-start | bytes 681992 | tf_op jit(solution)/shard_map/ppermute | solution.py:174
  21.3 0.1 collective-permute-start.8
  21.4 3.8 %collective-permute-done.7.refs_1_ = bf16[3,112,296]{2,1,0:T(8,128)(2,1)S(1)} collective-permute-done((bf16[3,112,296]{2,1,0:T(8,128)(2,1)S(1)}, bf16[3,112,296]{2,1,0:T(8,128)(2,1)S(1)}, u32[]{:S(2)}, u32[]{:S(2)}) %collective-permute-start.7) | collective-permute-done | bytes 198944 | tf_op jit(solution)/shard_map/ppermute | solution.py:182
  25.2 0.8 %collective-permute-start.9 = (bf16[3,112,296]{2,1,0:T(8,128)(2,1)S(1)}, bf16[3,112,296]{2,1,0:T(8,128)(2,1)S(1)}, u32[]{:S(2)}, u32[]{:S(2)}) collective-permute-start(bf16[3,112,296]{2,1,0:T(8,128)(2,1)S(1)} %collective-permute-done.7.refs_1_), channel_id=1, source_target_pairs={{0,16},{4,20},{8,24},{12,28},{16,0},{20,4},{24,8},{28,12},{1,17},{... | collective-permute-start | bytes 596744 | tf_op jit(solution)/shard_map/ppermute | solution.py:182
  26.0 0.7 %collective-permute-start.3 = (bf16[888,128]{1,0:T(8,128)(2,1)S(1)}, bf16[888,128]{1,0:T(8,128)(2,1)S(1)}, u32[]{:S(2)}, u32[]{:S(2)}) collective-permute-start(bf16[888,128]{1,0:T(8,128)(2,1)S(1)} %constant_dynamic-update-slice_fusion.column), channel_id=1, source_target_pairs={{1,2},{2,1},{5,6},{6,5},{9,10},{10,9},{13,14},{14,13},{17,18},{18,... | collective-permute-start | bytes 681992 | tf_op jit(solution)/shard_map/ppermute | solution.py:175
  26.7 0.1 collective-permute-start.10
  26.8 3.6 %collective-permute-done.8.refs_2_ = bf16[3,112,296]{2,1,0:T(8,128)(2,1)S(1)} collective-permute-done((bf16[3,112,296]{2,1,0:T(8,128)(2,1)S(1)}, bf16[3,112,296]{2,1,0:T(8,128)(2,1)S(1)}, u32[]{:S(2)}, u32[]{:S(2)}) %collective-permute-start.8) | collective-permute-done | bytes 198944 | tf_op jit(solution)/shard_map/ppermute | solution.py:182
  30.4 0.0 collective-permute-start.11
  30.4 0.0 collective-permute-done.2.near
  30.4 0.5 %collective-permute-start.12 = (bf16[3,112,296]{2,1,0:T(8,128)(2,1)S(1)}, bf16[3,112,296]{2,1,0:T(8,128)(2,1)S(1)}, u32[]{:S(2)}, u32[]{:S(2)}) collective-permute-start(bf16[3,112,296]{2,1,0:T(8,128)(2,1)S(1)} %collective-permute-done.8.refs_2_), channel_id=1, source_target_pairs={{0,4},{4,0},{8,12},{12,8},{16,20},{20,16},{24,28},{28,24},{1,5},{5... | collective-permute-start | bytes 596744 | tf_op jit(solution)/shard_map/ppermute | solution.py:183
  30.9 3.5 %collective-permute-done.9.refs_3_ = bf16[3,112,296]{2,1,0:T(8,128)(2,1)S(1)} collective-permute-done((bf16[3,112,296]{2,1,0:T(8,128)(2,1)S(1)}, bf16[3,112,296]{2,1,0:T(8,128)(2,1)S(1)}, u32[]{:S(2)}, u32[]{:S(2)}) %collective-permute-start.9) | collective-permute-done | bytes 198944 | tf_op jit(solution)/shard_map/ppermute | solution.py:182
  34.4 0.0 collective-permute-start.13
  34.4 0.0 copy-done.2
  34.4 0.0 copy-done.3
  34.4 0.0 copy-done.1
  34.4 0.0 copy-done.4
  34.4 1.8 %shard_map.65 = (bf16[12,128,296]{2,1,0:T(8,128)(2,1)S(1)}, s32[128,128]{1,0:T(8,128)S(1)}, bf16[296,296]{1,0:T(8,128)(2,1)S(1)}) custom-call(s32[2]{0:T(128)S(1)} %pad_add_fusion.ids, s32[1,128]{1,0:T(1,128)S(1)} %copy-done.4, s32[12,1,128]{2,1,0:T(1,128)S(1)} %bitcast.12, s32[12,1,128]{2,1,0:T(1,128)S(1)} %bitcast.13, ...), custom_call_target="tpu_custom_call" | custom-call | flops 349175808 | bytes 1048576 | tf_op jit(solution)/shard_map/pallas_call | solution.py:150
  36.2 0.0 collective-permute-done.3.far
  36.2 0.0 copy-done
  36.2 1.8 %shard_map.66 = (bf16[12,128,296]{2,1,0:T(8,128)(2,1)S(1)}, f32[128,296]{1,0:T(8,128)S(1)}) custom-call(s32[128,128]{1,0:T(8,128)S(1)} %get-tuple-element.13.index, bf16[12,128,296]{2,1,0:T(8,128)(2,1)S(1)} %get-tuple-element.14.part, bf16[888,128]{1,0:T(8,128)(2,1)S(1)} %collective-permute-done.2.near, bf16[888,128]{1,0:T(8,128)(2,1)S(1)} %collective-permute-done.3.far, ...), custom_call_target="tpu_custom_call" | custom-call | flops 698351616 | bytes 1048576 | tf_op jit(solution)/shard_map/pallas_call | solution.py:150
  38.0 0.0 collective-permute-done.10.refs_4_
  38.0 0.0 collective-permute-done.11.refs_5_
  38.0 0.0 collective-permute-done.12.refs_6_
  38.0 0.0 collective-permute-done.13.refs_7_
  38.0 2.4 %shard_map.67 = f32[296,128]{1,0:T(8,128)} custom-call(s32[2]{0:T(128)S(1)} %pad_add_fusion.ids, bf16[12,128,296]{2,1,0:T(8,128)(2,1)S(1)} %get-tuple-element.15.picked, f32[128,296]{1,0:T(8,128)S(1)} %get-tuple-element.16.before, bf16[296,296]{1,0:T(8,128)(2,1)S(1)} %get-tuple-element.17.c2e, ...), custom_call_target="tpu_custom_call" | custom-call | flops 269156352 | bytes 1048576 | tf_op jit(solution)/shard_map/pallas_call | solution.py:150
  (6 shorter events, 0.1 us)
Async XLA Ops:
  0.0 34.4 %copy-start.2 = (s32[1,128,12]{1,0,2:T(1,128)S(1)}, s32[1,128,12]{1,0,2:T(1,128)}, u32[]{:S(2)}) copy-start(s32[1,128,12]{1,0,2:T(1,128)} %param.8) | copy-start | bytes 18436
  0.0 34.4 %copy-start.3 = (s32[1,128,12]{1,0,2:T(1,128)S(1)}, s32[1,128,12]{1,0,2:T(1,128)}, u32[]{:S(2)}) copy-start(s32[1,128,12]{1,0,2:T(1,128)} %param.9) | copy-start | bytes 18436
  0.0 34.4 %copy-start.1 = (bf16[296,296]{1,0:T(8,128)(2,1)S(1)}, bf16[296,296]{1,0:T(8,128)(2,1)}, u32[]{:S(2)}) copy-start(bf16[296,296]{1,0:T(8,128)(2,1)} %c2e.1) | copy-start | bytes 525700
  0.0 34.4 %copy-start.4 = (s32[1,128]{1,0:T(1,128)S(1)}, s32[1,128]{1,0:T(1,128)}, u32[]{:S(2)}) copy-start(s32[1,128]{1,0:T(1,128)} %counts.1) | copy-start | bytes 1540
  0.0 18.9 %collective-permute-start = (bf16[296,128]{1,0:T(8,128)(2,1)}, bf16[296,128]{1,0:T(8,128)(2,1)S(1)}, u32[]{:S(2)}, u32[]{:S(2)}) collective-permute-start(bf16[296,128]{1,0:T(8,128)(2,1)} %bitcast.14), channel_id=1, source_target_pairs={{0,4},{4,0},{8,12},{12,8},{16,20},{20,16},{24,28},{28,24},{1,5},{5... | collective-permute-start | bytes 227336 | tf_op jit(solution)/shard_map/ppermute | solution.py:171
  0.6 18.4 %collective-permute-start.1 = (bf16[296,128]{1,0:T(8,128)(2,1)}, bf16[296,128]{1,0:T(8,128)(2,1)S(1)}, u32[]{:S(2)}, u32[]{:S(2)}) collective-permute-start(bf16[296,128]{1,0:T(8,128)(2,1)} %bitcast.15), channel_id=1, source_target_pairs={{4,8},{8,4},{12,16},{16,12},{20,24},{24,20},{5,9},{9,5},{13,17},{1... | collective-permute-start | bytes 227336 | tf_op jit(solution)/shard_map/ppermute | solution.py:172
  2.8 33.4 %copy-start = (bf16[3,296,296]{2,1,0:T(8,128)(2,1)S(1)}, bf16[3,296,296]{2,1,0:T(8,128)(2,1)}, u32[]{:S(2)}) copy-start(bf16[3,296,296]{2,1,0:T(8,128)(2,1)} %own.1) | copy-start | bytes 1577092
  2.8 5.4 %collective-permute-start.4 = (bf16[1,112,296]{2,1,0:T(8,128)(2,1)S(1)}, bf16[1,112,296]{2,1,0:T(8,128)(2,1)S(1)}, u32[]{:S(2)}, u32[]{:S(2)}) collective-permute-start(bf16[1,112,296]{2,1,0:T(8,128)(2,1)S(1)} %get-tuple-element.18), channel_id=1, source_target_pairs={{0,1},{1,0},{2,3},{3,2},{4,5},{5,4},{6,7},{7,6},{8,9},{9,8},{10,11... | collective-permute-start | bytes 198920 | tf_op jit(solution)/shard_map/ppermute | solution.py:176
  5.6 6.5 %collective-permute-start.5 = (bf16[1,112,296]{2,1,0:T(8,128)(2,1)S(1)}, bf16[1,112,296]{2,1,0:T(8,128)(2,1)S(1)}, u32[]{:S(2)}, u32[]{:S(2)}) collective-permute-start(bf16[1,112,296]{2,1,0:T(8,128)(2,1)S(1)} %get-tuple-element.18), channel_id=1, source_target_pairs={{0,2},{1,3},{2,0},{3,1},{4,6},{5,7},{6,4},{7,5},{8,10},{9,11},{10,... | collective-permute-start | bytes 198920 | tf_op jit(solution)/shard_map/ppermute | solution.py:176
  8.2 6.3 %collective-permute-start.6 = (bf16[1,112,296]{2,1,0:T(8,128)(2,1)S(1)}, bf16[1,112,296]{2,1,0:T(8,128)(2,1)S(1)}, u32[]{:S(2)}, u32[]{:S(2)}) collective-permute-start(bf16[1,112,296]{2,1,0:T(8,128)(2,1)S(1)} %get-tuple-element.18), channel_id=1, source_target_pairs={{0,3},{1,2},{2,1},{3,0},{4,7},{5,6},{6,5},{7,4},{8,11},{9,10},{10,... | collective-permute-start | bytes 198920 | tf_op jit(solution)/shard_map/ppermute | solution.py:176
  14.5 10.7 %collective-permute-start.7 = (bf16[3,112,296]{2,1,0:T(8,128)(2,1)S(1)}, bf16[3,112,296]{2,1,0:T(8,128)(2,1)S(1)}, u32[]{:S(2)}, u32[]{:S(2)}) collective-permute-start(bf16[3,112,296]{2,1,0:T(8,128)(2,1)S(1)} %constant_dynamic-update-slice_fusion.3.refs_0_), channel_id=1, source_target_pairs={{0,8},{4,12},{8,0},{12,4},{16,24},{20,28},{24,16},{28,20},{1,9},{5... | collective-permute-start | bytes 596744 | tf_op jit(solution)/shard_map/ppermute | solution.py:182
  19.0 11.4 %collective-permute-start.2 = (bf16[888,128]{1,0:T(8,128)(2,1)S(1)}, bf16[888,128]{1,0:T(8,128)(2,1)S(1)}, u32[]{:S(2)}, u32[]{:S(2)}) collective-permute-start(bf16[888,128]{1,0:T(8,128)(2,1)S(1)} %constant_dynamic-update-slice_fusion.column), channel_id=1, source_target_pairs={{0,1},{1,0},{2,3},{3,2},{4,5},{5,4},{6,7},{7,6},{8,9},{9,8},{10,11... | collective-permute-start | bytes 681992 | tf_op jit(solution)/shard_map/ppermute | solution.py:174
  21.3 9.1 %collective-permute-start.8 = (bf16[3,112,296]{2,1,0:T(8,128)(2,1)S(1)}, bf16[3,112,296]{2,1,0:T(8,128)(2,1)S(1)}, u32[]{:S(2)}, u32[]{:S(2)}) collective-permute-start(bf16[3,112,296]{2,1,0:T(8,128)(2,1)S(1)} %constant_dynamic-update-slice_fusion.3.refs_0_), channel_id=1, source_target_pairs={{0,16},{4,20},{8,24},{12,28},{16,0},{20,4},{24,8},{28,12},{1,17},{... | collective-permute-start | bytes 596744 | tf_op jit(solution)/shard_map/ppermute | solution.py:182
  25.2 9.2 %collective-permute-start.9 = (bf16[3,112,296]{2,1,0:T(8,128)(2,1)S(1)}, bf16[3,112,296]{2,1,0:T(8,128)(2,1)S(1)}, u32[]{:S(2)}, u32[]{:S(2)}) collective-permute-start(bf16[3,112,296]{2,1,0:T(8,128)(2,1)S(1)} %collective-permute-done.7.refs_1_), channel_id=1, source_target_pairs={{0,16},{4,20},{8,24},{12,28},{16,0},{20,4},{24,8},{28,12},{1,17},{... | collective-permute-start | bytes 596744 | tf_op jit(solution)/shard_map/ppermute | solution.py:182
  26.0 10.2 %collective-permute-start.3 = (bf16[888,128]{1,0:T(8,128)(2,1)S(1)}, bf16[888,128]{1,0:T(8,128)(2,1)S(1)}, u32[]{:S(2)}, u32[]{:S(2)}) collective-permute-start(bf16[888,128]{1,0:T(8,128)(2,1)S(1)} %constant_dynamic-update-slice_fusion.column), channel_id=1, source_target_pairs={{1,2},{2,1},{5,6},{6,5},{9,10},{10,9},{13,14},{14,13},{17,18},{18,... | collective-permute-start | bytes 681992 | tf_op jit(solution)/shard_map/ppermute | solution.py:175
  26.7 11.3 %collective-permute-start.10 = (bf16[3,112,296]{2,1,0:T(8,128)(2,1)S(1)}, bf16[3,112,296]{2,1,0:T(8,128)(2,1)S(1)}, u32[]{:S(2)}, u32[]{:S(2)}) collective-permute-start(bf16[3,112,296]{2,1,0:T(8,128)(2,1)S(1)} %constant_dynamic-update-slice_fusion.3.refs_0_), channel_id=1, source_target_pairs={{0,4},{4,0},{8,12},{12,8},{16,20},{20,16},{24,28},{28,24},{1,5},{5... | collective-permute-start | bytes 596744 | tf_op jit(solution)/shard_map/ppermute | solution.py:183
  30.4 7.6 %collective-permute-start.11 = (bf16[3,112,296]{2,1,0:T(8,128)(2,1)S(1)}, bf16[3,112,296]{2,1,0:T(8,128)(2,1)S(1)}, u32[]{:S(2)}, u32[]{:S(2)}) collective-permute-start(bf16[3,112,296]{2,1,0:T(8,128)(2,1)S(1)} %collective-permute-done.7.refs_1_), channel_id=1, source_target_pairs={{0,4},{4,0},{8,12},{12,8},{16,20},{20,16},{24,28},{28,24},{1,5},{5... | collective-permute-start | bytes 596744 | tf_op jit(solution)/shard_map/ppermute | solution.py:183
  30.4 7.6 %collective-permute-start.12 = (bf16[3,112,296]{2,1,0:T(8,128)(2,1)S(1)}, bf16[3,112,296]{2,1,0:T(8,128)(2,1)S(1)}, u32[]{:S(2)}, u32[]{:S(2)}) collective-permute-start(bf16[3,112,296]{2,1,0:T(8,128)(2,1)S(1)} %collective-permute-done.8.refs_2_), channel_id=1, source_target_pairs={{0,4},{4,0},{8,12},{12,8},{16,20},{20,16},{24,28},{28,24},{1,5},{5... | collective-permute-start | bytes 596744 | tf_op jit(solution)/shard_map/ppermute | solution.py:183
  34.4 3.7 %collective-permute-start.13 = (bf16[3,112,296]{2,1,0:T(8,128)(2,1)S(1)}, bf16[3,112,296]{2,1,0:T(8,128)(2,1)S(1)}, u32[]{:S(2)}, u32[]{:S(2)}) collective-permute-start(bf16[3,112,296]{2,1,0:T(8,128)(2,1)S(1)} %collective-permute-done.9.refs_3_), channel_id=1, source_target_pairs={{0,4},{4,0},{8,12},{12,8},{16,20},{20,16},{24,28},{28,24},{1,5},{5... | collective-permute-start | bytes 596744 | tf_op jit(solution)/shard_map/ppermute | solution.py:183

commit v2 on v1

--- a/solution.py
+++ b/solution.py
@@ -27,13 +27,14 @@
     return jnp.minimum(index * size, rows - size)
 
 
-def prep_kernel(rows, ids, flat, block, small, block_out, sems):
-    size = small.shape[1]
-    start = pl.multiple_of(part_start(rows, size, ids[1]), 8)
-    copies = [
-        pltpu.make_async_copy(flat.at[pl.ds(start, size), :], small.at[0], sems.at[0]),
-        pltpu.make_async_copy(block, block_out, sems.at[1]),
-    ]
+def prep_kernel(rows, ids, flat, block, small, mid, block_out, sems):
+    copies = []
+    for at, (out, parts) in enumerate(((small, None), (mid, 2))):
+        size = out.shape[1]
+        index = ids[1] if parts is None else ids[1] % parts
+        start = pl.multiple_of(part_start(rows, size, index), 8)
+        copies.append(pltpu.make_async_copy(flat.at[pl.ds(start, size), :], out.at[0], sems.at[at]))
+    copies.append(pltpu.make_async_copy(block, block_out, sems.at[2]))
     for copy in copies:
         copy.start()
     for copy in copies:
@@ -117,17 +118,20 @@
     buffer[pl.ds(pl.multiple_of(part_start(rows, size, index), 8), size), :] = part
 
 
-def far_kernel(per, width, count, ids, picked, before, c2e, *refs):
+def far_kernel(per, width, count, ids, picked, before, c2e, close, close_twin, *refs):
     pieces, twins, out, buffer = refs[:count], refs[count : 2 * count], refs[-2], refs[-1]
     rows = per * width
     groups, size = pieces[0].shape[:2]
-    total = before[...]
+    view = buffer.at[0]
+    for other, part in enumerate((close, close_twin)):
+        place_part(view, rows, part.shape[1], (ids[1] ^ other) % 2, part[0])
+    total = accumulate(before[...], picked, 1, view, per, width)
     for k in range(groups):
-        view = buffer.at[k]
+        view = buffer.at[k + 1]
         for j in range(count):
             place_part(view, rows, size, ids[1] ^ (2 * j), pieces[j][k])
             place_part(view, rows, size, ids[1] ^ (2 * j + 1), twins[j][k])
-        total = accumulate(total, picked, k + 1, view, per, width)
+        total = accumulate(total, picked, k + 2, view, per, width)
     check = total.astype(jnp.bfloat16)
     out[...] = jnp.dot(check, c2e[...], preferred_element_type=jnp.float32).T
 
@@ -141,7 +145,7 @@
 
     block = multipoles[0].T
     flat = operators.reshape(rows, width)
-    eighth = part_rows(rows, segs)
+    eighth, quarter = part_rows(rows, segs), part_rows(rows, 2)
     smem = pl.BlockSpec(memory_space=pltpu.SMEM)
     vmem = pl.BlockSpec(memory_space=pltpu.VMEM)
     hbm = pl.BlockSpec(memory_space=pltpu.HBM)
@@ -158,28 +162,31 @@
         )(*args)
 
     vec = jnp.stack([lane_id, seg_id]).astype(jnp.int32)
-    small, block_near = call(
+    small, mid, block_near = call(
         functools.partial(prep_kernel, rows),
         (
             jax.ShapeDtypeStruct((1, eighth, width), operators.dtype),
+            jax.ShapeDtypeStruct((1, quarter, width), operators.dtype),
             jax.ShapeDtypeStruct(block.shape, block.dtype),
         ),
         (vec, pltpu.with_memory_space_constraint(flat, pltpu.HBM), pltpu.with_memory_space_constraint(block, pltpu.HBM)),
         specs=[smem, hbm, hbm],
-        scratch=[pltpu.SemaphoreType.DMA((2,))],
+        scratch=[pltpu.SemaphoreType.DMA((3,))],
     )
     twin = lax.ppermute(block, "morton", pairs_xor(segs, 1))
     other = lax.ppermute(block, "morton", pairs_odd(segs))
     column = jnp.concatenate([block_near, twin, other], axis=0)
     near = lax.ppermute(column, "lane", pairs_xor(lanes, 1))
     far = lax.ppermute(column, "lane", pairs_odd(lanes))
-    landed = [lax.ppermute(small, "lane", pairs_xor(lanes, k)) for k in range(1, lanes)]
+    landed = [lax.ppermute(small, "lane", pairs_xor(lanes, k)) for k in range(2, lanes)]
+    close = lax.ppermute(mid, "lane", pairs_xor(lanes, 1))
 
     landed = jnp.concatenate(landed, axis=0)
     pieces = [landed]
     while len(pieces) < segs // 2:
         step = len(pieces)
         pieces += [lax.ppermute(piece, "morton", pairs_xor(segs, 2 * step)) for piece in pieces]
+    close_twin = lax.ppermute(close, "morton", pairs_xor(segs, 1))
     twins = [lax.ppermute(piece, "morton", pairs_xor(segs, 1)) for piece in pieces]
 
     sums = jax.ShapeDtypeStruct((boxes, width), jnp.float32)
@@ -200,7 +207,7 @@
     density = call(
         functools.partial(far_kernel, per, width, len(pieces)),
         jax.ShapeDtypeStruct((width, boxes), jnp.float32),
-        (vec, picked, before, c2e_near, *pieces, *twins),
+        (vec, picked, before, c2e_near, close, close_twin, *pieces, *twins),
         scratch=[pltpu.VMEM((lanes - 1, rows, width), jnp.bfloat16)],
         flops=2 * lanes * boxes * rows * width,
     )

time: 40.6 us -> 38 us (0.936)
  the two profiles are of different devices: /device:TPU:0 before, /device:TPU:9 now
where the time goes in v2:
time: 38 us; the launch traced here: 37.9 us
  starting transfers between devices  23.2 us (61%)
  Pallas kernels  7.59 us (20%)
  waiting for transfers between devices  6.72 us (18%)
    pallas_call x4, Pallas kernels, call(): pl.pallas_call(kernel, out_shape=out, in_specs=specs or [smem] + [vmem] *...  7.59 us
    ppermute x4, starting transfers between devices, per_device(): lax.ppermute(piece, 'morton', pairs_xor(segs, 1))  5.47 us
    ppermute x2, waiting for transfers between devices, per_device(): lax.ppermute(small, 'lane', pairs_xor(lanes, k))  4.68 us
    ppermute x3, starting transfers between devices, per_device(): lax.ppermute(piece, 'morton', pairs_xor(segs, 2 * step))  4.55 us
    ppermute x1, starting transfers between devices, per_device(): far = lax.ppermute(column, 'lane', pairs_odd(lanes))  4.1 us
    ppermute x1, starting transfers between devices, per_device(): other = lax.ppermute(block, 'morton', pairs_odd(segs))  3.15 us
    ppermute x2, starting transfers between devices, per_device(): lax.ppermute(small, 'lane', pairs_xor(lanes, k))  2.38 us
    ppermute x3, waiting for transfers between devices, per_device(): lax.ppermute(piece, 'morton', pairs_xor(segs, 2 * step))  2.02 us
  transfers between devices with their start and end apart: 15, of which 3 were waited for; matrix products, arithmetic and copies ran while one was open for 0% of the time, Pallas kernels for 14%

profile of v2, /device:TPU:9, one launch (start us, length us, event | category | flops | bytes accessed | tf_op | source)
XLA Modules:
  0.0 37.9 jit_solution(13291563941517317810)
XLA Ops:
  0.0 0.0 copy-start.2
  0.0 0.0 copy-start.3
  0.0 0.0 copy-start.1
  0.0 0.0 copy-start.4
  0.0 0.7 %collective-permute-start = (bf16[296,128]{1,0:T(8,128)(2,1)}, bf16[296,128]{1,0:T(8,128)(2,1)S(1)}, u32[]{:S(2)}, u32[]{:S(2)}) collective-permute-start(bf16[296,128]{1,0:T(8,128)(2,1)} %bitcast.14), channel_id=1, source_target_pairs={{0,4},{4,0},{8,12},{12,8},{16,20},{20,16},{24,28},{28,24},{1,5},{5... | collective-permute-start | bytes 227336 | tf_op jit(solution)/shard_map/ppermute | solution.py:176
  0.8 3.2 %collective-permute-start.1 = (bf16[296,128]{1,0:T(8,128)(2,1)}, bf16[296,128]{1,0:T(8,128)(2,1)S(1)}, u32[]{:S(2)}, u32[]{:S(2)}) collective-permute-start(bf16[296,128]{1,0:T(8,128)(2,1)} %bitcast.15), channel_id=1, source_target_pairs={{4,8},{8,4},{12,16},{16,12},{20,24},{24,20},{5,9},{9,5},{13,17},{1... | collective-permute-start | bytes 227336 | tf_op jit(solution)/shard_map/ppermute | solution.py:177
  3.9 0.1 pad_add_fusion.ids
  4.0 1.6 %shard_map.64 = (bf16[1,112,296]{2,1,0:T(8,128)(2,1)S(1)}, bf16[1,448,296]{2,1,0:T(8,128)(2,1)S(1)}, bf16[296,128]{1,0:T(8,128)(2,1)S(1)}) custom-call(s32[2]{0:T(128)S(1)} %pad_add_fusion.ids, bf16[888,296]{1,0:T(8,128)(2,1)} %bitcast.11, bf16[296,128]{1,0:T(8,128)(2,1)} %bitcast.16), custom_call_target="tpu_custom_call" | custom-call | bytes 1048576 | tf_op jit(solution)/shard_map/pallas_call | solution.py:154
  5.6 0.0 copy-start
  5.6 2.4 %collective-permute-start.6 = (bf16[1,112,296]{2,1,0:T(8,128)(2,1)S(1)}, bf16[1,112,296]{2,1,0:T(8,128)(2,1)S(1)}, u32[]{:S(2)}, u32[]{:S(2)}) collective-permute-start(bf16[1,112,296]{2,1,0:T(8,128)(2,1)S(1)} %get-tuple-element.20), channel_id=1, source_target_pairs={{0,2},{1,3},{2,0},{3,1},{4,6},{5,7},{6,4},{7,5},{8,10},{9,11},{10,... | collective-permute-start | bytes 198920 | tf_op jit(solution)/shard_map/ppermute | solution.py:181
  8.0 0.0 collective-permute-start.7
  8.0 1.3 %collective-permute-start.4 = (bf16[1,448,296]{2,1,0:T(8,128)(2,1)S(1)}, bf16[1,448,296]{2,1,0:T(8,128)(2,1)S(1)}, u32[]{:S(2)}, u32[]{:S(2)}) collective-permute-start(bf16[1,448,296]{2,1,0:T(8,128)(2,1)S(1)} %get-tuple-element.19), channel_id=1, source_target_pairs={{0,1},{1,0},{2,3},{3,2},{4,5},{5,4},{6,7},{7,6},{8,9},{9,8},{10,11... | collective-permute-start | bytes 795656 | tf_op jit(solution)/shard_map/ppermute | solution.py:182
  9.3 3.1 %collective-permute-done.6 = bf16[1,112,296]{2,1,0:T(8,128)(2,1)S(1)} collective-permute-done((bf16[1,112,296]{2,1,0:T(8,128)(2,1)S(1)}, bf16[1,112,296]{2,1,0:T(8,128)(2,1)S(1)}, u32[]{:S(2)}, u32[]{:S(2)}) %collective-permute-start.6) | collective-permute-done | bytes 66336 | tf_op jit(solution)/shard_map/ppermute | solution.py:181
  12.4 1.6 %collective-permute-done.7 = bf16[1,112,296]{2,1,0:T(8,128)(2,1)S(1)} collective-permute-done((bf16[1,112,296]{2,1,0:T(8,128)(2,1)S(1)}, bf16[1,112,296]{2,1,0:T(8,128)(2,1)S(1)}, u32[]{:S(2)}, u32[]{:S(2)}) %collective-permute-start.7) | collective-permute-done | bytes 66336 | tf_op jit(solution)/shard_map/ppermute | solution.py:181
  14.0 3.0 %collective-permute-start.8 = (bf16[2,112,296]{2,1,0:T(8,128)(2,1)S(1)}, bf16[2,112,296]{2,1,0:T(8,128)(2,1)S(1)}, u32[]{:S(2)}, u32[]{:S(2)}) collective-permute-start(bf16[2,112,296]{2,1,0:T(8,128)(2,1)S(1)} %constant_dynamic-update-slice_fusion.3.refs_0_), channel_id=1, source_target_pairs={{0,8},{4,12},{8,0},{12,4},{16,24},{20,28},{24,16},{28,20},{1,9},{5... | collective-permute-start | bytes 397832 | tf_op jit(solution)/shard_map/ppermute | solution.py:188
  17.0 0.0 collective-permute-done
  17.0 0.0 collective-permute-done.1
  17.1 0.1 collective-permute-start.2
  17.1 4.1 %collective-permute-start.3 = (bf16[888,128]{1,0:T(8,128)(2,1)S(1)}, bf16[888,128]{1,0:T(8,128)(2,1)S(1)}, u32[]{:S(2)}, u32[]{:S(2)}) collective-permute-start(bf16[888,128]{1,0:T(8,128)(2,1)S(1)} %constant_dynamic-update-slice_fusion.column), channel_id=1, source_target_pairs={{1,2},{2,1},{5,6},{6,5},{9,10},{10,9},{13,14},{14,13},{17,18},{18,... | collective-permute-start | bytes 681992 | tf_op jit(solution)/shard_map/ppermute | solution.py:180
  21.2 0.2 collective-permute-start.9
  21.4 0.0 collective-permute-done.8.refs_1_
  21.4 1.3 %collective-permute-start.10 = (bf16[2,112,296]{2,1,0:T(8,128)(2,1)S(1)}, bf16[2,112,296]{2,1,0:T(8,128)(2,1)S(1)}, u32[]{:S(2)}, u32[]{:S(2)}) collective-permute-start(bf16[2,112,296]{2,1,0:T(8,128)(2,1)S(1)} %collective-permute-done.8.refs_1_), channel_id=1, source_target_pairs={{0,16},{4,20},{8,24},{12,28},{16,0},{20,4},{24,8},{28,12},{1,17},{... | collective-permute-start | bytes 397832 | tf_op jit(solution)/shard_map/ppermute | solution.py:188
  22.8 0.0 collective-permute-done.4.close
  22.8 1.5 %collective-permute-start.5 = (bf16[1,448,296]{2,1,0:T(8,128)(2,1)S(1)}, bf16[1,448,296]{2,1,0:T(8,128)(2,1)S(1)}, u32[]{:S(2)}, u32[]{:S(2)}) collective-permute-start(bf16[1,448,296]{2,1,0:T(8,128)(2,1)S(1)} %collective-permute-done.4.close), channel_id=1, source_target_pairs={{0,4},{4,0},{8,12},{12,8},{16,20},{20,16},{24,28},{28,24},{1,5},{5... | collective-permute-start | bytes 795656 | tf_op jit(solution)/shard_map/ppermute | solution.py:189
  24.3 2.0 %collective-permute-done.9.refs_2_ = bf16[2,112,296]{2,1,0:T(8,128)(2,1)S(1)} collective-permute-done((bf16[2,112,296]{2,1,0:T(8,128)(2,1)S(1)}, bf16[2,112,296]{2,1,0:T(8,128)(2,1)S(1)}, u32[]{:S(2)}, u32[]{:S(2)}) %collective-permute-start.9) | collective-permute-done | bytes 132640 | tf_op jit(solution)/shard_map/ppermute | solution.py:188
  26.3 3.2 %collective-permute-start.11 = (bf16[2,112,296]{2,1,0:T(8,128)(2,1)S(1)}, bf16[2,112,296]{2,1,0:T(8,128)(2,1)S(1)}, u32[]{:S(2)}, u32[]{:S(2)}) collective-permute-start(bf16[2,112,296]{2,1,0:T(8,128)(2,1)S(1)} %constant_dynamic-update-slice_fusion.3.refs_0_), channel_id=1, source_target_pairs={{0,4},{4,0},{8,12},{12,8},{16,20},{20,16},{24,28},{28,24},{1,5},{5... | collective-permute-start | bytes 397832 | tf_op jit(solution)/shard_map/ppermute | solution.py:190
  29.5 0.0 collective-permute-done.2.near
  29.5 0.0 collective-permute-start.12
  29.5 0.0 collective-permute-done.3.far
  29.5 0.5 %collective-permute-start.13 = (bf16[2,112,296]{2,1,0:T(8,128)(2,1)S(1)}, bf16[2,112,296]{2,1,0:T(8,128)(2,1)S(1)}, u32[]{:S(2)}, u32[]{:S(2)}) collective-permute-start(bf16[2,112,296]{2,1,0:T(8,128)(2,1)S(1)} %collective-permute-done.9.refs_2_), channel_id=1, source_target_pairs={{0,4},{4,0},{8,12},{12,8},{16,20},{20,16},{24,28},{28,24},{1,5},{5... | collective-permute-start | bytes 397832 | tf_op jit(solution)/shard_map/ppermute | solution.py:190
  30.0 0.0 collective-permute-done.10.refs_3_
  30.0 1.8 %collective-permute-start.14 = (bf16[2,112,296]{2,1,0:T(8,128)(2,1)S(1)}, bf16[2,112,296]{2,1,0:T(8,128)(2,1)S(1)}, u32[]{:S(2)}, u32[]{:S(2)}) collective-permute-start(bf16[2,112,296]{2,1,0:T(8,128)(2,1)S(1)} %collective-permute-done.10.refs_3_), channel_id=1, source_target_pairs={{0,4},{4,0},{8,12},{12,8},{16,20},{20,16},{24,28},{28,24},{1,5},{5... | collective-permute-start | bytes 397832 | tf_op jit(solution)/shard_map/ppermute | solution.py:190
  31.8 0.0 copy-done.2
  31.8 0.0 copy-done.3
  31.8 0.0 copy-done.1
  31.8 0.0 copy-done.4
  31.8 1.8 %shard_map.65 = (bf16[12,128,296]{2,1,0:T(8,128)(2,1)S(1)}, s32[128,128]{1,0:T(8,128)S(1)}, bf16[296,296]{1,0:T(8,128)(2,1)S(1)}) custom-call(s32[2]{0:T(128)S(1)} %pad_add_fusion.ids, s32[1,128]{1,0:T(1,128)S(1)} %copy-done.4, s32[12,1,128]{2,1,0:T(1,128)S(1)} %bitcast.12, s32[12,1,128]{2,1,0:T(1,128)S(1)} %bitcast.13, ...), custom_call_target="tpu_custom_call" | custom-call | flops 349175808 | bytes 1048576 | tf_op jit(solution)/shard_map/pallas_call | solution.py:154
  33.6 0.0 copy-done
  33.6 1.8 %shard_map.66 = (bf16[12,128,296]{2,1,0:T(8,128)(2,1)S(1)}, f32[128,296]{1,0:T(8,128)S(1)}) custom-call(s32[128,128]{1,0:T(8,128)S(1)} %get-tuple-element.14.index, bf16[12,128,296]{2,1,0:T(8,128)(2,1)S(1)} %get-tuple-element.15.part, bf16[888,128]{1,0:T(8,128)(2,1)S(1)} %collective-permute-done.2.near, bf16[888,128]{1,0:T(8,128)(2,1)S(1)} %collective-permute-done.3.far, ...), custom_call_target="tpu_custom_call" | custom-call | flops 698351616 | bytes 1048576 | tf_op jit(solution)/shard_map/pallas_call | solution.py:154
  35.4 0.0 collective-permute-done.11.refs_4_
  35.4 0.0 collective-permute-done.12.refs_5_
  35.4 0.0 collective-permute-done.13.refs_6_
  35.4 0.0 collective-permute-done.14.refs_7_
  35.4 0.0 collective-permute-done.5.close_twin
  35.4 2.4 %shard_map.67 = f32[296,128]{1,0:T(8,128)} custom-call(s32[2]{0:T(128)S(1)} %pad_add_fusion.ids, bf16[12,128,296]{2,1,0:T(8,128)(2,1)S(1)} %get-tuple-element.16.picked, f32[128,296]{1,0:T(8,128)S(1)} %get-tuple-element.17.before, bf16[296,296]{1,0:T(8,128)(2,1)S(1)} %get-tuple-element.18.c2e, bf16[1,448,296]{2,1,0:T(8,128)(2,1)S(1)} %collective-permute-done.4.close, ...), custom_call_target="tpu_custom_call" | custom-call | flops 269156352 | bytes 1048576 | tf_op jit(solution)/shard_map/pallas_call | solution.py:154
  (5 shorter events, 0.1 us)
Async XLA Ops:
  0.0 31.8 %copy-start.2 = (s32[1,128,12]{1,0,2:T(1,128)S(1)}, s32[1,128,12]{1,0,2:T(1,128)}, u32[]{:S(2)}) copy-start(s32[1,128,12]{1,0,2:T(1,128)} %param.8) | copy-start | bytes 18436
  0.0 31.8 %copy-start.3 = (s32[1,128,12]{1,0,2:T(1,128)S(1)}, s32[1,128,12]{1,0,2:T(1,128)}, u32[]{:S(2)}) copy-start(s32[1,128,12]{1,0,2:T(1,128)} %param.9) | copy-start | bytes 18436
  0.0 31.8 %copy-start.1 = (bf16[296,296]{1,0:T(8,128)(2,1)S(1)}, bf16[296,296]{1,0:T(8,128)(2,1)}, u32[]{:S(2)}) copy-start(bf16[296,296]{1,0:T(8,128)(2,1)} %c2e.1) | copy-start | bytes 525700
  0.0 31.8 %copy-start.4 = (s32[1,128]{1,0:T(1,128)S(1)}, s32[1,128]{1,0:T(1,128)}, u32[]{:S(2)}) copy-start(s32[1,128]{1,0:T(1,128)} %counts.1) | copy-start | bytes 1540
  0.0 17.0 %collective-permute-start = (bf16[296,128]{1,0:T(8,128)(2,1)}, bf16[296,128]{1,0:T(8,128)(2,1)S(1)}, u32[]{:S(2)}, u32[]{:S(2)}) collective-permute-start(bf16[296,128]{1,0:T(8,128)(2,1)} %bitcast.14), channel_id=1, source_target_pairs={{0,4},{4,0},{8,12},{12,8},{16,20},{20,16},{24,28},{28,24},{1,5},{5... | collective-permute-start | bytes 227336 | tf_op jit(solution)/shard_map/ppermute | solution.py:176
  0.8 16.3 %collective-permute-start.1 = (bf16[296,128]{1,0:T(8,128)(2,1)}, bf16[296,128]{1,0:T(8,128)(2,1)S(1)}, u32[]{:S(2)}, u32[]{:S(2)}) collective-permute-start(bf16[296,128]{1,0:T(8,128)(2,1)} %bitcast.15), channel_id=1, source_target_pairs={{4,8},{8,4},{12,16},{16,12},{20,24},{24,20},{5,9},{9,5},{13,17},{1... | collective-permute-start | bytes 227336 | tf_op jit(solution)/shard_map/ppermute | solution.py:177
  5.6 28.0 %copy-start = (bf16[3,296,296]{2,1,0:T(8,128)(2,1)S(1)}, bf16[3,296,296]{2,1,0:T(8,128)(2,1)}, u32[]{:S(2)}) copy-start(bf16[3,296,296]{2,1,0:T(8,128)(2,1)} %own.1) | copy-start | bytes 1577092
  5.6 6.8 %collective-permute-start.6 = (bf16[1,112,296]{2,1,0:T(8,128)(2,1)S(1)}, bf16[1,112,296]{2,1,0:T(8,128)(2,1)S(1)}, u32[]{:S(2)}, u32[]{:S(2)}) collective-permute-start(bf16[1,112,296]{2,1,0:T(8,128)(2,1)S(1)} %get-tuple-element.20), channel_id=1, source_target_pairs={{0,2},{1,3},{2,0},{3,1},{4,6},{5,7},{6,4},{7,5},{8,10},{9,11},{10,... | collective-permute-start | bytes 198920 | tf_op jit(solution)/shard_map/ppermute | solution.py:181
  8.0 6.0 %collective-permute-start.7 = (bf16[1,112,296]{2,1,0:T(8,128)(2,1)S(1)}, bf16[1,112,296]{2,1,0:T(8,128)(2,1)S(1)}, u32[]{:S(2)}, u32[]{:S(2)}) collective-permute-start(bf16[1,112,296]{2,1,0:T(8,128)(2,1)S(1)} %get-tuple-element.20), channel_id=1, source_target_pairs={{0,3},{1,2},{2,1},{3,0},{4,7},{5,6},{6,5},{7,4},{8,11},{9,10},{10,... | collective-permute-start | bytes 198920 | tf_op jit(solution)/shard_map/ppermute | solution.py:181
  8.0 14.8 %collective-permute-start.4 = (bf16[1,448,296]{2,1,0:T(8,128)(2,1)S(1)}, bf16[1,448,296]{2,1,0:T(8,128)(2,1)S(1)}, u32[]{:S(2)}, u32[]{:S(2)}) collective-permute-start(bf16[1,448,296]{2,1,0:T(8,128)(2,1)S(1)} %get-tuple-element.19), channel_id=1, source_target_pairs={{0,1},{1,0},{2,3},{3,2},{4,5},{5,4},{6,7},{7,6},{8,9},{9,8},{10,11... | collective-permute-start | bytes 795656 | tf_op jit(solution)/shard_map/ppermute | solution.py:182
  14.0 7.5 %collective-permute-start.8 = (bf16[2,112,296]{2,1,0:T(8,128)(2,1)S(1)}, bf16[2,112,296]{2,1,0:T(8,128)(2,1)S(1)}, u32[]{:S(2)}, u32[]{:S(2)}) collective-permute-start(bf16[2,112,296]{2,1,0:T(8,128)(2,1)S(1)} %constant_dynamic-update-slice_fusion.3.refs_0_), channel_id=1, source_target_pairs={{0,8},{4,12},{8,0},{12,4},{16,24},{20,28},{24,16},{28,20},{1,9},{5... | collective-permute-start | bytes 397832 | tf_op jit(solution)/shard_map/ppermute | solution.py:188
  17.1 12.4 %collective-permute-start.2 = (bf16[888,128]{1,0:T(8,128)(2,1)S(1)}, bf16[888,128]{1,0:T(8,128)(2,1)S(1)}, u32[]{:S(2)}, u32[]{:S(2)}) collective-permute-start(bf16[888,128]{1,0:T(8,128)(2,1)S(1)} %constant_dynamic-update-slice_fusion.column), channel_id=1, source_target_pairs={{0,1},{1,0},{2,3},{3,2},{4,5},{5,4},{6,7},{7,6},{8,9},{9,8},{10,11... | collective-permute-start | bytes 681992 | tf_op jit(solution)/shard_map/ppermute | solution.py:179
  17.1 12.4 %collective-permute-start.3 = (bf16[888,128]{1,0:T(8,128)(2,1)S(1)}, bf16[888,128]{1,0:T(8,128)(2,1)S(1)}, u32[]{:S(2)}, u32[]{:S(2)}) collective-permute-start(bf16[888,128]{1,0:T(8,128)(2,1)S(1)} %constant_dynamic-update-slice_fusion.column), channel_id=1, source_target_pairs={{1,2},{2,1},{5,6},{6,5},{9,10},{10,9},{13,14},{14,13},{17,18},{18,... | collective-permute-start | bytes 681992 | tf_op jit(solution)/shard_map/ppermute | solution.py:180
  21.2 5.1 %collective-permute-start.9 = (bf16[2,112,296]{2,1,0:T(8,128)(2,1)S(1)}, bf16[2,112,296]{2,1,0:T(8,128)(2,1)S(1)}, u32[]{:S(2)}, u32[]{:S(2)}) collective-permute-start(bf16[2,112,296]{2,1,0:T(8,128)(2,1)S(1)} %constant_dynamic-update-slice_fusion.3.refs_0_), channel_id=1, source_target_pairs={{0,16},{4,20},{8,24},{12,28},{16,0},{20,4},{24,8},{28,12},{1,17},{... | collective-permute-start | bytes 397832 | tf_op jit(solution)/shard_map/ppermute | solution.py:188
  21.4 8.6 %collective-permute-start.10 = (bf16[2,112,296]{2,1,0:T(8,128)(2,1)S(1)}, bf16[2,112,296]{2,1,0:T(8,128)(2,1)S(1)}, u32[]{:S(2)}, u32[]{:S(2)}) collective-permute-start(bf16[2,112,296]{2,1,0:T(8,128)(2,1)S(1)} %collective-permute-done.8.refs_1_), channel_id=1, source_target_pairs={{0,16},{4,20},{8,24},{12,28},{16,0},{20,4},{24,8},{28,12},{1,17},{... | collective-permute-start | bytes 397832 | tf_op jit(solution)/shard_map/ppermute | solution.py:188
  22.8 12.6 %collective-permute-start.5 = (bf16[1,448,296]{2,1,0:T(8,128)(2,1)S(1)}, bf16[1,448,296]{2,1,0:T(8,128)(2,1)S(1)}, u32[]{:S(2)}, u32[]{:S(2)}) collective-permute-start(bf16[1,448,296]{2,1,0:T(8,128)(2,1)S(1)} %collective-permute-done.4.close), channel_id=1, source_target_pairs={{0,4},{4,0},{8,12},{12,8},{16,20},{20,16},{24,28},{28,24},{1,5},{5... | collective-permute-start | bytes 795656 | tf_op jit(solution)/shard_map/ppermute | solution.py:189
  26.3 9.1 %collective-permute-start.11 = (bf16[2,112,296]{2,1,0:T(8,128)(2,1)S(1)}, bf16[2,112,296]{2,1,0:T(8,128)(2,1)S(1)}, u32[]{:S(2)}, u32[]{:S(2)}) collective-permute-start(bf16[2,112,296]{2,1,0:T(8,128)(2,1)S(1)} %constant_dynamic-update-slice_fusion.3.refs_0_), channel_id=1, source_target_pairs={{0,4},{4,0},{8,12},{12,8},{16,20},{20,16},{24,28},{28,24},{1,5},{5... | collective-permute-start | bytes 397832 | tf_op jit(solution)/shard_map/ppermute | solution.py:190
  29.5 5.9 %collective-permute-start.12 = (bf16[2,112,296]{2,1,0:T(8,128)(2,1)S(1)}, bf16[2,112,296]{2,1,0:T(8,128)(2,1)S(1)}, u32[]{:S(2)}, u32[]{:S(2)}) collective-permute-start(bf16[2,112,296]{2,1,0:T(8,128)(2,1)S(1)} %collective-permute-done.8.refs_1_), channel_id=1, source_target_pairs={{0,4},{4,0},{8,12},{12,8},{16,20},{20,16},{24,28},{28,24},{1,5},{5... | collective-permute-start | bytes 397832 | tf_op jit(solution)/shard_map/ppermute | solution.py:190
  29.5 5.9 %collective-permute-start.13 = (bf16[2,112,296]{2,1,0:T(8,128)(2,1)S(1)}, bf16[2,112,296]{2,1,0:T(8,128)(2,1)S(1)}, u32[]{:S(2)}, u32[]{:S(2)}) collective-permute-start(bf16[2,112,296]{2,1,0:T(8,128)(2,1)S(1)} %collective-permute-done.9.refs_2_), channel_id=1, source_target_pairs={{0,4},{4,0},{8,12},{12,8},{16,20},{20,16},{24,28},{28,24},{1,5},{5... | collective-permute-start | bytes 397832 | tf_op jit(solution)/shard_map/ppermute | solution.py:190
  30.0 5.4 %collective-permute-start.14 = (bf16[2,112,296]{2,1,0:T(8,128)(2,1)S(1)}, bf16[2,112,296]{2,1,0:T(8,128)(2,1)S(1)}, u32[]{:S(2)}, u32[]{:S(2)}) collective-permute-start(bf16[2,112,296]{2,1,0:T(8,128)(2,1)S(1)} %collective-permute-done.10.refs_3_), channel_id=1, source_target_pairs={{0,4},{4,0},{8,12},{12,8},{16,20},{20,16},{24,28},{28,24},{1,5},{5... | collective-permute-start | bytes 397832 | tf_op jit(solution)/shard_map/ppermute | solution.py:190

commit v3 on v2

v3 whole, which is shorter than its diff:
```python
import functools

import jax
import jax.numpy as jnp
from jax import lax
from jax.experimental import pallas as pl
from jax.experimental.pallas import tpu as pltpu
from jax.sharding import PartitionSpec as P


def pairs_xor(count, mask):
    return [(i, i ^ mask) for i in range(count)]


def pairs_odd(count):
    out = []
    for i in range(1, count - 1, 2):
        out += [(i, i + 1), (i + 1, i)]
    return out


def part_rows(rows, parts):
    return 16 * -(-rows // (16 * parts))


def copy_part(flat, out, size, index, sem, act):
    rows = flat.shape[0]
    whole, rest = divmod(rows, size)

    def move(count):
        start = pl.multiple_of(index * size, 16)
        copy = pltpu.make_async_copy(flat.at[pl.ds(start, count), :], out.at[pl.ds(0, count), :], sem)
        copy.start() if act == "start" else copy.wait()

    pl.when(index < whole)(lambda: move(size))
    if rest:
        pl.when(index == whole)(lambda: move(rest))


def prep_kernel(flat, block, small, mid, block_out, sems):
    seg_id = lax.axis_index("morton")

    def parts(act):
        for at, (out, index) in enumerate(((small, seg_id), (mid, seg_id % 2))):
            copy_part(flat, out.at[0], out.shape[1], index, sems.at[at], act)

    whole = pltpu.make_async_copy(block, block_out, sems.at[2])
    parts("start")
    whole.start()
    parts("wait")
    whole.wait()


def side_tables(refs, width):
    parts = []
    for ref in refs:
        for j in range(3):
            parts.append(ref[pl.ds(j * width, width), :])
    return jnp.concatenate(parts, axis=1)


def pick_rows(index, table, first, at, count, boxes):
    spot = lax.broadcasted_iota(jnp.int32, (table.shape[1], boxes), 0) + first
    picks = [(index[at + i : at + i + 1, :] == spot).astype(jnp.float32).astype(jnp.bfloat16) for i in range(count)]
    picks = jnp.concatenate(picks, axis=1) if count > 1 else picks[0]
    return jnp.dot(table, picks, preferred_element_type=jnp.float32).astype(jnp.bfloat16)


def first_kernel(boxes, per, lanes, counts, sources, relpos, column, c2e, out, index_out, c2e_out):
    lane_id, seg_id = lax.axis_index("lane"), lax.axis_index("morton")
    code = sources[:, 0, :]
    rel = relpos[:, 0, :]
    slot = lax.broadcasted_iota(jnp.int32, rel.shape, 0)
    live = slot < counts[...]
    nb = jnp.zeros_like(code)
    for k in range(1, 9):
        nb = nb + (code >= k * boxes).astype(jnp.int32)
    a = (nb >= 3).astype(jnp.int32) + (nb >= 6).astype(jnp.int32)
    b = nb - 3 * a
    offset = code - nb * boxes

    def place(v, odd):
        return jnp.where(v == 1, 0, jnp.where(v == 2 - 2 * odd, 1, 2))

    mapped = (place(b, lane_id % 2) * 3 + place(a, seg_id % 2)) * boxes + offset + 1
    mapped = jnp.where(live, mapped, 0)
    rows = []
    for g in range(lanes):
        for i in range(per):
            wanted = (lane_id ^ g) * per + i
            rows.append(jnp.sum(jnp.where(rel == wanted, mapped, 0), axis=0, keepdims=True) - 1)
    index = jnp.concatenate(rows, axis=0)
    index_out[...] = index
    table = side_tables((column,), out.shape[1])
    for at in range(0, len(rows), 2):
        count = min(2, len(rows) - at)
        found = pick_rows(index, table, 0, at, count, boxes)
        for i in range(count):
            out[at + i] = found[:, i * boxes : (i + 1) * boxes]
    c2e_out[...] = c2e[...]


def second_kernel(boxes, index, part, near, far, out):
    table = side_tables((near, far), out.shape[2])
    values = index[...]
    total = values.shape[0]
    for at in range(0, total, 2):
        count = min(2, total - at)
        found = pick_rows(values, table, 3 * boxes, at, count, boxes)
        for i in range(count):
            out[at + i] = (part[at + i] + found[:, i * boxes : (i + 1) * boxes]).T


def accumulate(total, picked, group, buffer, per, width):
    for i in range(per):
        term = jnp.dot(picked[group * per + i], buffer[pl.ds(i * width, width), :], preferred_element_type=jnp.float32)
        total = total + term
    return total


def place_part(buffer, index, part):
    size = part.shape[0]
    buffer[pl.ds(pl.multiple_of(index * size, 16), size), :] = part


def place_pieces(buffer, seg_id, first, pieces, twins):
    for k in range(pieces[0].shape[0]):
        for j, (piece, twin) in enumerate(zip(pieces, twins)):
            place_part(buffer.at[k], seg_id ^ (2 * (first + j)), piece[k])
            place_part(buffer.at[k], seg_id ^ (2 * (first + j) + 1), twin[k])


def mid_kernel(per, width, count, picked, own, close, close_twin, *refs):
    pieces, twins = refs[:count], refs[count : 2 * count]
    before, buffer, near = refs[2 * count :]
    seg_id = lax.axis_index("morton")
    core = seg_id % 2
    place_part(near, core, close[0])
    place_part(near, 1 - core, close_twin[0])
    total = None
    for i in range(per):
        term = jnp.dot(picked[i], own[i], preferred_element_type=jnp.float32)
        total = term if total is None else total + term
    before[...] = accumulate(total, picked, 1, near, per, width)
    place_pieces(buffer, seg_id, 0, pieces, twins)


def far_kernel(per, width, first, picked, before, c2e, piece, twin, filled, out, buffer):
    place_pieces(buffer, lax.axis_index("morton"), first, [piece], [twin])
    total = before[...]
    for k in range(buffer.shape[0]):
        total = accumulate(total, picked, k + 2, buffer.at[k], per, width)
    check = total.astype(jnp.bfloat16)
    out[...] = jnp.dot(check, c2e[...], preferred_element_type=jnp.float32).T


def per_device(multipoles, counts, sources, relpos, operators, c2e):
    segs, lanes = lax.axis_size("morton"), lax.axis_size("lane")
    boxes, width = multipoles.shape[1:]
    per = operators.shape[0]
    rows = per * width

    block = multipoles[0].T
    flat = operators.reshape(rows, width)
    eighth, quarter = part_rows(rows, segs), part_rows(rows, 2)
    vmem = pl.BlockSpec(memory_space=pltpu.VMEM)
    hbm = pl.BlockSpec(memory_space=pltpu.HBM)

    def call(kernel, out, args, specs=None, scratch=(), flops=0, limit=24 << 20, alias=None):
        return pl.pallas_call(
            kernel,
            out_shape=out,
            in_specs=specs or [vmem] * len(args),
            out_specs=jax.tree.map(lambda _: vmem, out),
            scratch_shapes=list(scratch),
            input_output_aliases=alias or {},
            compiler_params=pltpu.CompilerParams(vmem_limit_bytes=limit),
            cost_estimate=pl.CostEstimate(flops=flops, bytes_accessed=1 << 20, transcendentals=0),
        )(*args)

    small, mid, block_near = call(
        prep_kernel,
        (
            jax.ShapeDtypeStruct((1, eighth, width), operators.dtype),
            jax.ShapeDtypeStruct((1, quarter, width), operators.dtype),
            jax.ShapeDtypeStruct(block.shape, block.dtype),
        ),
        (pltpu.with_memory_space_constraint(flat, pltpu.HBM), pltpu.with_memory_space_constraint(block, pltpu.HBM)),
        specs=[hbm, hbm],
        scratch=[pltpu.SemaphoreType.DMA((3,))],
    )
    twin = lax.ppermute(block, "morton", pairs_xor(segs, 1))
    other = lax.ppermute(block, "morton", pairs_odd(segs))
    column = jnp.concatenate([block_near, twin, other], axis=0)
    near = lax.ppermute(column, "lane", pairs_xor(lanes, 1))
    far = lax.ppermute(column, "lane", pairs_odd(lanes))
    landed = [lax.ppermute(small, "lane", pairs_xor(lanes, k)) for k in range(2, lanes)]
    close = lax.ppermute(mid, "lane", pairs_xor(lanes, 1))

    landed = jnp.concatenate(landed, axis=0)
    pieces = [landed]
    while len(pieces) < segs // 2:
        step = len(pieces)
        pieces += [lax.ppermute(piece, "morton", pairs_xor(segs, 2 * step)) for piece in pieces]
    close_twin = lax.ppermute(close, "morton", pairs_xor(segs, 1))
    twins = [lax.ppermute(piece, "morton", pairs_xor(segs, 1)) for piece in pieces]

    sums = jax.ShapeDtypeStruct((boxes, width), jnp.float32)
    total = lanes * per
    part, index, c2e_near = call(
        functools.partial(first_kernel, boxes, per, lanes),
        (
            jax.ShapeDtypeStruct((total, width, boxes), jnp.bfloat16),
            jax.ShapeDtypeStruct((total, boxes), jnp.int32),
            jax.ShapeDtypeStruct(c2e.shape, c2e.dtype),
        ),
        (counts, jnp.transpose(sources, (2, 0, 1)), jnp.transpose(relpos, (2, 0, 1)), column, c2e),
        flops=2 * total * boxes * boxes * 3 * width,
    )
    picked = call(
        functools.partial(second_kernel, boxes),
        jax.ShapeDtypeStruct((total, boxes, width), jnp.bfloat16),
        (index, part, near, far),
        specs=[vmem] * 4,
        flops=2 * total * boxes * boxes * 6 * width,
    )
    buffer = jax.ShapeDtypeStruct((lanes - 2, eighth * segs, width), jnp.bfloat16)
    early = len(pieces) - 1
    before, buffer_mid = call(
        functools.partial(mid_kernel, per, width, early),
        (sums, buffer),
        (picked, operators, close, close_twin, *pieces[:early], *twins[:early]),
        scratch=[pltpu.VMEM((2 * quarter, width), jnp.bfloat16)],
        flops=4 * boxes * rows * width,
    )
    density, _ = call(
        functools.partial(far_kernel, per, width, early),
        (jax.ShapeDtypeStruct((width, boxes), jnp.float32), buffer),
        (picked, before, c2e_near, pieces[early], twins[early], buffer_mid),
        alias={5: 1},
        flops=2 * lanes * boxes * rows * width,
    )
    return density.T.reshape(1, boxes, width)


def solution(mesh):
    return jax.shard_map(
        per_device,
        mesh=mesh,
        in_specs=(
            P("morton", "lane", None),
            P("morton", "lane"),
            P("morton", "lane", None),
            P("morton", "lane", None),
            P("lane", None, None),
            P(),
        ),
        out_specs=P("morton", "lane", None),
        check_vma=False,
    )
```

time: 38 us -> 35.5 us (0.934)
  Pallas kernels: 7.59 us -> 5.16 us
    pallas_call x4 -> x5, Pallas kernels: 7.59 us -> 5.16 us  [call(): pl.pallas_call(kernel, out_shape=out, in_specs=specs or [vmem] * len(args...]
    ppermute x1, starting transfers between devices: 1.5 us -> 1.03 us  [per_device(): close_twin = lax.ppermute(close, 'morton', pairs_xor(segs, 1))]
  transfers between devices with their start and end apart: 15 -> 15, of which waited for: 3 -> 3; matrix products, arithmetic and copies ran while one was open for 0% -> 0% of each run, Pallas kernels for 14% -> 10%
where the time goes in v3:
time: 35.5 us; the launch traced here: 35.4 us
  starting transfers between devices  23 us (65%)
  waiting for transfers between devices  7 us (20%)
  Pallas kernels  5.16 us (15%)
    ppermute x4, starting transfers between devices, per_device(): lax.ppermute(piece, 'morton', pairs_xor(segs, 1))  5.48 us
    pallas_call x5, Pallas kernels, call(): pl.pallas_call(kernel, out_shape=out, in_specs=specs or [vmem] * len(args...  5.16 us
    ppermute x3, starting transfers between devices, per_device(): lax.ppermute(piece, 'morton', pairs_xor(segs, 2 * step))  4.75 us
    ppermute x2, waiting for transfers between devices, per_device(): lax.ppermute(small, 'lane', pairs_xor(lanes, k))  4.69 us
    ppermute x1, starting transfers between devices, per_device(): far = lax.ppermute(column, 'lane', pairs_odd(lanes))  4.11 us
    ppermute x1, starting transfers between devices, per_device(): other = lax.ppermute(block, 'morton', pairs_odd(segs))  3.15 us
    ppermute x2, starting transfers between devices, per_device(): lax.ppermute(small, 'lane', pairs_xor(lanes, k))  2.38 us
    ppermute x3, waiting for transfers between devices, per_device(): lax.ppermute(piece, 'morton', pairs_xor(segs, 2 * step))  2.29 us
  transfers between devices with their start and end apart: 15, of which 3 were waited for; matrix products, arithmetic and copies ran while one was open for 0% of the time, Pallas kernels for 10%

profile of v3, /device:TPU:9, one launch (start us, length us, event | category | flops | bytes accessed | tf_op | source)
XLA Modules:
  0.0 35.4 jit_solution(13750908471160662911)
XLA Ops:
  0.0 0.0 copy-start.2
  0.0 0.0 copy-start.3
  0.0 0.0 copy-start.1
  0.0 0.0 copy-start.4
  0.0 0.7 %collective-permute-start = (bf16[296,128]{1,0:T(8,128)(2,1)}, bf16[296,128]{1,0:T(8,128)(2,1)S(1)}, u32[]{:S(2)}, u32[]{:S(2)}) collective-permute-start(bf16[296,128]{1,0:T(8,128)(2,1)} %bitcast.12), channel_id=1, source_target_pairs={{0,4},{4,0},{8,12},{12,8},{16,20},{20,16},{24,28},{28,24},{1,5},{5... | collective-permute-start | bytes 227336 | tf_op jit(solution)/shard_map/ppermute | solution.py:192
  0.8 3.1 %collective-permute-start.1 = (bf16[296,128]{1,0:T(8,128)(2,1)}, bf16[296,128]{1,0:T(8,128)(2,1)S(1)}, u32[]{:S(2)}, u32[]{:S(2)}) collective-permute-start(bf16[296,128]{1,0:T(8,128)(2,1)} %bitcast.13), channel_id=1, source_target_pairs={{4,8},{8,4},{12,16},{16,12},{20,24},{24,20},{5,9},{9,5},{13,17},{1... | collective-permute-start | bytes 227336 | tf_op jit(solution)/shard_map/ppermute | solution.py:193
  3.9 1.1 %shard_map.64 = (bf16[1,112,296]{2,1,0:T(8,128)(2,1)S(1)}, bf16[1,448,296]{2,1,0:T(8,128)(2,1)S(1)}, bf16[296,128]{1,0:T(8,128)(2,1)S(1)}) custom-call(bf16[888,296]{1,0:T(8,128)(2,1)} %bitcast.9, bf16[296,128]{1,0:T(8,128)(2,1)} %bitcast.14), custom_call_target="tpu_custom_call" | custom-call | bytes 1048576 | tf_op jit(solution)/shard_map/pallas_call | solution.py:170
  5.0 2.4 %collective-permute-start.6 = (bf16[1,112,296]{2,1,0:T(8,128)(2,1)S(1)}, bf16[1,112,296]{2,1,0:T(8,128)(2,1)S(1)}, u32[]{:S(2)}, u32[]{:S(2)}) collective-permute-start(bf16[1,112,296]{2,1,0:T(8,128)(2,1)S(1)} %get-tuple-element.18), channel_id=1, source_target_pairs={{0,2},{1,3},{2,0},{3,1},{4,6},{5,7},{6,4},{7,5},{8,10},{9,11},{10,... | collective-permute-start | bytes 198920 | tf_op jit(solution)/shard_map/ppermute | solution.py:197
  7.4 0.0 collective-permute-start.7
  7.4 1.3 %collective-permute-start.4 = (bf16[1,448,296]{2,1,0:T(8,128)(2,1)S(1)}, bf16[1,448,296]{2,1,0:T(8,128)(2,1)S(1)}, u32[]{:S(2)}, u32[]{:S(2)}) collective-permute-start(bf16[1,448,296]{2,1,0:T(8,128)(2,1)S(1)} %get-tuple-element.17), channel_id=1, source_target_pairs={{0,1},{1,0},{2,3},{3,2},{4,5},{5,4},{6,7},{7,6},{8,9},{9,8},{10,11... | collective-permute-start | bytes 795656 | tf_op jit(solution)/shard_map/ppermute | solution.py:198
  8.6 3.1 %collective-permute-done.6 = bf16[1,112,296]{2,1,0:T(8,128)(2,1)S(1)} collective-permute-done((bf16[1,112,296]{2,1,0:T(8,128)(2,1)S(1)}, bf16[1,112,296]{2,1,0:T(8,128)(2,1)S(1)}, u32[]{:S(2)}, u32[]{:S(2)}) %collective-permute-start.6) | collective-permute-done | bytes 66336 | tf_op jit(solution)/shard_map/ppermute | solution.py:197
  11.8 1.6 %collective-permute-done.7 = bf16[1,112,296]{2,1,0:T(8,128)(2,1)S(1)} collective-permute-done((bf16[1,112,296]{2,1,0:T(8,128)(2,1)S(1)}, bf16[1,112,296]{2,1,0:T(8,128)(2,1)S(1)}, u32[]{:S(2)}, u32[]{:S(2)}) %collective-permute-start.7) | collective-permute-done | bytes 66336 | tf_op jit(solution)/shard_map/ppermute | solution.py:197
  13.4 3.0 %collective-permute-start.8 = (bf16[2,112,296]{2,1,0:T(8,128)(2,1)S(1)}, bf16[2,112,296]{2,1,0:T(8,128)(2,1)S(1)}, u32[]{:S(2)}, u32[]{:S(2)}) collective-permute-start(bf16[2,112,296]{2,1,0:T(8,128)(2,1)S(1)} %constant_dynamic-update-slice_fusion.3.refs_0_), channel_id=1, source_target_pairs={{0,8},{4,12},{8,0},{12,4},{16,24},{20,28},{24,16},{28,20},{1,9},{5... | collective-permute-start | bytes 397832 | tf_op jit(solution)/shard_map/ppermute | solution.py:204
  16.4 0.0 collective-permute-done
  16.4 0.0 collective-permute-done.1
  16.4 0.1 collective-permute-start.2
  16.5 4.1 %collective-permute-start.3 = (bf16[888,128]{1,0:T(8,128)(2,1)S(1)}, bf16[888,128]{1,0:T(8,128)(2,1)S(1)}, u32[]{:S(2)}, u32[]{:S(2)}) collective-permute-start(bf16[888,128]{1,0:T(8,128)(2,1)S(1)} %constant_dynamic-update-slice_fusion.column), channel_id=1, source_target_pairs={{1,2},{2,1},{5,6},{6,5},{9,10},{10,9},{13,14},{14,13},{17,18},{18,... | collective-permute-start | bytes 681992 | tf_op jit(solution)/shard_map/ppermute | solution.py:196
  20.6 0.2 collective-permute-start.9
  20.8 0.0 collective-permute-done.4.close
  20.8 1.0 %collective-permute-start.5 = (bf16[1,448,296]{2,1,0:T(8,128)(2,1)S(1)}, bf16[1,448,296]{2,1,0:T(8,128)(2,1)S(1)}, u32[]{:S(2)}, u32[]{:S(2)}) collective-permute-start(bf16[1,448,296]{2,1,0:T(8,128)(2,1)S(1)} %collective-permute-done.4.close), channel_id=1, source_target_pairs={{0,4},{4,0},{8,12},{12,8},{16,20},{20,16},{24,28},{28,24},{1,5},{5... | collective-permute-start | bytes 795656 | tf_op jit(solution)/shard_map/ppermute | solution.py:205
  21.8 0.0 collective-permute-done.8.refs_1_
  21.8 1.5 %collective-permute-start.13 = (bf16[2,112,296]{2,1,0:T(8,128)(2,1)S(1)}, bf16[2,112,296]{2,1,0:T(8,128)(2,1)S(1)}, u32[]{:S(2)}, u32[]{:S(2)}) collective-permute-start(bf16[2,112,296]{2,1,0:T(8,128)(2,1)S(1)} %collective-permute-done.8.refs_1_), channel_id=1, source_target_pairs={{0,16},{4,20},{8,24},{12,28},{16,0},{20,4},{24,8},{28,12},{1,17},{... | collective-permute-start | bytes 397832 | tf_op jit(solution)/shard_map/ppermute | solution.py:204
  23.4 2.3 %collective-permute-done.9.refs_2_ = bf16[2,112,296]{2,1,0:T(8,128)(2,1)S(1)} collective-permute-done((bf16[2,112,296]{2,1,0:T(8,128)(2,1)S(1)}, bf16[2,112,296]{2,1,0:T(8,128)(2,1)S(1)}, u32[]{:S(2)}, u32[]{:S(2)}) %collective-permute-start.9) | collective-permute-done | bytes 132640 | tf_op jit(solution)/shard_map/ppermute | solution.py:204
  25.7 3.2 %collective-permute-start.10 = (bf16[2,112,296]{2,1,0:T(8,128)(2,1)S(1)}, bf16[2,112,296]{2,1,0:T(8,128)(2,1)S(1)}, u32[]{:S(2)}, u32[]{:S(2)}) collective-permute-start(bf16[2,112,296]{2,1,0:T(8,128)(2,1)S(1)} %constant_dynamic-update-slice_fusion.3.refs_0_), channel_id=1, source_target_pairs={{0,4},{4,0},{8,12},{12,8},{16,20},{20,16},{24,28},{28,24},{1,5},{5... | collective-permute-start | bytes 397832 | tf_op jit(solution)/shard_map/ppermute | solution.py:206
  28.9 0.0 collective-permute-done.2.near
  28.9 0.0 collective-permute-start.11
  28.9 0.0 collective-permute-done.3.far
  28.9 0.5 %collective-permute-start.12 = (bf16[2,112,296]{2,1,0:T(8,128)(2,1)S(1)}, bf16[2,112,296]{2,1,0:T(8,128)(2,1)S(1)}, u32[]{:S(2)}, u32[]{:S(2)}) collective-permute-start(bf16[2,112,296]{2,1,0:T(8,128)(2,1)S(1)} %collective-permute-done.9.refs_2_), channel_id=1, source_target_pairs={{0,4},{4,0},{8,12},{12,8},{16,20},{20,16},{24,28},{28,24},{1,5},{5... | collective-permute-start | bytes 397832 | tf_op jit(solution)/shard_map/ppermute | solution.py:206
  29.4 0.0 collective-permute-done.13.piece
  29.4 1.8 %collective-permute-start.14 = (bf16[2,112,296]{2,1,0:T(8,128)(2,1)S(1)}, bf16[2,112,296]{2,1,0:T(8,128)(2,1)S(1)}, u32[]{:S(2)}, u32[]{:S(2)}) collective-permute-start(bf16[2,112,296]{2,1,0:T(8,128)(2,1)S(1)} %collective-permute-done.13.piece), channel_id=1, source_target_pairs={{0,4},{4,0},{8,12},{12,8},{16,20},{20,16},{24,28},{28,24},{1,5},{5... | collective-permute-start | bytes 397832 | tf_op jit(solution)/shard_map/ppermute | solution.py:206
  31.2 0.0 copy-done.2
  31.2 0.0 copy-done.3
  31.2 0.0 copy-done.1
  31.2 0.0 copy-done.4
  31.2 0.8 %shard_map.65 = (bf16[12,296,128]{2,1,0:T(8,128)(2,1)S(1)}, s32[12,128]{1,0:T(8,128)S(1)}, bf16[296,296]{1,0:T(8,128)(2,1)S(1)}) custom-call(s32[1,128]{1,0:T(1,128)S(1)} %copy-done.4, s32[12,1,128]{2,1,0:T(1,128)S(1)} %bitcast.10, s32[12,1,128]{2,1,0:T(1,128)S(1)} %bitcast.11, bf16[888,128]{1,0:T(8,128)(2,1)S(1)} %constant_dynamic-update-slice_fusion.column, ...), custom_call_target="tpu_custom_call" | custom-call | flops 349175808 | bytes 1048576 | tf_op jit(solution)/shard_map/pallas_call | solution.py:170
  32.0 0.0 copy-start
  32.0 1.1 %shard_map.66.picked = bf16[12,128,296]{2,1,0:T(8,128)(2,1)S(1)} custom-call(s32[12,128]{1,0:T(8,128)S(1)} %get-tuple-element.15.index, bf16[12,296,128]{2,1,0:T(8,128)(2,1)S(1)} %get-tuple-element.16.part, bf16[888,128]{1,0:T(8,128)(2,1)S(1)} %collective-permute-done.2.near, bf16[888,128]{1,0:T(8,128)(2,1)S(1)} %collective-permute-done.3.far), custom_call_target="tpu_custom_call" | custom-call | flops 698351616 | bytes 1048576 | tf_op jit(solution)/shard_map/pallas_call | solution.py:170
  33.1 0.0 collective-permute-done.10.refs_3_
  33.1 0.0 collective-permute-done.11.refs_4_
  33.1 0.0 collective-permute-done.12.refs_5_
  33.1 0.0 collective-permute-done.5.close_twin
  33.1 0.0 copy-done
  33.1 0.7 %shard_map.67 = (f32[128,296]{1,0:T(8,128)S(1)}, bf16[2,896,296]{2,1,0:T(8,128)(2,1)S(1)}) custom-call(bf16[12,128,296]{2,1,0:T(8,128)(2,1)S(1)} %shard_map.66.picked, bf16[3,296,296]{2,1,0:T(8,128)(2,1)S(1)} %copy-done, bf16[1,448,296]{2,1,0:T(8,128)(2,1)S(1)} %collective-permute-done.4.close, bf16[1,448,296]{2,1,0:T(8,128)(2,1)S(1)} %collective-permute-done.5.close_twin, ...), custom_call_target="tpu_custom_call" | custom-call | flops 134578176 | bytes 1048576 | tf_op jit(solution)/shard_map/pallas_call | solution.py:170
  33.8 0.0 collective-permute-done.14.twin
  33.8 1.5 %shard_map.68 = (f32[296,128]{1,0:T(8,128)}, bf16[2,896,296]{2,1,0:T(8,128)(2,1)S(1)}) custom-call(bf16[12,128,296]{2,1,0:T(8,128)(2,1)S(1)} %shard_map.66.picked, f32[128,296]{1,0:T(8,128)S(1)} %get-tuple-element.19.before, bf16[296,296]{1,0:T(8,128)(2,1)S(1)} %get-tuple-element.20.c2e, ...), custom_call_target="tpu_custom_call", output_to_operand_aliasing={{1}: (5, {})} | custom-call | flops 269156352 | bytes 1048576 | tf_op jit(solution)/shard_map/pallas_call | solution.py:170
  (5 shorter events, 0.1 us)
Async XLA Ops:
  0.0 31.2 %copy-start.2 = (s32[1,128,12]{1,0,2:T(1,128)S(1)}, s32[1,128,12]{1,0,2:T(1,128)}, u32[]{:S(2)}) copy-start(s32[1,128,12]{1,0,2:T(1,128)} %param.8) | copy-start | bytes 18436
  0.0 31.2 %copy-start.3 = (s32[1,128,12]{1,0,2:T(1,128)S(1)}, s32[1,128,12]{1,0,2:T(1,128)}, u32[]{:S(2)}) copy-start(s32[1,128,12]{1,0,2:T(1,128)} %param.9) | copy-start | bytes 18436
  0.0 31.2 %copy-start.1 = (bf16[296,296]{1,0:T(8,128)(2,1)S(1)}, bf16[296,296]{1,0:T(8,128)(2,1)}, u32[]{:S(2)}) copy-start(bf16[296,296]{1,0:T(8,128)(2,1)} %c2e.1) | copy-start | bytes 525700
  0.0 31.2 %copy-start.4 = (s32[1,128]{1,0:T(1,128)S(1)}, s32[1,128]{1,0:T(1,128)}, u32[]{:S(2)}) copy-start(s32[1,128]{1,0:T(1,128)} %counts.1) | copy-start | bytes 1540
  0.0 16.3 %collective-permute-start = (bf16[296,128]{1,0:T(8,128)(2,1)}, bf16[296,128]{1,0:T(8,128)(2,1)S(1)}, u32[]{:S(2)}, u32[]{:S(2)}) collective-permute-start(bf16[296,128]{1,0:T(8,128)(2,1)} %bitcast.12), channel_id=1, source_target_pairs={{0,4},{4,0},{8,12},{12,8},{16,20},{20,16},{24,28},{28,24},{1,5},{5... | collective-permute-start | bytes 227336 | tf_op jit(solution)/shard_map/ppermute | solution.py:192
  0.8 15.6 %collective-permute-start.1 = (bf16[296,128]{1,0:T(8,128)(2,1)}, bf16[296,128]{1,0:T(8,128)(2,1)S(1)}, u32[]{:S(2)}, u32[]{:S(2)}) collective-permute-start(bf16[296,128]{1,0:T(8,128)(2,1)} %bitcast.13), channel_id=1, source_target_pairs={{4,8},{8,4},{12,16},{16,12},{20,24},{24,20},{5,9},{9,5},{13,17},{1... | collective-permute-start | bytes 227336 | tf_op jit(solution)/shard_map/ppermute | solution.py:193
  5.0 6.8 %collective-permute-start.6 = (bf16[1,112,296]{2,1,0:T(8,128)(2,1)S(1)}, bf16[1,112,296]{2,1,0:T(8,128)(2,1)S(1)}, u32[]{:S(2)}, u32[]{:S(2)}) collective-permute-start(bf16[1,112,296]{2,1,0:T(8,128)(2,1)S(1)} %get-tuple-element.18), channel_id=1, source_target_pairs={{0,2},{1,3},{2,0},{3,1},{4,6},{5,7},{6,4},{7,5},{8,10},{9,11},{10,... | collective-permute-start | bytes 198920 | tf_op jit(solution)/shard_map/ppermute | solution.py:197
  7.4 6.0 %collective-permute-start.7 = (bf16[1,112,296]{2,1,0:T(8,128)(2,1)S(1)}, bf16[1,112,296]{2,1,0:T(8,128)(2,1)S(1)}, u32[]{:S(2)}, u32[]{:S(2)}) collective-permute-start(bf16[1,112,296]{2,1,0:T(8,128)(2,1)S(1)} %get-tuple-element.18), channel_id=1, source_target_pairs={{0,3},{1,2},{2,1},{3,0},{4,7},{5,6},{6,5},{7,4},{8,11},{9,10},{10,... | collective-permute-start | bytes 198920 | tf_op jit(solution)/shard_map/ppermute | solution.py:197
  7.4 13.4 %collective-permute-start.4 = (bf16[1,448,296]{2,1,0:T(8,128)(2,1)S(1)}, bf16[1,448,296]{2,1,0:T(8,128)(2,1)S(1)}, u32[]{:S(2)}, u32[]{:S(2)}) collective-permute-start(bf16[1,448,296]{2,1,0:T(8,128)(2,1)S(1)} %get-tuple-element.17), channel_id=1, source_target_pairs={{0,1},{1,0},{2,3},{3,2},{4,5},{5,4},{6,7},{7,6},{8,9},{9,8},{10,11... | collective-permute-start | bytes 795656 | tf_op jit(solution)/shard_map/ppermute | solution.py:198
  13.4 8.5 %collective-permute-start.8 = (bf16[2,112,296]{2,1,0:T(8,128)(2,1)S(1)}, bf16[2,112,296]{2,1,0:T(8,128)(2,1)S(1)}, u32[]{:S(2)}, u32[]{:S(2)}) collective-permute-start(bf16[2,112,296]{2,1,0:T(8,128)(2,1)S(1)} %constant_dynamic-update-slice_fusion.3.refs_0_), channel_id=1, source_target_pairs={{0,8},{4,12},{8,0},{12,4},{16,24},{20,28},{24,16},{28,20},{1,9},{5... | collective-permute-start | bytes 397832 | tf_op jit(solution)/shard_map/ppermute | solution.py:204
  16.4 12.5 %collective-permute-start.2 = (bf16[888,128]{1,0:T(8,128)(2,1)S(1)}, bf16[888,128]{1,0:T(8,128)(2,1)S(1)}, u32[]{:S(2)}, u32[]{:S(2)}) collective-permute-start(bf16[888,128]{1,0:T(8,128)(2,1)S(1)} %constant_dynamic-update-slice_fusion.column), channel_id=1, source_target_pairs={{0,1},{1,0},{2,3},{3,2},{4,5},{5,4},{6,7},{7,6},{8,9},{9,8},{10,11... | collective-permute-start | bytes 681992 | tf_op jit(solution)/shard_map/ppermute | solution.py:195
  16.5 12.4 %collective-permute-start.3 = (bf16[888,128]{1,0:T(8,128)(2,1)S(1)}, bf16[888,128]{1,0:T(8,128)(2,1)S(1)}, u32[]{:S(2)}, u32[]{:S(2)}) collective-permute-start(bf16[888,128]{1,0:T(8,128)(2,1)S(1)} %constant_dynamic-update-slice_fusion.column), channel_id=1, source_target_pairs={{1,2},{2,1},{5,6},{6,5},{9,10},{10,9},{13,14},{14,13},{17,18},{18,... | collective-permute-start | bytes 681992 | tf_op jit(solution)/shard_map/ppermute | solution.py:196
  20.6 5.1 %collective-permute-start.9 = (bf16[2,112,296]{2,1,0:T(8,128)(2,1)S(1)}, bf16[2,112,296]{2,1,0:T(8,128)(2,1)S(1)}, u32[]{:S(2)}, u32[]{:S(2)}) collective-permute-start(bf16[2,112,296]{2,1,0:T(8,128)(2,1)S(1)} %constant_dynamic-update-slice_fusion.3.refs_0_), channel_id=1, source_target_pairs={{0,16},{4,20},{8,24},{12,28},{16,0},{20,4},{24,8},{28,12},{1,17},{... | collective-permute-start | bytes 397832 | tf_op jit(solution)/shard_map/ppermute | solution.py:204
  20.8 12.3 %collective-permute-start.5 = (bf16[1,448,296]{2,1,0:T(8,128)(2,1)S(1)}, bf16[1,448,296]{2,1,0:T(8,128)(2,1)S(1)}, u32[]{:S(2)}, u32[]{:S(2)}) collective-permute-start(bf16[1,448,296]{2,1,0:T(8,128)(2,1)S(1)} %collective-permute-done.4.close), channel_id=1, source_target_pairs={{0,4},{4,0},{8,12},{12,8},{16,20},{20,16},{24,28},{28,24},{1,5},{5... | collective-permute-start | bytes 795656 | tf_op jit(solution)/shard_map/ppermute | solution.py:205
  21.8 7.6 %collective-permute-start.13 = (bf16[2,112,296]{2,1,0:T(8,128)(2,1)S(1)}, bf16[2,112,296]{2,1,0:T(8,128)(2,1)S(1)}, u32[]{:S(2)}, u32[]{:S(2)}) collective-permute-start(bf16[2,112,296]{2,1,0:T(8,128)(2,1)S(1)} %collective-permute-done.8.refs_1_), channel_id=1, source_target_pairs={{0,16},{4,20},{8,24},{12,28},{16,0},{20,4},{24,8},{28,12},{1,17},{... | collective-permute-start | bytes 397832 | tf_op jit(solution)/shard_map/ppermute | solution.py:204
  25.7 7.4 %collective-permute-start.10 = (bf16[2,112,296]{2,1,0:T(8,128)(2,1)S(1)}, bf16[2,112,296]{2,1,0:T(8,128)(2,1)S(1)}, u32[]{:S(2)}, u32[]{:S(2)}) collective-permute-start(bf16[2,112,296]{2,1,0:T(8,128)(2,1)S(1)} %constant_dynamic-update-slice_fusion.3.refs_0_), channel_id=1, source_target_pairs={{0,4},{4,0},{8,12},{12,8},{16,20},{20,16},{24,28},{28,24},{1,5},{5... | collective-permute-start | bytes 397832 | tf_op jit(solution)/shard_map/ppermute | solution.py:206
  28.9 4.2 %collective-permute-start.11 = (bf16[2,112,296]{2,1,0:T(8,128)(2,1)S(1)}, bf16[2,112,296]{2,1,0:T(8,128)(2,1)S(1)}, u32[]{:S(2)}, u32[]{:S(2)}) collective-permute-start(bf16[2,112,296]{2,1,0:T(8,128)(2,1)S(1)} %collective-permute-done.8.refs_1_), channel_id=1, source_target_pairs={{0,4},{4,0},{8,12},{12,8},{16,20},{20,16},{24,28},{28,24},{1,5},{5... | collective-permute-start | bytes 397832 | tf_op jit(solution)/shard_map/ppermute | solution.py:206
  28.9 4.2 %collective-permute-start.12 = (bf16[2,112,296]{2,1,0:T(8,128)(2,1)S(1)}, bf16[2,112,296]{2,1,0:T(8,128)(2,1)S(1)}, u32[]{:S(2)}, u32[]{:S(2)}) collective-permute-start(bf16[2,112,296]{2,1,0:T(8,128)(2,1)S(1)} %collective-permute-done.9.refs_2_), channel_id=1, source_target_pairs={{0,4},{4,0},{8,12},{12,8},{16,20},{20,16},{24,28},{28,24},{1,5},{5... | collective-permute-start | bytes 397832 | tf_op jit(solution)/shard_map/ppermute | solution.py:206
  29.4 4.4 %collective-permute-start.14 = (bf16[2,112,296]{2,1,0:T(8,128)(2,1)S(1)}, bf16[2,112,296]{2,1,0:T(8,128)(2,1)S(1)}, u32[]{:S(2)}, u32[]{:S(2)}) collective-permute-start(bf16[2,112,296]{2,1,0:T(8,128)(2,1)S(1)} %collective-permute-done.13.piece), channel_id=1, source_target_pairs={{0,4},{4,0},{8,12},{12,8},{16,20},{20,16},{24,28},{28,24},{1,5},{5... | collective-permute-start | bytes 397832 | tf_op jit(solution)/shard_map/ppermute | solution.py:206
  32.0 1.1 %copy-start = (bf16[3,296,296]{2,1,0:T(8,128)(2,1)S(1)}, bf16[3,296,296]{2,1,0:T(8,128)(2,1)}, u32[]{:S(2)}) copy-start(bf16[3,296,296]{2,1,0:T(8,128)(2,1)} %own.1) | copy-start | bytes 1577092

commit v4 on v3

--- a/solution.py
+++ b/solution.py
@@ -13,9 +13,18 @@
 
 
 def pairs_odd(count):
-    out = []
+    out = [(0, count - 1), (count - 1, 0)]
     for i in range(1, count - 1, 2):
         out += [(i, i + 1), (i + 1, i)]
+    return out
+
+
+def pairs_far(segs, lanes):
+    ends = (0, lanes - 1)
+    out = [(i * lanes + j, (i ^ 1) * lanes + j) for i in range(segs) for j in ends]
+    for i, j in pairs_odd(lanes):
+        if i not in ends:
+            out += [(k * lanes + i, k * lanes + j) for k in range(segs)]
     return out
 
 
@@ -193,7 +202,7 @@
     other = lax.ppermute(block, "morton", pairs_odd(segs))
     column = jnp.concatenate([block_near, twin, other], axis=0)
     near = lax.ppermute(column, "lane", pairs_xor(lanes, 1))
-    far = lax.ppermute(column, "lane", pairs_odd(lanes))
+    far = lax.ppermute(column, ("morton", "lane"), pairs_far(segs, lanes))
     landed = [lax.ppermute(small, "lane", pairs_xor(lanes, k)) for k in range(2, lanes)]
     close = lax.ppermute(mid, "lane", pairs_xor(lanes, 1))
 

time: 35.5 us -> 32.5 us (0.915)
  the two profiles are of different devices: /device:TPU:9 before, /device:TPU:0 now
where the time goes in v4:
time: 32.5 us; the launch traced here: 32.3 us
  waiting for transfers between devices  13.7 us (42%)
  starting transfers between devices  13.2 us (41%)
  Pallas kernels  5.17 us (16%)
    ppermute x2, waiting for transfers between devices, per_device(): lax.ppermute(small, 'lane', pairs_xor(lanes, k))  5.6 us
    pallas_call x5, Pallas kernels, call(): pl.pallas_call(kernel, out_shape=out, in_specs=specs or [vmem] * len(args...  5.17 us
    ppermute x3, waiting for transfers between devices, per_device(): lax.ppermute(piece, 'morton', pairs_xor(segs, 2 * step))  4.62 us
    ppermute x2, starting transfers between devices, per_device(): lax.ppermute(small, 'lane', pairs_xor(lanes, k))  4 us
    ppermute x1, starting transfers between devices, per_device(): other = lax.ppermute(block, 'morton', pairs_odd(segs))  3.54 us
    ppermute x1, waiting for transfers between devices, per_device(): close = lax.ppermute(mid, 'lane', pairs_xor(lanes, 1))  3.05 us
    ppermute x1, starting transfers between devices, per_device(): near = lax.ppermute(column, 'lane', pairs_xor(lanes, 1))  2.37 us
    ppermute x3, starting transfers between devices, per_device(): lax.ppermute(piece, 'morton', pairs_xor(segs, 2 * step))  1.95 us
  transfers between devices with their start and end apart: 15, of which 6 were waited for; matrix products, arithmetic and copies ran while one was open for 0% of the time, Pallas kernels for 11%

profile of v4, /device:TPU:0, one launch (start us, length us, event | category | flops | bytes accessed | tf_op | source)
XLA Modules:
  0.0 32.3 jit_solution(4484421549625945298)
XLA Ops:
  0.0 0.0 copy-start.2
  0.0 0.0 copy-start.3
  0.0 0.0 copy-start.1
  0.0 0.0 copy-start.4
  0.0 0.6 %collective-permute-start = (bf16[296,128]{1,0:T(8,128)(2,1)}, bf16[296,128]{1,0:T(8,128)(2,1)S(1)}, u32[]{:S(2)}, u32[]{:S(2)}) collective-permute-start(bf16[296,128]{1,0:T(8,128)(2,1)} %bitcast.12), channel_id=1, source_target_pairs={{0,4},{4,0},{8,12},{12,8},{16,20},{20,16},{24,28},{28,24},{1,5},{5... | collective-permute-start | bytes 227336 | tf_op jit(solution)/shard_map/ppermute | solution.py:201
  0.6 3.5 %collective-permute-start.1 = (bf16[296,128]{1,0:T(8,128)(2,1)}, bf16[296,128]{1,0:T(8,128)(2,1)S(1)}, u32[]{:S(2)}, u32[]{:S(2)}) collective-permute-start(bf16[296,128]{1,0:T(8,128)(2,1)} %bitcast.13), channel_id=1, source_target_pairs={{0,28},{28,0},{4,8},{8,4},{12,16},{16,12},{20,24},{24,20},{1,29},{... | collective-permute-start | bytes 227336 | tf_op jit(solution)/shard_map/ppermute | solution.py:202
  4.1 1.1 %shard_map.64 = (bf16[1,112,296]{2,1,0:T(8,128)(2,1)S(1)}, bf16[1,448,296]{2,1,0:T(8,128)(2,1)S(1)}, bf16[296,128]{1,0:T(8,128)(2,1)S(1)}) custom-call(bf16[888,296]{1,0:T(8,128)(2,1)} %bitcast.9, bf16[296,128]{1,0:T(8,128)(2,1)} %bitcast.14), custom_call_target="tpu_custom_call" | custom-call | bytes 1048576 | tf_op jit(solution)/shard_map/pallas_call | solution.py:179
  5.2 2.7 %collective-permute-start.6 = (bf16[1,112,296]{2,1,0:T(8,128)(2,1)S(1)}, bf16[1,112,296]{2,1,0:T(8,128)(2,1)S(1)}, u32[]{:S(2)}, u32[]{:S(2)}) collective-permute-start(bf16[1,112,296]{2,1,0:T(8,128)(2,1)S(1)} %get-tuple-element.18), channel_id=1, source_target_pairs={{0,2},{1,3},{2,0},{3,1},{4,6},{5,7},{6,4},{7,5},{8,10},{9,11},{10,... | collective-permute-start | bytes 198920 | tf_op jit(solution)/shard_map/ppermute | solution.py:206
  7.9 1.3 %collective-permute-start.7 = (bf16[1,112,296]{2,1,0:T(8,128)(2,1)S(1)}, bf16[1,112,296]{2,1,0:T(8,128)(2,1)S(1)}, u32[]{:S(2)}, u32[]{:S(2)}) collective-permute-start(bf16[1,112,296]{2,1,0:T(8,128)(2,1)S(1)} %get-tuple-element.18), channel_id=1, source_target_pairs={{0,3},{1,2},{2,1},{3,0},{4,7},{5,6},{6,5},{7,4},{8,11},{9,10},{10,... | collective-permute-start | bytes 198920 | tf_op jit(solution)/shard_map/ppermute | solution.py:206
  9.2 0.2 collective-permute-start.4
  9.5 3.5 %collective-permute-done.6 = bf16[1,112,296]{2,1,0:T(8,128)(2,1)S(1)} collective-permute-done((bf16[1,112,296]{2,1,0:T(8,128)(2,1)S(1)}, bf16[1,112,296]{2,1,0:T(8,128)(2,1)S(1)}, u32[]{:S(2)}, u32[]{:S(2)}) %collective-permute-start.6) | collective-permute-done | bytes 66336 | tf_op jit(solution)/shard_map/ppermute | solution.py:206
  13.0 2.1 %collective-permute-done.7 = bf16[1,112,296]{2,1,0:T(8,128)(2,1)S(1)} collective-permute-done((bf16[1,112,296]{2,1,0:T(8,128)(2,1)S(1)}, bf16[1,112,296]{2,1,0:T(8,128)(2,1)S(1)}, u32[]{:S(2)}, u32[]{:S(2)}) %collective-permute-start.7) | collective-permute-done | bytes 66336 | tf_op jit(solution)/shard_map/ppermute | solution.py:206
  15.1 0.1 collective-permute-start.8
  15.2 0.0 collective-permute-done
  15.2 0.0 collective-permute-done.1
  15.2 2.4 %collective-permute-start.2 = (bf16[888,128]{1,0:T(8,128)(2,1)S(1)}, bf16[888,128]{1,0:T(8,128)(2,1)S(1)}, u32[]{:S(2)}, u32[]{:S(2)}) collective-permute-start(bf16[888,128]{1,0:T(8,128)(2,1)S(1)} %constant_dynamic-update-slice_fusion.column), channel_id=1, source_target_pairs={{0,1},{1,0},{2,3},{3,2},{4,5},{5,4},{6,7},{7,6},{8,9},{9,8},{10,11... | collective-permute-start | bytes 681992 | tf_op jit(solution)/shard_map/ppermute | solution.py:204
  17.6 0.0 collective-permute-start.3
  17.6 0.6 %collective-permute-start.9 = (bf16[2,112,296]{2,1,0:T(8,128)(2,1)S(1)}, bf16[2,112,296]{2,1,0:T(8,128)(2,1)S(1)}, u32[]{:S(2)}, u32[]{:S(2)}) collective-permute-start(bf16[2,112,296]{2,1,0:T(8,128)(2,1)S(1)} %constant_dynamic-update-slice_fusion.3.refs_0_), channel_id=1, source_target_pairs={{0,16},{4,20},{8,24},{12,28},{16,0},{20,4},{24,8},{28,12},{1,17},{... | collective-permute-start | bytes 397832 | tf_op jit(solution)/shard_map/ppermute | solution.py:213
  18.2 3.1 %collective-permute-done.4.close = bf16[1,448,296]{2,1,0:T(8,128)(2,1)S(1)} collective-permute-done((bf16[1,448,296]{2,1,0:T(8,128)(2,1)S(1)}, bf16[1,448,296]{2,1,0:T(8,128)(2,1)S(1)}, u32[]{:S(2)}, u32[]{:S(2)}) %collective-permute-start.4) | collective-permute-done | bytes 265248 | tf_op jit(solution)/shard_map/ppermute | solution.py:207
  21.2 0.0 collective-permute-start.5
  21.2 0.0 collective-permute-done.8.refs_1_
  21.2 1.3 %collective-permute-start.13 = (bf16[2,112,296]{2,1,0:T(8,128)(2,1)S(1)}, bf16[2,112,296]{2,1,0:T(8,128)(2,1)S(1)}, u32[]{:S(2)}, u32[]{:S(2)}) collective-permute-start(bf16[2,112,296]{2,1,0:T(8,128)(2,1)S(1)} %collective-permute-done.8.refs_1_), channel_id=1, source_target_pairs={{0,16},{4,20},{8,24},{12,28},{16,0},{20,4},{24,8},{28,12},{1,17},{... | collective-permute-start | bytes 397832 | tf_op jit(solution)/shard_map/ppermute | solution.py:213
  22.5 1.9 %collective-permute-done.9.refs_2_ = bf16[2,112,296]{2,1,0:T(8,128)(2,1)S(1)} collective-permute-done((bf16[2,112,296]{2,1,0:T(8,128)(2,1)S(1)}, bf16[2,112,296]{2,1,0:T(8,128)(2,1)S(1)}, u32[]{:S(2)}, u32[]{:S(2)}) %collective-permute-start.9) | collective-permute-done | bytes 132640 | tf_op jit(solution)/shard_map/ppermute | solution.py:213
  24.4 0.0 collective-permute-start.10
  24.4 0.4 %collective-permute-done.2.near = bf16[888,128]{1,0:T(8,128)(2,1)S(1)} collective-permute-done((bf16[888,128]{1,0:T(8,128)(2,1)S(1)}, bf16[888,128]{1,0:T(8,128)(2,1)S(1)}, u32[]{:S(2)}, u32[]{:S(2)}) %collective-permute-start.2) | collective-permute-done | bytes 227360 | tf_op jit(solution)/shard_map/ppermute | solution.py:204
  24.8 0.1 collective-permute-start.11
  25.0 0.0 collective-permute-done.3.far
  25.0 0.4 %collective-permute-start.12 = (bf16[2,112,296]{2,1,0:T(8,128)(2,1)S(1)}, bf16[2,112,296]{2,1,0:T(8,128)(2,1)S(1)}, u32[]{:S(2)}, u32[]{:S(2)}) collective-permute-start(bf16[2,112,296]{2,1,0:T(8,128)(2,1)S(1)} %collective-permute-done.9.refs_2_), channel_id=1, source_target_pairs={{0,4},{4,0},{8,12},{12,8},{16,20},{20,16},{24,28},{28,24},{1,5},{5... | collective-permute-start | bytes 397832 | tf_op jit(solution)/shard_map/ppermute | solution.py:215
  25.4 2.7 %collective-permute-done.13.piece = bf16[2,112,296]{2,1,0:T(8,128)(2,1)S(1)} collective-permute-done((bf16[2,112,296]{2,1,0:T(8,128)(2,1)S(1)}, bf16[2,112,296]{2,1,0:T(8,128)(2,1)S(1)}, u32[]{:S(2)}, u32[]{:S(2)}) %collective-permute-start.13) | collective-permute-done | bytes 132640 | tf_op jit(solution)/shard_map/ppermute | solution.py:213
  28.1 0.0 collective-permute-start.14
  28.1 0.0 copy-done.2
  28.1 0.0 copy-done.3
  28.1 0.0 copy-done.1
  28.1 0.0 copy-done.4
  28.1 0.8 %shard_map.65 = (bf16[12,296,128]{2,1,0:T(8,128)(2,1)S(1)}, s32[12,128]{1,0:T(8,128)S(1)}, bf16[296,296]{1,0:T(8,128)(2,1)S(1)}) custom-call(s32[1,128]{1,0:T(1,128)S(1)} %copy-done.4, s32[12,1,128]{2,1,0:T(1,128)S(1)} %bitcast.10, s32[12,1,128]{2,1,0:T(1,128)S(1)} %bitcast.11, bf16[888,128]{1,0:T(8,128)(2,1)S(1)} %constant_dynamic-update-slice_fusion.column, ...), custom_call_target="tpu_custom_call" | custom-call | flops 349175808 | bytes 1048576 | tf_op jit(solution)/shard_map/pallas_call | solution.py:179
  28.9 0.0 copy-start
  29.0 1.1 %shard_map.66.picked = bf16[12,128,296]{2,1,0:T(8,128)(2,1)S(1)} custom-call(s32[12,128]{1,0:T(8,128)S(1)} %get-tuple-element.15.index, bf16[12,296,128]{2,1,0:T(8,128)(2,1)S(1)} %get-tuple-element.16.part, bf16[888,128]{1,0:T(8,128)(2,1)S(1)} %collective-permute-done.2.near, bf16[888,128]{1,0:T(8,128)(2,1)S(1)} %collective-permute-done.3.far), custom_call_target="tpu_custom_call" | custom-call | flops 698351616 | bytes 1048576 | tf_op jit(solution)/shard_map/pallas_call | solution.py:179
  30.0 0.0 collective-permute-done.10.refs_3_
  30.0 0.0 collective-permute-done.11.refs_4_
  30.0 0.0 collective-permute-done.12.refs_5_
  30.0 0.0 collective-permute-done.5.close_twin
  30.1 0.0 copy-done
  30.1 0.7 %shard_map.67 = (f32[128,296]{1,0:T(8,128)S(1)}, bf16[2,896,296]{2,1,0:T(8,128)(2,1)S(1)}) custom-call(bf16[12,128,296]{2,1,0:T(8,128)(2,1)S(1)} %shard_map.66.picked, bf16[3,296,296]{2,1,0:T(8,128)(2,1)S(1)} %copy-done, bf16[1,448,296]{2,1,0:T(8,128)(2,1)S(1)} %collective-permute-done.4.close, bf16[1,448,296]{2,1,0:T(8,128)(2,1)S(1)} %collective-permute-done.5.close_twin, ...), custom_call_target="tpu_custom_call" | custom-call | flops 134578176 | bytes 1048576 | tf_op jit(solution)/shard_map/pallas_call | solution.py:179
  30.8 0.0 collective-permute-done.14.twin
  30.8 1.5 %shard_map.68 = (f32[296,128]{1,0:T(8,128)}, bf16[2,896,296]{2,1,0:T(8,128)(2,1)S(1)}) custom-call(bf16[12,128,296]{2,1,0:T(8,128)(2,1)S(1)} %shard_map.66.picked, f32[128,296]{1,0:T(8,128)S(1)} %get-tuple-element.19.before, bf16[296,296]{1,0:T(8,128)(2,1)S(1)} %get-tuple-element.20.c2e, ...), custom_call_target="tpu_custom_call", output_to_operand_aliasing={{1}: (5, {})} | custom-call | flops 269156352 | bytes 1048576 | tf_op jit(solution)/shard_map/pallas_call | solution.py:179
  (5 shorter events, 0.1 us)
Async XLA Ops:
  0.0 28.1 %copy-start.2 = (s32[1,128,12]{1,0,2:T(1,128)S(1)}, s32[1,128,12]{1,0,2:T(1,128)}, u32[]{:S(2)}) copy-start(s32[1,128,12]{1,0,2:T(1,128)} %param.8) | copy-start | bytes 18436
  0.0 28.1 %copy-start.3 = (s32[1,128,12]{1,0,2:T(1,128)S(1)}, s32[1,128,12]{1,0,2:T(1,128)}, u32[]{:S(2)}) copy-start(s32[1,128,12]{1,0,2:T(1,128)} %param.9) | copy-start | bytes 18436
  0.0 28.1 %copy-start.1 = (bf16[296,296]{1,0:T(8,128)(2,1)S(1)}, bf16[296,296]{1,0:T(8,128)(2,1)}, u32[]{:S(2)}) copy-start(bf16[296,296]{1,0:T(8,128)(2,1)} %c2e.1) | copy-start | bytes 525700
  0.0 28.1 %copy-start.4 = (s32[1,128]{1,0:T(1,128)S(1)}, s32[1,128]{1,0:T(1,128)}, u32[]{:S(2)}) copy-start(s32[1,128]{1,0:T(1,128)} %counts.1) | copy-start | bytes 1540
  0.0 15.2 %collective-permute-start = (bf16[296,128]{1,0:T(8,128)(2,1)}, bf16[296,128]{1,0:T(8,128)(2,1)S(1)}, u32[]{:S(2)}, u32[]{:S(2)}) collective-permute-start(bf16[296,128]{1,0:T(8,128)(2,1)} %bitcast.12), channel_id=1, source_target_pairs={{0,4},{4,0},{8,12},{12,8},{16,20},{20,16},{24,28},{28,24},{1,5},{5... | collective-permute-start | bytes 227336 | tf_op jit(solution)/shard_map/ppermute | solution.py:201
  0.6 14.6 %collective-permute-start.1 = (bf16[296,128]{1,0:T(8,128)(2,1)}, bf16[296,128]{1,0:T(8,128)(2,1)S(1)}, u32[]{:S(2)}, u32[]{:S(2)}) collective-permute-start(bf16[296,128]{1,0:T(8,128)(2,1)} %bitcast.13), channel_id=1, source_target_pairs={{0,28},{28,0},{4,8},{8,4},{12,16},{16,12},{20,24},{24,20},{1,29},{... | collective-permute-start | bytes 227336 | tf_op jit(solution)/shard_map/ppermute | solution.py:202
  5.2 7.8 %collective-permute-start.6 = (bf16[1,112,296]{2,1,0:T(8,128)(2,1)S(1)}, bf16[1,112,296]{2,1,0:T(8,128)(2,1)S(1)}, u32[]{:S(2)}, u32[]{:S(2)}) collective-permute-start(bf16[1,112,296]{2,1,0:T(8,128)(2,1)S(1)} %get-tuple-element.18), channel_id=1, source_target_pairs={{0,2},{1,3},{2,0},{3,1},{4,6},{5,7},{6,4},{7,5},{8,10},{9,11},{10,... | collective-permute-start | bytes 198920 | tf_op jit(solution)/shard_map/ppermute | solution.py:206
  7.9 7.2 %collective-permute-start.7 = (bf16[1,112,296]{2,1,0:T(8,128)(2,1)S(1)}, bf16[1,112,296]{2,1,0:T(8,128)(2,1)S(1)}, u32[]{:S(2)}, u32[]{:S(2)}) collective-permute-start(bf16[1,112,296]{2,1,0:T(8,128)(2,1)S(1)} %get-tuple-element.18), channel_id=1, source_target_pairs={{0,3},{1,2},{2,1},{3,0},{4,7},{5,6},{6,5},{7,4},{8,11},{9,10},{10,... | collective-permute-start | bytes 198920 | tf_op jit(solution)/shard_map/ppermute | solution.py:206
  9.2 12.0 %collective-permute-start.4 = (bf16[1,448,296]{2,1,0:T(8,128)(2,1)S(1)}, bf16[1,448,296]{2,1,0:T(8,128)(2,1)S(1)}, u32[]{:S(2)}, u32[]{:S(2)}) collective-permute-start(bf16[1,448,296]{2,1,0:T(8,128)(2,1)S(1)} %get-tuple-element.17), channel_id=1, source_target_pairs={{0,1},{1,0},{2,3},{3,2},{4,5},{5,4},{6,7},{7,6},{8,9},{9,8},{10,11... | collective-permute-start | bytes 795656 | tf_op jit(solution)/shard_map/ppermute | solution.py:207
  15.1 6.1 %collective-permute-start.8 = (bf16[2,112,296]{2,1,0:T(8,128)(2,1)S(1)}, bf16[2,112,296]{2,1,0:T(8,128)(2,1)S(1)}, u32[]{:S(2)}, u32[]{:S(2)}) collective-permute-start(bf16[2,112,296]{2,1,0:T(8,128)(2,1)S(1)} %constant_dynamic-update-slice_fusion.3.refs_0_), channel_id=1, source_target_pairs={{0,8},{4,12},{8,0},{12,4},{16,24},{20,28},{24,16},{28,20},{1,9},{5... | collective-permute-start | bytes 397832 | tf_op jit(solution)/shard_map/ppermute | solution.py:213
  15.2 9.6 %collective-permute-start.2 = (bf16[888,128]{1,0:T(8,128)(2,1)S(1)}, bf16[888,128]{1,0:T(8,128)(2,1)S(1)}, u32[]{:S(2)}, u32[]{:S(2)}) collective-permute-start(bf16[888,128]{1,0:T(8,128)(2,1)S(1)} %constant_dynamic-update-slice_fusion.column), channel_id=1, source_target_pairs={{0,1},{1,0},{2,3},{3,2},{4,5},{5,4},{6,7},{7,6},{8,9},{9,8},{10,11... | collective-permute-start | bytes 681992 | tf_op jit(solution)/shard_map/ppermute | solution.py:204
  17.6 7.4 %collective-permute-start.3 = (bf16[888,128]{1,0:T(8,128)(2,1)S(1)}, bf16[888,128]{1,0:T(8,128)(2,1)S(1)}, u32[]{:S(2)}, u32[]{:S(2)}) collective-permute-start(bf16[888,128]{1,0:T(8,128)(2,1)S(1)} %constant_dynamic-update-slice_fusion.column), channel_id=1, source_target_pairs={{0,4},{3,7},{4,0},{7,3},{8,12},{11,15},{12,8},{15,11},{16,20},{19,... | collective-permute-start | bytes 681992 | tf_op jit(solution)/shard_map/ppermute | solution.py:205
  17.6 6.8 %collective-permute-start.9 = (bf16[2,112,296]{2,1,0:T(8,128)(2,1)S(1)}, bf16[2,112,296]{2,1,0:T(8,128)(2,1)S(1)}, u32[]{:S(2)}, u32[]{:S(2)}) collective-permute-start(bf16[2,112,296]{2,1,0:T(8,128)(2,1)S(1)} %constant_dynamic-update-slice_fusion.3.refs_0_), channel_id=1, source_target_pairs={{0,16},{4,20},{8,24},{12,28},{16,0},{20,4},{24,8},{28,12},{1,17},{... | collective-permute-start | bytes 397832 | tf_op jit(solution)/shard_map/ppermute | solution.py:213
  21.2 8.8 %collective-permute-start.5 = (bf16[1,448,296]{2,1,0:T(8,128)(2,1)S(1)}, bf16[1,448,296]{2,1,0:T(8,128)(2,1)S(1)}, u32[]{:S(2)}, u32[]{:S(2)}) collective-permute-start(bf16[1,448,296]{2,1,0:T(8,128)(2,1)S(1)} %collective-permute-done.4.close), channel_id=1, source_target_pairs={{0,4},{4,0},{8,12},{12,8},{16,20},{20,16},{24,28},{28,24},{1,5},{5... | collective-permute-start | bytes 795656 | tf_op jit(solution)/shard_map/ppermute | solution.py:214
  21.2 6.8 %collective-permute-start.13 = (bf16[2,112,296]{2,1,0:T(8,128)(2,1)S(1)}, bf16[2,112,296]{2,1,0:T(8,128)(2,1)S(1)}, u32[]{:S(2)}, u32[]{:S(2)}) collective-permute-start(bf16[2,112,296]{2,1,0:T(8,128)(2,1)S(1)} %collective-permute-done.8.refs_1_), channel_id=1, source_target_pairs={{0,16},{4,20},{8,24},{12,28},{16,0},{20,4},{24,8},{28,12},{1,17},{... | collective-permute-start | bytes 397832 | tf_op jit(solution)/shard_map/ppermute | solution.py:213
  24.4 5.6 %collective-permute-start.10 = (bf16[2,112,296]{2,1,0:T(8,128)(2,1)S(1)}, bf16[2,112,296]{2,1,0:T(8,128)(2,1)S(1)}, u32[]{:S(2)}, u32[]{:S(2)}) collective-permute-start(bf16[2,112,296]{2,1,0:T(8,128)(2,1)S(1)} %constant_dynamic-update-slice_fusion.3.refs_0_), channel_id=1, source_target_pairs={{0,4},{4,0},{8,12},{12,8},{16,20},{20,16},{24,28},{28,24},{1,5},{5... | collective-permute-start | bytes 397832 | tf_op jit(solution)/shard_map/ppermute | solution.py:215
  24.8 5.2 %collective-permute-start.11 = (bf16[2,112,296]{2,1,0:T(8,128)(2,1)S(1)}, bf16[2,112,296]{2,1,0:T(8,128)(2,1)S(1)}, u32[]{:S(2)}, u32[]{:S(2)}) collective-permute-start(bf16[2,112,296]{2,1,0:T(8,128)(2,1)S(1)} %collective-permute-done.8.refs_1_), channel_id=1, source_target_pairs={{0,4},{4,0},{8,12},{12,8},{16,20},{20,16},{24,28},{28,24},{1,5},{5... | collective-permute-start | bytes 397832 | tf_op jit(solution)/shard_map/ppermute | solution.py:215
  25.0 5.1 %collective-permute-start.12 = (bf16[2,112,296]{2,1,0:T(8,128)(2,1)S(1)}, bf16[2,112,296]{2,1,0:T(8,128)(2,1)S(1)}, u32[]{:S(2)}, u32[]{:S(2)}) collective-permute-start(bf16[2,112,296]{2,1,0:T(8,128)(2,1)S(1)} %collective-permute-done.9.refs_2_), channel_id=1, source_target_pairs={{0,4},{4,0},{8,12},{12,8},{16,20},{20,16},{24,28},{28,24},{1,5},{5... | collective-permute-start | bytes 397832 | tf_op jit(solution)/shard_map/ppermute | solution.py:215
  28.1 2.7 %collective-permute-start.14 = (bf16[2,112,296]{2,1,0:T(8,128)(2,1)S(1)}, bf16[2,112,296]{2,1,0:T(8,128)(2,1)S(1)}, u32[]{:S(2)}, u32[]{:S(2)}) collective-permute-start(bf16[2,112,296]{2,1,0:T(8,128)(2,1)S(1)} %collective-permute-done.13.piece), channel_id=1, source_target_pairs={{0,4},{4,0},{8,12},{12,8},{16,20},{20,16},{24,28},{28,24},{1,5},{5... | collective-permute-start | bytes 397832 | tf_op jit(solution)/shard_map/ppermute | solution.py:215
  28.9 1.1 %copy-start = (bf16[3,296,296]{2,1,0:T(8,128)(2,1)S(1)}, bf16[3,296,296]{2,1,0:T(8,128)(2,1)}, u32[]{:S(2)}) copy-start(bf16[3,296,296]{2,1,0:T(8,128)(2,1)} %own.1) | copy-start | bytes 1577092

commit v5 on v4

--- a/solution.py
+++ b/solution.py
@@ -46,17 +46,62 @@
         pl.when(index == whole)(lambda: move(rest))
 
 
-def prep_kernel(flat, block, small, mid, block_out, sems):
+def packing(width, size):
+    full = width // 128
+    tail = width - 128 * full
+    fold = 128 // tail if tail else 1
+    third = 16 * -(-size // (16 * fold)) if tail else 0
+    return full, tail, fold, third
+
+
+def packed_rows(width, size):
+    full, _, _, third = packing(width, size)
+    return full * size + third
+
+
+def pack(out, part):
+    size, width = part.shape
+    full, tail, fold, third = packing(width, size)
+    for t in range(full):
+        out[t * size : (t + 1) * size, :] = part[:, t * 128 : (t + 1) * 128]
+    if not tail:
+        return
+    columns = []
+    for f in range(fold):
+        count = max(0, min(size - f * third, third))
+        column = []
+        if count:
+            column.append(part[f * third : f * third + count, 128 * full :])
+        if count < third:
+            column.append(jnp.zeros((third - count, tail), part.dtype))
+        columns.append(jnp.concatenate(column, axis=0) if len(column) > 1 else column[0])
+    if fold * tail < 128:
+        columns.append(jnp.zeros((third, 128 - fold * tail), part.dtype))
+    out[full * size :, :] = jnp.concatenate(columns, axis=1)
+
+
+def place_part(buffer, index, part, size):
+    full, tail, fold, third = packing(buffer.shape[1], size)
+    at = pl.multiple_of(index * size, 16)
+    for t in range(full):
+        buffer[pl.ds(at, size), t * 128 : (t + 1) * 128] = part[t * size : (t + 1) * size, :]
+    for f in range(fold if tail else 0):
+        count = min(size - f * third, third)
+        if count > 0:
+            spot = pl.ds(pl.multiple_of(at + f * third, 16), count)
+            buffer[spot, 128 * full :] = part[full * size : full * size + count, f * tail : (f + 1) * tail]
+
+
+def prep_kernel(flat, block, small, mid, block_out, small_raw, mid_raw, sems):
     seg_id = lax.axis_index("morton")
-
-    def parts(act):
-        for at, (out, index) in enumerate(((small, seg_id), (mid, seg_id % 2))):
-            copy_part(flat, out.at[0], out.shape[1], index, sems.at[at], act)
-
+    jobs = ((small_raw, seg_id, sems.at[0]), (mid_raw, seg_id % 2, sems.at[1]))
     whole = pltpu.make_async_copy(block, block_out, sems.at[2])
-    parts("start")
+    for raw, index, sem in jobs:
+        copy_part(flat, raw, raw.shape[0], index, sem, "start")
     whole.start()
-    parts("wait")
+    for (raw, index, sem), out in zip(jobs, (small, mid)):
+        copy_part(flat, raw, raw.shape[0], index, sem, "wait")
+        pack(out.at[0], raw[...])
     whole.wait()
 
 
@@ -127,35 +172,30 @@
     return total
 
 
-def place_part(buffer, index, part):
-    size = part.shape[0]
-    buffer[pl.ds(pl.multiple_of(index * size, 16), size), :] = part
-
-
-def place_pieces(buffer, seg_id, first, pieces, twins):
+def place_pieces(buffer, seg_id, first, pieces, twins, size):
     for k in range(pieces[0].shape[0]):
         for j, (piece, twin) in enumerate(zip(pieces, twins)):
-            place_part(buffer.at[k], seg_id ^ (2 * (first + j)), piece[k])
-            place_part(buffer.at[k], seg_id ^ (2 * (first + j) + 1), twin[k])
-
-
-def mid_kernel(per, width, count, picked, own, close, close_twin, *refs):
+            place_part(buffer.at[k], seg_id ^ (2 * (first + j)), piece[k], size)
+            place_part(buffer.at[k], seg_id ^ (2 * (first + j) + 1), twin[k], size)
+
+
+def mid_kernel(per, width, count, quarter, eighth, picked, own, close, close_twin, *refs):
     pieces, twins = refs[:count], refs[count : 2 * count]
     before, buffer, near = refs[2 * count :]
     seg_id = lax.axis_index("morton")
     core = seg_id % 2
-    place_part(near, core, close[0])
-    place_part(near, 1 - core, close_twin[0])
+    place_part(near, core, close[0], quarter)
+    place_part(near, 1 - core, close_twin[0], quarter)
     total = None
     for i in range(per):
         term = jnp.dot(picked[i], own[i], preferred_element_type=jnp.float32)
         total = term if total is None else total + term
     before[...] = accumulate(total, picked, 1, near, per, width)
-    place_pieces(buffer, seg_id, 0, pieces, twins)
-
-
-def far_kernel(per, width, first, picked, before, c2e, piece, twin, filled, out, buffer):
-    place_pieces(buffer, lax.axis_index("morton"), first, [piece], [twin])
+    place_pieces(buffer, seg_id, 0, pieces, twins, eighth)
+
+
+def far_kernel(per, width, first, eighth, picked, before, c2e, piece, twin, filled, out, buffer):
+    place_pieces(buffer, lax.axis_index("morton"), first, [piece], [twin], eighth)
     total = before[...]
     for k in range(buffer.shape[0]):
         total = accumulate(total, picked, k + 2, buffer.at[k], per, width)
@@ -190,13 +230,17 @@
     small, mid, block_near = call(
         prep_kernel,
         (
-            jax.ShapeDtypeStruct((1, eighth, width), operators.dtype),
-            jax.ShapeDtypeStruct((1, quarter, width), operators.dtype),
+            jax.ShapeDtypeStruct((1, packed_rows(width, eighth), 128), operators.dtype),
+            jax.ShapeDtypeStruct((1, packed_rows(width, quarter), 128), operators.dtype),
             jax.ShapeDtypeStruct(block.shape, block.dtype),
         ),
         (pltpu.with_memory_space_constraint(flat, pltpu.HBM), pltpu.with_memory_space_constraint(block, pltpu.HBM)),
         specs=[hbm, hbm],
-        scratch=[pltpu.SemaphoreType.DMA((3,))],
+        scratch=[
+            pltpu.VMEM((eighth, width), operators.dtype),
+            pltpu.VMEM((quarter, width), operators.dtype),
+            pltpu.SemaphoreType.DMA((3,)),
+        ],
     )
     twin = lax.ppermute(block, "morton", pairs_xor(segs, 1))
     other = lax.ppermute(block, "morton", pairs_odd(segs))
@@ -236,14 +280,14 @@
     buffer = jax.ShapeDtypeStruct((lanes - 2, eighth * segs, width), jnp.bfloat16)
     early = len(pieces) - 1
     before, buffer_mid = call(
-        functools.partial(mid_kernel, per, width, early),
+        functools.partial(mid_kernel, per, width, early, quarter, eighth),
         (sums, buffer),
         (picked, operators, close, close_twin, *pieces[:early], *twins[:early]),
         scratch=[pltpu.VMEM((2 * quarter, width), jnp.bfloat16)],
         flops=4 * boxes * rows * width,
     )
     density, _ = call(
-        functools.partial(far_kernel, per, width, early),
+        functools.partial(far_kernel, per, width, early, eighth),
         (jax.ShapeDtypeStruct((width, boxes), jnp.float32), buffer),
         (picked, before, c2e_near, pieces[early], twins[early], buffer_mid),
         alias={5: 1},

time: 32.5 us -> 30.2 us (0.929)
  waiting for transfers between devices: 13.7 us -> 11.9 us
  starting transfers between devices: 13.2 us -> 12.6 us
    ppermute x1, waiting for transfers between devices: 3.05 us -> 0.28 us  [per_device(): close = lax.ppermute(mid, 'lane', pairs_xor(lanes, 1))]
    ppermute x3, waiting for transfers between devices: 4.62 us -> 5.82 us  [per_device(): lax.ppermute(piece, 'morton', pairs_xor(segs, 2 * step))]
    ppermute x1, starting transfers between devices: 0.57 us -> 0.01 us  [per_device(): twin = lax.ppermute(block, 'morton', pairs_xor(segs, 1))]
    ppermute x1, starting transfers between devices: 0.23 us -> 0.78 us  [per_device(): close = lax.ppermute(mid, 'lane', pairs_xor(lanes, 1))]
    ppermute x1, starting transfers between devices: 2.37 us -> 1.86 us  [per_device(): near = lax.ppermute(column, 'lane', pairs_xor(lanes, 1))]
    ppermute x1, waiting for transfers between devices: 0.4 us -> 0.01 us  [per_device(): near = lax.ppermute(column, 'lane', pairs_xor(lanes, 1))]
    ppermute x2, starting transfers between devices: 4 us -> 3.67 us  [per_device(): lax.ppermute(small, 'lane', pairs_xor(lanes, k))]
  transfers between devices with their start and end apart: 15 -> 15, of which waited for: 6 -> 5; matrix products, arithmetic and copies ran while one was open for 0% -> 0% of each run, Pallas kernels for 11% -> 12%
where the time goes in v5:
time: 30.2 us; the launch traced here: 30.1 us
  starting transfers between devices  12.6 us (42%)
  waiting for transfers between devices  11.9 us (39%)
  Pallas kernels  5.36 us (18%)
    ppermute x3, waiting for transfers between devices, per_device(): lax.ppermute(piece, 'morton', pairs_xor(segs, 2 * step))  5.82 us
    ppermute x2, waiting for transfers between devices, per_device(): lax.ppermute(small, 'lane', pairs_xor(lanes, k))  5.75 us
    pallas_call x5, Pallas kernels, call(): pl.pallas_call(kernel, out_shape=out, in_specs=specs or [vmem] * len(args...  5.36 us
    ppermute x2, starting transfers between devices, per_device(): lax.ppermute(small, 'lane', pairs_xor(lanes, k))  3.67 us
    ppermute x1, starting transfers between devices, per_device(): other = lax.ppermute(block, 'morton', pairs_odd(segs))  3.44 us
    ppermute x3, starting transfers between devices, per_device(): lax.ppermute(piece, 'morton', pairs_xor(segs, 2 * step))  2.21 us
    ppermute x1, starting transfers between devices, per_device(): near = lax.ppermute(column, 'lane', pairs_xor(lanes, 1))  1.86 us
    ppermute x1, starting transfers between devices, per_device(): close = lax.ppermute(mid, 'lane', pairs_xor(lanes, 1))  0.78 us
  transfers between devices with their start and end apart: 15, of which 5 were waited for; matrix products, arithmetic and copies ran while one was open for 0% of the time, Pallas kernels for 12%

profile of v5, /device:TPU:0, one launch (start us, length us, event | category | flops | bytes accessed | tf_op | source)
XLA Modules:
  0.0 30.1 jit_solution(17165433096810271539)
XLA Ops:
  0.0 0.0 copy-start.1
  0.0 0.0 copy-start.3
  0.0 0.0 copy-start.2
  0.0 0.0 copy-start.4
  0.0 3.4 %collective-permute-start.1 = (bf16[296,128]{1,0:T(8,128)(2,1)}, bf16[296,128]{1,0:T(8,128)(2,1)S(1)}, u32[]{:S(2)}, u32[]{:S(2)}) collective-permute-start(bf16[296,128]{1,0:T(8,128)(2,1)} %bitcast.12), channel_id=1, source_target_pairs={{0,28},{28,0},{4,8},{8,4},{12,16},{16,12},{20,24},{24,20},{1,29},{... | collective-permute-start | bytes 227336 | tf_op jit(solution)/shard_map/ppermute | solution.py:246
  3.4 0.0 collective-permute-start
  3.5 1.2 %shard_map.64 = (bf16[1,272,128]{2,1,0:T(8,128)(2,1)S(1)}, bf16[1,1056,128]{2,1,0:T(8,128)(2,1)S(1)}, bf16[296,128]{1,0:T(8,128)(2,1)S(1)}) custom-call(bf16[888,296]{1,0:T(8,128)(2,1)} %bitcast.9, bf16[296,128]{1,0:T(8,128)(2,1)} %bitcast.14), custom_call_target="tpu_custom_call" | custom-call | bytes 1048576 | tf_op jit(solution)/shard_map/pallas_call | solution.py:219
  4.7 3.7 %collective-permute-start.7 = (bf16[1,272,128]{2,1,0:T(8,128)(2,1)S(1)}, bf16[1,272,128]{2,1,0:T(8,128)(2,1)S(1)}, u32[]{:S(2)}, u32[]{:S(2)}) collective-permute-start(bf16[1,272,128]{2,1,0:T(8,128)(2,1)S(1)} %get-tuple-element.18), channel_id=1, source_target_pairs={{0,3},{1,2},{2,1},{3,0},{4,7},{5,6},{6,5},{7,4},{8,11},{9,10},{10,... | collective-permute-start | bytes 208904 | tf_op jit(solution)/shard_map/ppermute | solution.py:250
  8.3 0.0 collective-permute-start.6
  8.3 0.8 %collective-permute-start.4 = (bf16[1,1056,128]{2,1,0:T(8,128)(2,1)S(1)}, bf16[1,1056,128]{2,1,0:T(8,128)(2,1)S(1)}, u32[]{:S(2)}, u32[]{:S(2)}) collective-permute-start(bf16[1,1056,128]{2,1,0:T(8,128)(2,1)S(1)} %get-tuple-element.17), channel_id=1, source_target_pairs={{0,1},{1,0},{2,3},{3,2},{4,5},{5,4},{6,7},{7,6},{8,9},{9,8},{10,11... | collective-permute-start | bytes 811016 | tf_op jit(solution)/shard_map/ppermute | solution.py:251
  9.1 5.8 %collective-permute-done.6 = bf16[1,272,128]{2,1,0:T(8,128)(2,1)S(1)} collective-permute-done((bf16[1,272,128]{2,1,0:T(8,128)(2,1)S(1)}, bf16[1,272,128]{2,1,0:T(8,128)(2,1)S(1)}, u32[]{:S(2)}, u32[]{:S(2)}) %collective-permute-start.6) | collective-permute-done | bytes 69664 | tf_op jit(solution)/shard_map/ppermute | solution.py:250
  14.9 0.0 collective-permute-done.7
  14.9 0.9 %collective-permute-start.8 = (bf16[2,272,128]{2,1,0:T(8,128)(2,1)S(1)}, bf16[2,272,128]{2,1,0:T(8,128)(2,1)S(1)}, u32[]{:S(2)}, u32[]{:S(2)}) collective-permute-start(bf16[2,272,128]{2,1,0:T(8,128)(2,1)S(1)} %constant_dynamic-update-slice_fusion.3.refs_0_), channel_id=1, source_target_pairs={{0,8},{4,12},{8,0},{12,4},{16,24},{20,28},{24,16},{28,20},{1,9},{5... | collective-permute-start | bytes 417800 | tf_op jit(solution)/shard_map/ppermute | solution.py:257
  15.8 0.0 collective-permute-done
  15.8 0.0 collective-permute-done.1
  15.8 0.1 collective-permute-start.3
  15.9 1.9 %collective-permute-start.2 = (bf16[888,128]{1,0:T(8,128)(2,1)S(1)}, bf16[888,128]{1,0:T(8,128)(2,1)S(1)}, u32[]{:S(2)}, u32[]{:S(2)}) collective-permute-start(bf16[888,128]{1,0:T(8,128)(2,1)S(1)} %constant_dynamic-update-slice_fusion.column), channel_id=1, source_target_pairs={{0,1},{1,0},{2,3},{3,2},{4,5},{5,4},{6,7},{7,6},{8,9},{9,8},{10,11... | collective-permute-start | bytes 681992 | tf_op jit(solution)/shard_map/ppermute | solution.py:248
  17.8 0.5 %collective-permute-start.9 = (bf16[2,272,128]{2,1,0:T(8,128)(2,1)S(1)}, bf16[2,272,128]{2,1,0:T(8,128)(2,1)S(1)}, u32[]{:S(2)}, u32[]{:S(2)}) collective-permute-start(bf16[2,272,128]{2,1,0:T(8,128)(2,1)S(1)} %constant_dynamic-update-slice_fusion.3.refs_0_), channel_id=1, source_target_pairs={{0,16},{4,20},{8,24},{12,28},{16,0},{20,4},{24,8},{28,12},{1,17},{... | collective-permute-start | bytes 417800 | tf_op jit(solution)/shard_map/ppermute | solution.py:257
  18.3 0.3 collective-permute-done.4.close
  18.6 0.0 collective-permute-start.5
  18.6 1.5 %collective-permute-done.8.refs_1_ = bf16[2,272,128]{2,1,0:T(8,128)(2,1)S(1)} collective-permute-done((bf16[2,272,128]{2,1,0:T(8,128)(2,1)S(1)}, bf16[2,272,128]{2,1,0:T(8,128)(2,1)S(1)}, u32[]{:S(2)}, u32[]{:S(2)}) %collective-permute-start.8) | collective-permute-done | bytes 139296 | tf_op jit(solution)/shard_map/ppermute | solution.py:257
  20.1 0.8 %collective-permute-start.13 = (bf16[2,272,128]{2,1,0:T(8,128)(2,1)S(1)}, bf16[2,272,128]{2,1,0:T(8,128)(2,1)S(1)}, u32[]{:S(2)}, u32[]{:S(2)}) collective-permute-start(bf16[2,272,128]{2,1,0:T(8,128)(2,1)S(1)} %collective-permute-done.8.refs_1_), channel_id=1, source_target_pairs={{0,16},{4,20},{8,24},{12,28},{16,0},{20,4},{24,8},{28,12},{1,17},{... | collective-permute-start | bytes 417800 | tf_op jit(solution)/shard_map/ppermute | solution.py:257
  20.9 3.1 %collective-permute-done.9.refs_2_ = bf16[2,272,128]{2,1,0:T(8,128)(2,1)S(1)} collective-permute-done((bf16[2,272,128]{2,1,0:T(8,128)(2,1)S(1)}, bf16[2,272,128]{2,1,0:T(8,128)(2,1)S(1)}, u32[]{:S(2)}, u32[]{:S(2)}) %collective-permute-start.9) | collective-permute-done | bytes 139296 | tf_op jit(solution)/shard_map/ppermute | solution.py:257
  24.0 0.0 collective-permute-start.10
  24.0 0.0 collective-permute-done.3.far
  24.0 0.5 %collective-permute-start.12 = (bf16[2,272,128]{2,1,0:T(8,128)(2,1)S(1)}, bf16[2,272,128]{2,1,0:T(8,128)(2,1)S(1)}, u32[]{:S(2)}, u32[]{:S(2)}) collective-permute-start(bf16[2,272,128]{2,1,0:T(8,128)(2,1)S(1)} %collective-permute-done.9.refs_2_), channel_id=1, source_target_pairs={{0,4},{4,0},{8,12},{12,8},{16,20},{20,16},{24,28},{28,24},{1,5},{5... | collective-permute-start | bytes 417800 | tf_op jit(solution)/shard_map/ppermute | solution.py:259
  24.5 0.0 collective-permute-done.2.near
  24.5 0.1 collective-permute-start.11
  24.6 1.2 %collective-permute-done.13.piece = bf16[2,272,128]{2,1,0:T(8,128)(2,1)S(1)} collective-permute-done((bf16[2,272,128]{2,1,0:T(8,128)(2,1)S(1)}, bf16[2,272,128]{2,1,0:T(8,128)(2,1)S(1)}, u32[]{:S(2)}, u32[]{:S(2)}) %collective-permute-start.13) | collective-permute-done | bytes 139296 | tf_op jit(solution)/shard_map/ppermute | solution.py:257
  25.8 0.0 collective-permute-start.14
  25.8 0.0 copy-done.1
  25.8 0.0 copy-done.3
  25.8 0.0 copy-done.2
  25.8 0.0 copy-done.4
  25.8 0.8 %shard_map.65 = (bf16[12,296,128]{2,1,0:T(8,128)(2,1)S(1)}, s32[12,128]{1,0:T(8,128)S(1)}, bf16[296,296]{1,0:T(8,128)(2,1)S(1)}) custom-call(s32[1,128]{1,0:T(1,128)S(1)} %copy-done.4, s32[12,1,128]{2,1,0:T(1,128)S(1)} %bitcast.10, s32[12,1,128]{2,1,0:T(1,128)S(1)} %bitcast.11, bf16[888,128]{1,0:T(8,128)(2,1)S(1)} %constant_dynamic-update-slice_fusion.column, ...), custom_call_target="tpu_custom_call" | custom-call | flops 349175808 | bytes 1048576 | tf_op jit(solution)/shard_map/pallas_call | solution.py:219
  26.7 0.0 copy-start
  26.7 1.1 %shard_map.66.picked = bf16[12,128,296]{2,1,0:T(8,128)(2,1)S(1)} custom-call(s32[12,128]{1,0:T(8,128)S(1)} %get-tuple-element.15.index, bf16[12,296,128]{2,1,0:T(8,128)(2,1)S(1)} %get-tuple-element.16.part, bf16[888,128]{1,0:T(8,128)(2,1)S(1)} %collective-permute-done.2.near, bf16[888,128]{1,0:T(8,128)(2,1)S(1)} %collective-permute-done.3.far), custom_call_target="tpu_custom_call" | custom-call | flops 698351616 | bytes 1048576 | tf_op jit(solution)/shard_map/pallas_call | solution.py:219
  27.7 0.0 collective-permute-done.10.refs_3_
  27.8 0.0 collective-permute-done.12.refs_5_
  27.8 0.0 collective-permute-done.11.refs_4_
  27.8 0.0 collective-permute-done.5.close_twin
  27.8 0.0 copy-done
  27.8 0.7 %shard_map.67 = (f32[128,296]{1,0:T(8,128)S(1)}, bf16[2,896,296]{2,1,0:T(8,128)(2,1)S(1)}) custom-call(bf16[12,128,296]{2,1,0:T(8,128)(2,1)S(1)} %shard_map.66.picked, bf16[3,296,296]{2,1,0:T(8,128)(2,1)S(1)} %copy-done, bf16[1,1056,128]{2,1,0:T(8,128)(2,1)S(1)} %collective-permute-done.4.close, bf16[1,1056,128]{2,1,0:T(8,128)(2,1)S(1)} %collective-permute-done.5.close_twin, ...), custom_call_target="tpu_custom_call" | custom-call | flops 134578176 | bytes 1048576 | tf_op jit(solution)/shard_map/pallas_call | solution.py:219
  28.5 0.0 collective-permute-done.14.twin
  28.5 1.6 %shard_map.68 = (f32[296,128]{1,0:T(8,128)}, bf16[2,896,296]{2,1,0:T(8,128)(2,1)S(1)}) custom-call(bf16[12,128,296]{2,1,0:T(8,128)(2,1)S(1)} %shard_map.66.picked, f32[128,296]{1,0:T(8,128)S(1)} %get-tuple-element.19.before, bf16[296,296]{1,0:T(8,128)(2,1)S(1)} %get-tuple-element.20.c2e, ...), custom_call_target="tpu_custom_call", output_to_operand_aliasing={{1}: (5, {})} | custom-call | flops 269156352 | bytes 1048576 | tf_op jit(solution)/shard_map/pallas_call | solution.py:219
  (5 shorter events, 0.1 us)
Async XLA Ops:
  0.0 25.8 %copy-start.1 = (bf16[296,296]{1,0:T(8,128)(2,1)S(1)}, bf16[296,296]{1,0:T(8,128)(2,1)}, u32[]{:S(2)}) copy-start(bf16[296,296]{1,0:T(8,128)(2,1)} %c2e.1) | copy-start | bytes 525700
  0.0 25.8 %copy-start.3 = (s32[1,128,12]{1,0,2:T(1,128)S(1)}, s32[1,128,12]{1,0,2:T(1,128)}, u32[]{:S(2)}) copy-start(s32[1,128,12]{1,0,2:T(1,128)} %param.9) | copy-start | bytes 18436
  0.0 25.8 %copy-start.2 = (s32[1,128,12]{1,0,2:T(1,128)S(1)}, s32[1,128,12]{1,0,2:T(1,128)}, u32[]{:S(2)}) copy-start(s32[1,128,12]{1,0,2:T(1,128)} %param.8) | copy-start | bytes 18436
  0.0 25.8 %copy-start.4 = (s32[1,128]{1,0:T(1,128)S(1)}, s32[1,128]{1,0:T(1,128)}, u32[]{:S(2)}) copy-start(s32[1,128]{1,0:T(1,128)} %counts.1) | copy-start | bytes 1540
  0.0 15.8 %collective-permute-start.1 = (bf16[296,128]{1,0:T(8,128)(2,1)}, bf16[296,128]{1,0:T(8,128)(2,1)S(1)}, u32[]{:S(2)}, u32[]{:S(2)}) collective-permute-start(bf16[296,128]{1,0:T(8,128)(2,1)} %bitcast.12), channel_id=1, source_target_pairs={{0,28},{28,0},{4,8},{8,4},{12,16},{16,12},{20,24},{24,20},{1,29},{... | collective-permute-start | bytes 227336 | tf_op jit(solution)/shard_map/ppermute | solution.py:246
  3.4 12.3 %collective-permute-start = (bf16[296,128]{1,0:T(8,128)(2,1)}, bf16[296,128]{1,0:T(8,128)(2,1)S(1)}, u32[]{:S(2)}, u32[]{:S(2)}) collective-permute-start(bf16[296,128]{1,0:T(8,128)(2,1)} %bitcast.13), channel_id=1, source_target_pairs={{0,4},{4,0},{8,12},{12,8},{16,20},{20,16},{24,28},{28,24},{1,5},{5... | collective-permute-start | bytes 227336 | tf_op jit(solution)/shard_map/ppermute | solution.py:245
  4.7 10.2 %collective-permute-start.7 = (bf16[1,272,128]{2,1,0:T(8,128)(2,1)S(1)}, bf16[1,272,128]{2,1,0:T(8,128)(2,1)S(1)}, u32[]{:S(2)}, u32[]{:S(2)}) collective-permute-start(bf16[1,272,128]{2,1,0:T(8,128)(2,1)S(1)} %get-tuple-element.18), channel_id=1, source_target_pairs={{0,3},{1,2},{2,1},{3,0},{4,7},{5,6},{6,5},{7,4},{8,11},{9,10},{10,... | collective-permute-start | bytes 208904 | tf_op jit(solution)/shard_map/ppermute | solution.py:250
  8.3 6.5 %collective-permute-start.6 = (bf16[1,272,128]{2,1,0:T(8,128)(2,1)S(1)}, bf16[1,272,128]{2,1,0:T(8,128)(2,1)S(1)}, u32[]{:S(2)}, u32[]{:S(2)}) collective-permute-start(bf16[1,272,128]{2,1,0:T(8,128)(2,1)S(1)} %get-tuple-element.18), channel_id=1, source_target_pairs={{0,2},{1,3},{2,0},{3,1},{4,6},{5,7},{6,4},{7,5},{8,10},{9,11},{10,... | collective-permute-start | bytes 208904 | tf_op jit(solution)/shard_map/ppermute | solution.py:250
  8.3 10.2 %collective-permute-start.4 = (bf16[1,1056,128]{2,1,0:T(8,128)(2,1)S(1)}, bf16[1,1056,128]{2,1,0:T(8,128)(2,1)S(1)}, u32[]{:S(2)}, u32[]{:S(2)}) collective-permute-start(bf16[1,1056,128]{2,1,0:T(8,128)(2,1)S(1)} %get-tuple-element.17), channel_id=1, source_target_pairs={{0,1},{1,0},{2,3},{3,2},{4,5},{5,4},{6,7},{7,6},{8,9},{9,8},{10,11... | collective-permute-start | bytes 811016 | tf_op jit(solution)/shard_map/ppermute | solution.py:251
  14.9 5.2 %collective-permute-start.8 = (bf16[2,272,128]{2,1,0:T(8,128)(2,1)S(1)}, bf16[2,272,128]{2,1,0:T(8,128)(2,1)S(1)}, u32[]{:S(2)}, u32[]{:S(2)}) collective-permute-start(bf16[2,272,128]{2,1,0:T(8,128)(2,1)S(1)} %constant_dynamic-update-slice_fusion.3.refs_0_), channel_id=1, source_target_pairs={{0,8},{4,12},{8,0},{12,4},{16,24},{20,28},{24,16},{28,20},{1,9},{5... | collective-permute-start | bytes 417800 | tf_op jit(solution)/shard_map/ppermute | solution.py:257
  15.8 8.1 %collective-permute-start.3 = (bf16[888,128]{1,0:T(8,128)(2,1)S(1)}, bf16[888,128]{1,0:T(8,128)(2,1)S(1)}, u32[]{:S(2)}, u32[]{:S(2)}) collective-permute-start(bf16[888,128]{1,0:T(8,128)(2,1)S(1)} %constant_dynamic-update-slice_fusion.column), channel_id=1, source_target_pairs={{0,4},{3,7},{4,0},{7,3},{8,12},{11,15},{12,8},{15,11},{16,20},{19,... | collective-permute-start | bytes 681992 | tf_op jit(solution)/shard_map/ppermute | solution.py:249
  15.9 8.6 %collective-permute-start.2 = (bf16[888,128]{1,0:T(8,128)(2,1)S(1)}, bf16[888,128]{1,0:T(8,128)(2,1)S(1)}, u32[]{:S(2)}, u32[]{:S(2)}) collective-permute-start(bf16[888,128]{1,0:T(8,128)(2,1)S(1)} %constant_dynamic-update-slice_fusion.column), channel_id=1, source_target_pairs={{0,1},{1,0},{2,3},{3,2},{4,5},{5,4},{6,7},{7,6},{8,9},{9,8},{10,11... | collective-permute-start | bytes 681992 | tf_op jit(solution)/shard_map/ppermute | solution.py:248
  17.8 6.2 %collective-permute-start.9 = (bf16[2,272,128]{2,1,0:T(8,128)(2,1)S(1)}, bf16[2,272,128]{2,1,0:T(8,128)(2,1)S(1)}, u32[]{:S(2)}, u32[]{:S(2)}) collective-permute-start(bf16[2,272,128]{2,1,0:T(8,128)(2,1)S(1)} %constant_dynamic-update-slice_fusion.3.refs_0_), channel_id=1, source_target_pairs={{0,16},{4,20},{8,24},{12,28},{16,0},{20,4},{24,8},{28,12},{1,17},{... | collective-permute-start | bytes 417800 | tf_op jit(solution)/shard_map/ppermute | solution.py:257
  18.6 9.2 %collective-permute-start.5 = (bf16[1,1056,128]{2,1,0:T(8,128)(2,1)S(1)}, bf16[1,1056,128]{2,1,0:T(8,128)(2,1)S(1)}, u32[]{:S(2)}, u32[]{:S(2)}) collective-permute-start(bf16[1,1056,128]{2,1,0:T(8,128)(2,1)S(1)} %collective-permute-done.4.close), channel_id=1, source_target_pairs={{0,4},{4,0},{8,12},{12,8},{16,20},{20,16},{24,28},{28,24},{1,5},{5... | collective-permute-start | bytes 811016 | tf_op jit(solution)/shard_map/ppermute | solution.py:258
  20.1 5.7 %collective-permute-start.13 = (bf16[2,272,128]{2,1,0:T(8,128)(2,1)S(1)}, bf16[2,272,128]{2,1,0:T(8,128)(2,1)S(1)}, u32[]{:S(2)}, u32[]{:S(2)}) collective-permute-start(bf16[2,272,128]{2,1,0:T(8,128)(2,1)S(1)} %collective-permute-done.8.refs_1_), channel_id=1, source_target_pairs={{0,16},{4,20},{8,24},{12,28},{16,0},{20,4},{24,8},{28,12},{1,17},{... | collective-permute-start | bytes 417800 | tf_op jit(solution)/shard_map/ppermute | solution.py:257
  24.0 3.8 %collective-permute-start.10 = (bf16[2,272,128]{2,1,0:T(8,128)(2,1)S(1)}, bf16[2,272,128]{2,1,0:T(8,128)(2,1)S(1)}, u32[]{:S(2)}, u32[]{:S(2)}) collective-permute-start(bf16[2,272,128]{2,1,0:T(8,128)(2,1)S(1)} %constant_dynamic-update-slice_fusion.3.refs_0_), channel_id=1, source_target_pairs={{0,4},{4,0},{8,12},{12,8},{16,20},{20,16},{24,28},{28,24},{1,5},{5... | collective-permute-start | bytes 417800 | tf_op jit(solution)/shard_map/ppermute | solution.py:259
  24.0 3.8 %collective-permute-start.12 = (bf16[2,272,128]{2,1,0:T(8,128)(2,1)S(1)}, bf16[2,272,128]{2,1,0:T(8,128)(2,1)S(1)}, u32[]{:S(2)}, u32[]{:S(2)}) collective-permute-start(bf16[2,272,128]{2,1,0:T(8,128)(2,1)S(1)} %collective-permute-done.9.refs_2_), channel_id=1, source_target_pairs={{0,4},{4,0},{8,12},{12,8},{16,20},{20,16},{24,28},{28,24},{1,5},{5... | collective-permute-start | bytes 417800 | tf_op jit(solution)/shard_map/ppermute | solution.py:259
  24.5 3.3 %collective-permute-start.11 = (bf16[2,272,128]{2,1,0:T(8,128)(2,1)S(1)}, bf16[2,272,128]{2,1,0:T(8,128)(2,1)S(1)}, u32[]{:S(2)}, u32[]{:S(2)}) collective-permute-start(bf16[2,272,128]{2,1,0:T(8,128)(2,1)S(1)} %collective-permute-done.8.refs_1_), channel_id=1, source_target_pairs={{0,4},{4,0},{8,12},{12,8},{16,20},{20,16},{24,28},{28,24},{1,5},{5... | collective-permute-start | bytes 417800 | tf_op jit(solution)/shard_map/ppermute | solution.py:259
  25.8 2.7 %collective-permute-start.14 = (bf16[2,272,128]{2,1,0:T(8,128)(2,1)S(1)}, bf16[2,272,128]{2,1,0:T(8,128)(2,1)S(1)}, u32[]{:S(2)}, u32[]{:S(2)}) collective-permute-start(bf16[2,272,128]{2,1,0:T(8,128)(2,1)S(1)} %collective-permute-done.13.piece), channel_id=1, source_target_pairs={{0,4},{4,0},{8,12},{12,8},{16,20},{20,16},{24,28},{28,24},{1,5},{5... | collective-permute-start | bytes 417800 | tf_op jit(solution)/shard_map/ppermute | solution.py:259
  26.7 1.1 %copy-start = (bf16[3,296,296]{2,1,0:T(8,128)(2,1)S(1)}, bf16[3,296,296]{2,1,0:T(8,128)(2,1)}, u32[]{:S(2)}) copy-start(bf16[3,296,296]{2,1,0:T(8,128)(2,1)} %own.1) | copy-start | bytes 1577092

commit v6 on v5

--- a/solution.py
+++ b/solution.py
@@ -154,51 +154,50 @@
     c2e_out[...] = c2e[...]
 
 
-def second_kernel(boxes, index, part, near, far, out):
-    table = side_tables((near, far), out.shape[2])
+def second_kernel(boxes, per, index, part, near, far, out, stacked):
+    width = part.shape[1]
+    table = side_tables((near, far), width)
     values = index[...]
     total = values.shape[0]
     for at in range(0, total, 2):
         count = min(2, total - at)
         found = pick_rows(values, table, 3 * boxes, at, count, boxes)
         for i in range(count):
-            out[at + i] = (part[at + i] + found[:, i * boxes : (i + 1) * boxes]).T
-
-
-def accumulate(total, picked, group, buffer, per, width):
-    for i in range(per):
-        term = jnp.dot(picked[group * per + i], buffer[pl.ds(i * width, width), :], preferred_element_type=jnp.float32)
-        total = total + term
-    return total
-
-
-def place_pieces(buffer, seg_id, first, pieces, twins, size):
+            spot = slice((at + i) * width, (at + i + 1) * width)
+            stacked[spot, :] = part[at + i] + found[:, i * boxes : (i + 1) * boxes]
+    for g in range(total // per):
+        out[g] = stacked[g * per * width : (g + 1) * per * width, :].T
+
+
+def accumulate(total, picked, group, buffer):
+    rows = picked.shape[2]
+    return total + jnp.dot(picked[group], buffer[pl.ds(0, rows), :], preferred_element_type=jnp.float32)
+
+
+def place_pieces(buffer, seg_id, first, pieces, size):
     for k in range(pieces[0].shape[0]):
-        for j, (piece, twin) in enumerate(zip(pieces, twins)):
+        for j, piece in enumerate(pieces):
             place_part(buffer.at[k], seg_id ^ (2 * (first + j)), piece[k], size)
-            place_part(buffer.at[k], seg_id ^ (2 * (first + j) + 1), twin[k], size)
-
-
-def mid_kernel(per, width, count, quarter, eighth, picked, own, close, close_twin, *refs):
-    pieces, twins = refs[:count], refs[count : 2 * count]
-    before, buffer, near = refs[2 * count :]
+
+
+def mid_kernel(count, quarter, eighth, picked, own, close, close_twin, *refs):
+    pieces, twins = refs[:count], refs[count : 2 * count - 1]
+    before, buffer, near = refs[2 * count - 1 :]
     seg_id = lax.axis_index("morton")
     core = seg_id % 2
     place_part(near, core, close[0], quarter)
     place_part(near, 1 - core, close_twin[0], quarter)
-    total = None
-    for i in range(per):
-        term = jnp.dot(picked[i], own[i], preferred_element_type=jnp.float32)
-        total = term if total is None else total + term
-    before[...] = accumulate(total, picked, 1, near, per, width)
-    place_pieces(buffer, seg_id, 0, pieces, twins, eighth)
-
-
-def far_kernel(per, width, first, eighth, picked, before, c2e, piece, twin, filled, out, buffer):
-    place_pieces(buffer, lax.axis_index("morton"), first, [piece], [twin], eighth)
+    total = jnp.dot(picked[0], own[...], preferred_element_type=jnp.float32)
+    before[...] = accumulate(total, picked, 1, near)
+    place_pieces(buffer, seg_id, 0, pieces, eighth)
+    place_pieces(buffer, seg_id ^ 1, 0, twins, eighth)
+
+
+def far_kernel(first, eighth, picked, before, c2e, twin, filled, out, buffer):
+    place_pieces(buffer, lax.axis_index("morton") ^ 1, first, [twin], eighth)
     total = before[...]
     for k in range(buffer.shape[0]):
-        total = accumulate(total, picked, k + 2, buffer.at[k], per, width)
+        total = accumulate(total, picked, k + 2, buffer.at[k])
     check = total.astype(jnp.bfloat16)
     out[...] = jnp.dot(check, c2e[...], preferred_element_type=jnp.float32).T
 
@@ -271,26 +270,26 @@
         flops=2 * total * boxes * boxes * 3 * width,
     )
     picked = call(
-        functools.partial(second_kernel, boxes),
-        jax.ShapeDtypeStruct((total, boxes, width), jnp.bfloat16),
+        functools.partial(second_kernel, boxes, per),
+        jax.ShapeDtypeStruct((lanes, boxes, rows), jnp.bfloat16),
         (index, part, near, far),
-        specs=[vmem] * 4,
+        scratch=[pltpu.VMEM((total * width, boxes), jnp.bfloat16)],
         flops=2 * total * boxes * boxes * 6 * width,
     )
     buffer = jax.ShapeDtypeStruct((lanes - 2, eighth * segs, width), jnp.bfloat16)
     early = len(pieces) - 1
     before, buffer_mid = call(
-        functools.partial(mid_kernel, per, width, early, quarter, eighth),
+        functools.partial(mid_kernel, len(pieces), quarter, eighth),
         (sums, buffer),
-        (picked, operators, close, close_twin, *pieces[:early], *twins[:early]),
+        (picked, flat, close, close_twin, *pieces, *twins[:early]),
         scratch=[pltpu.VMEM((2 * quarter, width), jnp.bfloat16)],
         flops=4 * boxes * rows * width,
     )
     density, _ = call(
-        functools.partial(far_kernel, per, width, early, eighth),
+        functools.partial(far_kernel, early, eighth),
         (jax.ShapeDtypeStruct((width, boxes), jnp.float32), buffer),
-        (picked, before, c2e_near, pieces[early], twins[early], buffer_mid),
-        alias={5: 1},
+        (picked, before, c2e_near, twins[early], buffer_mid),
+        alias={4: 1},
         flops=2 * lanes * boxes * rows * width,
     )
     return density.T.reshape(1, boxes, width)

time: 30.2 us -> 30.2 us (level)
  transfers between devices with their start and end apart: 15 -> 15, of which waited for: 5 -> 5; matrix products, arithmetic and copies ran while one was open for 0% -> 0% of each run, Pallas kernels for 12% -> 13%
where the time goes in v6:
time: 30.2 us; the launch traced here: 30 us
  starting transfers between devices  12.6 us (42%)
  waiting for transfers between devices  11.9 us (39%)
  Pallas kernels  5.29 us (18%)
    ppermute x3, waiting for transfers between devices, per_device(): lax.ppermute(piece, 'morton', pairs_xor(segs, 2 * step))  5.82 us
    ppermute x2, waiting for transfers between devices, per_device(): lax.ppermute(small, 'lane', pairs_xor(lanes, k))  5.75 us
    pallas_call x5, Pallas kernels, call(): pl.pallas_call(kernel, out_shape=out, in_specs=specs or [vmem] * len(args...  5.29 us
    ppermute x2, starting transfers between devices, per_device(): lax.ppermute(small, 'lane', pairs_xor(lanes, k))  3.67 us
    ppermute x1, starting transfers between devices, per_device(): other = lax.ppermute(block, 'morton', pairs_odd(segs))  3.44 us
    ppermute x3, starting transfers between devices, per_device(): lax.ppermute(piece, 'morton', pairs_xor(segs, 2 * step))  2.21 us
    ppermute x1, starting transfers between devices, per_device(): near = lax.ppermute(column, 'lane', pairs_xor(lanes, 1))  1.86 us
    ppermute x1, starting transfers between devices, per_device(): close = lax.ppermute(mid, 'lane', pairs_xor(lanes, 1))  0.78 us
  transfers between devices with their start and end apart: 15, of which 5 were waited for; matrix products, arithmetic and copies ran while one was open for 0% of the time, Pallas kernels for 13%

profile of v6, /device:TPU:0, one launch (start us, length us, event | category | flops | bytes accessed | tf_op | source)
XLA Modules:
  0.0 30.0 jit_solution(3394693039359558413)
XLA Ops:
  0.0 0.0 copy-start.1
  0.0 0.0 copy-start.3
  0.0 0.0 copy-start.2
  0.0 0.0 copy-start.4
  0.0 3.4 %collective-permute-start.1 = (bf16[296,128]{1,0:T(8,128)(2,1)}, bf16[296,128]{1,0:T(8,128)(2,1)S(1)}, u32[]{:S(2)}, u32[]{:S(2)}) collective-permute-start(bf16[296,128]{1,0:T(8,128)(2,1)} %bitcast.13), channel_id=1, source_target_pairs={{0,28},{28,0},{4,8},{8,4},{12,16},{16,12},{20,24},{24,20},{1,29},{... | collective-permute-start | bytes 227336 | tf_op jit(solution)/shard_map/ppermute | solution.py:245
  3.4 0.0 collective-permute-start
  3.5 1.2 %shard_map.64 = (bf16[1,272,128]{2,1,0:T(8,128)(2,1)S(1)}, bf16[1,1056,128]{2,1,0:T(8,128)(2,1)S(1)}, bf16[296,128]{1,0:T(8,128)(2,1)S(1)}) custom-call(bf16[888,296]{1,0:T(8,128)(2,1)} %bitcast.9, bf16[296,128]{1,0:T(8,128)(2,1)} %bitcast.15), custom_call_target="tpu_custom_call" | custom-call | bytes 1048576 | tf_op jit(solution)/shard_map/pallas_call | solution.py:218
  4.7 3.7 %collective-permute-start.7 = (bf16[1,272,128]{2,1,0:T(8,128)(2,1)S(1)}, bf16[1,272,128]{2,1,0:T(8,128)(2,1)S(1)}, u32[]{:S(2)}, u32[]{:S(2)}) collective-permute-start(bf16[1,272,128]{2,1,0:T(8,128)(2,1)S(1)} %get-tuple-element.18), channel_id=1, source_target_pairs={{0,3},{1,2},{2,1},{3,0},{4,7},{5,6},{6,5},{7,4},{8,11},{9,10},{10,... | collective-permute-start | bytes 208904 | tf_op jit(solution)/shard_map/ppermute | solution.py:249
  8.3 0.0 collective-permute-start.6
  8.3 0.8 %collective-permute-start.4 = (bf16[1,1056,128]{2,1,0:T(8,128)(2,1)S(1)}, bf16[1,1056,128]{2,1,0:T(8,128)(2,1)S(1)}, u32[]{:S(2)}, u32[]{:S(2)}) collective-permute-start(bf16[1,1056,128]{2,1,0:T(8,128)(2,1)S(1)} %get-tuple-element.17), channel_id=1, source_target_pairs={{0,1},{1,0},{2,3},{3,2},{4,5},{5,4},{6,7},{7,6},{8,9},{9,8},{10,11... | collective-permute-start | bytes 811016 | tf_op jit(solution)/shard_map/ppermute | solution.py:250
  9.1 5.8 %collective-permute-done.6 = bf16[1,272,128]{2,1,0:T(8,128)(2,1)S(1)} collective-permute-done((bf16[1,272,128]{2,1,0:T(8,128)(2,1)S(1)}, bf16[1,272,128]{2,1,0:T(8,128)(2,1)S(1)}, u32[]{:S(2)}, u32[]{:S(2)}) %collective-permute-start.6) | collective-permute-done | bytes 69664 | tf_op jit(solution)/shard_map/ppermute | solution.py:249
  14.9 0.0 collective-permute-done.7
  14.9 0.9 %collective-permute-start.8 = (bf16[2,272,128]{2,1,0:T(8,128)(2,1)S(1)}, bf16[2,272,128]{2,1,0:T(8,128)(2,1)S(1)}, u32[]{:S(2)}, u32[]{:S(2)}) collective-permute-start(bf16[2,272,128]{2,1,0:T(8,128)(2,1)S(1)} %constant_dynamic-update-slice_fusion.3.refs_0_), channel_id=1, source_target_pairs={{0,8},{4,12},{8,0},{12,4},{16,24},{20,28},{24,16},{28,20},{1,9},{5... | collective-permute-start | bytes 417800 | tf_op jit(solution)/shard_map/ppermute | solution.py:256
  15.8 0.0 collective-permute-done
  15.8 0.0 collective-permute-done.1
  15.8 0.1 collective-permute-start.3
  15.9 1.9 %collective-permute-start.2 = (bf16[888,128]{1,0:T(8,128)(2,1)S(1)}, bf16[888,128]{1,0:T(8,128)(2,1)S(1)}, u32[]{:S(2)}, u32[]{:S(2)}) collective-permute-start(bf16[888,128]{1,0:T(8,128)(2,1)S(1)} %constant_dynamic-update-slice_fusion.column), channel_id=1, source_target_pairs={{0,1},{1,0},{2,3},{3,2},{4,5},{5,4},{6,7},{7,6},{8,9},{9,8},{10,11... | collective-permute-start | bytes 681992 | tf_op jit(solution)/shard_map/ppermute | solution.py:247
  17.8 0.5 %collective-permute-start.9 = (bf16[2,272,128]{2,1,0:T(8,128)(2,1)S(1)}, bf16[2,272,128]{2,1,0:T(8,128)(2,1)S(1)}, u32[]{:S(2)}, u32[]{:S(2)}) collective-permute-start(bf16[2,272,128]{2,1,0:T(8,128)(2,1)S(1)} %constant_dynamic-update-slice_fusion.3.refs_0_), channel_id=1, source_target_pairs={{0,16},{4,20},{8,24},{12,28},{16,0},{20,4},{24,8},{28,12},{1,17},{... | collective-permute-start | bytes 417800 | tf_op jit(solution)/shard_map/ppermute | solution.py:256
  18.3 0.3 collective-permute-done.4.close
  18.6 0.0 collective-permute-start.5
  18.6 1.5 %collective-permute-done.8.refs_1_ = bf16[2,272,128]{2,1,0:T(8,128)(2,1)S(1)} collective-permute-done((bf16[2,272,128]{2,1,0:T(8,128)(2,1)S(1)}, bf16[2,272,128]{2,1,0:T(8,128)(2,1)S(1)}, u32[]{:S(2)}, u32[]{:S(2)}) %collective-permute-start.8) | collective-permute-done | bytes 139296 | tf_op jit(solution)/shard_map/ppermute | solution.py:256
  20.1 0.8 %collective-permute-start.10 = (bf16[2,272,128]{2,1,0:T(8,128)(2,1)S(1)}, bf16[2,272,128]{2,1,0:T(8,128)(2,1)S(1)}, u32[]{:S(2)}, u32[]{:S(2)}) collective-permute-start(bf16[2,272,128]{2,1,0:T(8,128)(2,1)S(1)} %collective-permute-done.8.refs_1_), channel_id=1, source_target_pairs={{0,16},{4,20},{8,24},{12,28},{16,0},{20,4},{24,8},{28,12},{1,17},{... | collective-permute-start | bytes 417800 | tf_op jit(solution)/shard_map/ppermute | solution.py:256
  20.9 3.1 %collective-permute-done.9.refs_2_ = bf16[2,272,128]{2,1,0:T(8,128)(2,1)S(1)} collective-permute-done((bf16[2,272,128]{2,1,0:T(8,128)(2,1)S(1)}, bf16[2,272,128]{2,1,0:T(8,128)(2,1)S(1)}, u32[]{:S(2)}, u32[]{:S(2)}) %collective-permute-start.9) | collective-permute-done | bytes 139296 | tf_op jit(solution)/shard_map/ppermute | solution.py:256
  24.0 0.0 collective-permute-start.11
  24.0 0.0 collective-permute-done.3.far
  24.0 0.5 %collective-permute-start.13 = (bf16[2,272,128]{2,1,0:T(8,128)(2,1)S(1)}, bf16[2,272,128]{2,1,0:T(8,128)(2,1)S(1)}, u32[]{:S(2)}, u32[]{:S(2)}) collective-permute-start(bf16[2,272,128]{2,1,0:T(8,128)(2,1)S(1)} %collective-permute-done.9.refs_2_), channel_id=1, source_target_pairs={{0,4},{4,0},{8,12},{12,8},{16,20},{20,16},{24,28},{28,24},{1,5},{5... | collective-permute-start | bytes 417800 | tf_op jit(solution)/shard_map/ppermute | solution.py:258
  24.5 0.0 collective-permute-done.2.near
  24.5 0.1 collective-permute-start.12
  24.6 1.2 %collective-permute-done.10.refs_3_ = bf16[2,272,128]{2,1,0:T(8,128)(2,1)S(1)} collective-permute-done((bf16[2,272,128]{2,1,0:T(8,128)(2,1)S(1)}, bf16[2,272,128]{2,1,0:T(8,128)(2,1)S(1)}, u32[]{:S(2)}, u32[]{:S(2)}) %collective-permute-start.10) | collective-permute-done | bytes 139296 | tf_op jit(solution)/shard_map/ppermute | solution.py:256
  25.8 0.0 collective-permute-start.14
  25.8 0.0 copy-done.1
  25.8 0.0 copy-done.3
  25.8 0.0 copy-done.2
  25.8 0.0 copy-done.4
  25.8 0.8 %shard_map.65 = (bf16[12,296,128]{2,1,0:T(8,128)(2,1)S(1)}, s32[12,128]{1,0:T(8,128)S(1)}, bf16[296,296]{1,0:T(8,128)(2,1)S(1)}) custom-call(s32[1,128]{1,0:T(1,128)S(1)} %copy-done.4, s32[12,1,128]{2,1,0:T(1,128)S(1)} %bitcast.11, s32[12,1,128]{2,1,0:T(1,128)S(1)} %bitcast.12, bf16[888,128]{1,0:T(8,128)(2,1)S(1)} %constant_dynamic-update-slice_fusion.column, ...), custom_call_target="tpu_custom_call" | custom-call | flops 349175808 | bytes 1048576 | tf_op jit(solution)/shard_map/pallas_call | solution.py:218
  26.7 0.0 copy-start
  26.7 1.1 %shard_map.66.picked = bf16[4,128,888]{2,1,0:T(8,128)(2,1)S(1)} custom-call(s32[12,128]{1,0:T(8,128)S(1)} %get-tuple-element.15.index, bf16[12,296,128]{2,1,0:T(8,128)(2,1)S(1)} %get-tuple-element.16.part, bf16[888,128]{1,0:T(8,128)(2,1)S(1)} %collective-permute-done.2.near, bf16[888,128]{1,0:T(8,128)(2,1)S(1)} %collective-permute-done.3.far), custom_call_target="tpu_custom_call" | custom-call | flops 698351616 | bytes 1048576 | tf_op jit(solution)/shard_map/pallas_call | solution.py:218
  27.8 0.0 collective-permute-done.11.refs_4_
  27.8 0.0 collective-permute-done.13.refs_6_
  27.8 0.0 collective-permute-done.12.refs_5_
  27.8 0.0 collective-permute-done.5.close_twin
  27.8 0.0 copy-done
  27.8 0.7 %shard_map.67 = (f32[128,296]{1,0:T(8,128)S(1)}, bf16[2,896,296]{2,1,0:T(8,128)(2,1)S(1)}) custom-call(bf16[4,128,888]{2,1,0:T(8,128)(2,1)S(1)} %shard_map.66.picked, bf16[888,296]{1,0:T(8,128)(2,1)S(1)} %bitcast.10, bf16[1,1056,128]{2,1,0:T(8,128)(2,1)S(1)} %collective-permute-done.4.close, bf16[1,1056,128]{2,1,0:T(8,128)(2,1)S(1)} %collective-permute-done.5.close_twin, ...), custom_call_target="tpu_custom_call" | custom-call | flops 134578176 | bytes 1048576 | tf_op jit(solution)/shard_map/pallas_call | solution.py:218
  28.6 0.0 collective-permute-done.14.twin
  28.6 1.4 %shard_map.68 = (f32[296,128]{1,0:T(8,128)}, bf16[2,896,296]{2,1,0:T(8,128)(2,1)S(1)}) custom-call(bf16[4,128,888]{2,1,0:T(8,128)(2,1)S(1)} %shard_map.66.picked, f32[128,296]{1,0:T(8,128)S(1)} %get-tuple-element.19.before, bf16[296,296]{1,0:T(8,128)(2,1)S(1)} %get-tuple-element.20.c2e, ...), custom_call_target="tpu_custom_call", output_to_operand_aliasing={{1}: (4, {})} | custom-call | flops 269156352 | bytes 1048576 | tf_op jit(solution)/shard_map/pallas_call | solution.py:218
  (5 shorter events, 0.1 us)
Async XLA Ops:
  0.0 25.8 %copy-start.1 = (bf16[296,296]{1,0:T(8,128)(2,1)S(1)}, bf16[296,296]{1,0:T(8,128)(2,1)}, u32[]{:S(2)}) copy-start(bf16[296,296]{1,0:T(8,128)(2,1)} %c2e.1) | copy-start | bytes 525700
  0.0 25.8 %copy-start.3 = (s32[1,128,12]{1,0,2:T(1,128)S(1)}, s32[1,128,12]{1,0,2:T(1,128)}, u32[]{:S(2)}) copy-start(s32[1,128,12]{1,0,2:T(1,128)} %param.9) | copy-start | bytes 18436
  0.0 25.8 %copy-start.2 = (s32[1,128,12]{1,0,2:T(1,128)S(1)}, s32[1,128,12]{1,0,2:T(1,128)}, u32[]{:S(2)}) copy-start(s32[1,128,12]{1,0,2:T(1,128)} %param.8) | copy-start | bytes 18436
  0.0 25.8 %copy-start.4 = (s32[1,128]{1,0:T(1,128)S(1)}, s32[1,128]{1,0:T(1,128)}, u32[]{:S(2)}) copy-start(s32[1,128]{1,0:T(1,128)} %counts.1) | copy-start | bytes 1540
  0.0 15.8 %collective-permute-start.1 = (bf16[296,128]{1,0:T(8,128)(2,1)}, bf16[296,128]{1,0:T(8,128)(2,1)S(1)}, u32[]{:S(2)}, u32[]{:S(2)}) collective-permute-start(bf16[296,128]{1,0:T(8,128)(2,1)} %bitcast.13), channel_id=1, source_target_pairs={{0,28},{28,0},{4,8},{8,4},{12,16},{16,12},{20,24},{24,20},{1,29},{... | collective-permute-start | bytes 227336 | tf_op jit(solution)/shard_map/ppermute | solution.py:245
  3.4 12.3 %collective-permute-start = (bf16[296,128]{1,0:T(8,128)(2,1)}, bf16[296,128]{1,0:T(8,128)(2,1)S(1)}, u32[]{:S(2)}, u32[]{:S(2)}) collective-permute-start(bf16[296,128]{1,0:T(8,128)(2,1)} %bitcast.14), channel_id=1, source_target_pairs={{0,4},{4,0},{8,12},{12,8},{16,20},{20,16},{24,28},{28,24},{1,5},{5... | collective-permute-start | bytes 227336 | tf_op jit(solution)/shard_map/ppermute | solution.py:244
  4.7 10.2 %collective-permute-start.7 = (bf16[1,272,128]{2,1,0:T(8,128)(2,1)S(1)}, bf16[1,272,128]{2,1,0:T(8,128)(2,1)S(1)}, u32[]{:S(2)}, u32[]{:S(2)}) collective-permute-start(bf16[1,272,128]{2,1,0:T(8,128)(2,1)S(1)} %get-tuple-element.18), channel_id=1, source_target_pairs={{0,3},{1,2},{2,1},{3,0},{4,7},{5,6},{6,5},{7,4},{8,11},{9,10},{10,... | collective-permute-start | bytes 208904 | tf_op jit(solution)/shard_map/ppermute | solution.py:249
  8.3 6.5 %collective-permute-start.6 = (bf16[1,272,128]{2,1,0:T(8,128)(2,1)S(1)}, bf16[1,272,128]{2,1,0:T(8,128)(2,1)S(1)}, u32[]{:S(2)}, u32[]{:S(2)}) collective-permute-start(bf16[1,272,128]{2,1,0:T(8,128)(2,1)S(1)} %get-tuple-element.18), channel_id=1, source_target_pairs={{0,2},{1,3},{2,0},{3,1},{4,6},{5,7},{6,4},{7,5},{8,10},{9,11},{10,... | collective-permute-start | bytes 208904 | tf_op jit(solution)/shard_map/ppermute | solution.py:249
  8.3 10.2 %collective-permute-start.4 = (bf16[1,1056,128]{2,1,0:T(8,128)(2,1)S(1)}, bf16[1,1056,128]{2,1,0:T(8,128)(2,1)S(1)}, u32[]{:S(2)}, u32[]{:S(2)}) collective-permute-start(bf16[1,1056,128]{2,1,0:T(8,128)(2,1)S(1)} %get-tuple-element.17), channel_id=1, source_target_pairs={{0,1},{1,0},{2,3},{3,2},{4,5},{5,4},{6,7},{7,6},{8,9},{9,8},{10,11... | collective-permute-start | bytes 811016 | tf_op jit(solution)/shard_map/ppermute | solution.py:250
  14.9 5.2 %collective-permute-start.8 = (bf16[2,272,128]{2,1,0:T(8,128)(2,1)S(1)}, bf16[2,272,128]{2,1,0:T(8,128)(2,1)S(1)}, u32[]{:S(2)}, u32[]{:S(2)}) collective-permute-start(bf16[2,272,128]{2,1,0:T(8,128)(2,1)S(1)} %constant_dynamic-update-slice_fusion.3.refs_0_), channel_id=1, source_target_pairs={{0,8},{4,12},{8,0},{12,4},{16,24},{20,28},{24,16},{28,20},{1,9},{5... | collective-permute-start | bytes 417800 | tf_op jit(solution)/shard_map/ppermute | solution.py:256
  15.8 8.1 %collective-permute-start.3 = (bf16[888,128]{1,0:T(8,128)(2,1)S(1)}, bf16[888,128]{1,0:T(8,128)(2,1)S(1)}, u32[]{:S(2)}, u32[]{:S(2)}) collective-permute-start(bf16[888,128]{1,0:T(8,128)(2,1)S(1)} %constant_dynamic-update-slice_fusion.column), channel_id=1, source_target_pairs={{0,4},{3,7},{4,0},{7,3},{8,12},{11,15},{12,8},{15,11},{16,20},{19,... | collective-permute-start | bytes 681992 | tf_op jit(solution)/shard_map/ppermute | solution.py:248
  15.9 8.6 %collective-permute-start.2 = (bf16[888,128]{1,0:T(8,128)(2,1)S(1)}, bf16[888,128]{1,0:T(8,128)(2,1)S(1)}, u32[]{:S(2)}, u32[]{:S(2)}) collective-permute-start(bf16[888,128]{1,0:T(8,128)(2,1)S(1)} %constant_dynamic-update-slice_fusion.column), channel_id=1, source_target_pairs={{0,1},{1,0},{2,3},{3,2},{4,5},{5,4},{6,7},{7,6},{8,9},{9,8},{10,11... | collective-permute-start | bytes 681992 | tf_op jit(solution)/shard_map/ppermute | solution.py:247
  17.8 6.2 %collective-permute-start.9 = (bf16[2,272,128]{2,1,0:T(8,128)(2,1)S(1)}, bf16[2,272,128]{2,1,0:T(8,128)(2,1)S(1)}, u32[]{:S(2)}, u32[]{:S(2)}) collective-permute-start(bf16[2,272,128]{2,1,0:T(8,128)(2,1)S(1)} %constant_dynamic-update-slice_fusion.3.refs_0_), channel_id=1, source_target_pairs={{0,16},{4,20},{8,24},{12,28},{16,0},{20,4},{24,8},{28,12},{1,17},{... | collective-permute-start | bytes 417800 | tf_op jit(solution)/shard_map/ppermute | solution.py:256
  18.6 9.3 %collective-permute-start.5 = (bf16[1,1056,128]{2,1,0:T(8,128)(2,1)S(1)}, bf16[1,1056,128]{2,1,0:T(8,128)(2,1)S(1)}, u32[]{:S(2)}, u32[]{:S(2)}) collective-permute-start(bf16[1,1056,128]{2,1,0:T(8,128)(2,1)S(1)} %collective-permute-done.4.close), channel_id=1, source_target_pairs={{0,4},{4,0},{8,12},{12,8},{16,20},{20,16},{24,28},{28,24},{1,5},{5... | collective-permute-start | bytes 811016 | tf_op jit(solution)/shard_map/ppermute | solution.py:257
  20.1 5.7 %collective-permute-start.10 = (bf16[2,272,128]{2,1,0:T(8,128)(2,1)S(1)}, bf16[2,272,128]{2,1,0:T(8,128)(2,1)S(1)}, u32[]{:S(2)}, u32[]{:S(2)}) collective-permute-start(bf16[2,272,128]{2,1,0:T(8,128)(2,1)S(1)} %collective-permute-done.8.refs_1_), channel_id=1, source_target_pairs={{0,16},{4,20},{8,24},{12,28},{16,0},{20,4},{24,8},{28,12},{1,17},{... | collective-permute-start | bytes 417800 | tf_op jit(solution)/shard_map/ppermute | solution.py:256
  24.0 3.8 %collective-permute-start.11 = (bf16[2,272,128]{2,1,0:T(8,128)(2,1)S(1)}, bf16[2,272,128]{2,1,0:T(8,128)(2,1)S(1)}, u32[]{:S(2)}, u32[]{:S(2)}) collective-permute-start(bf16[2,272,128]{2,1,0:T(8,128)(2,1)S(1)} %constant_dynamic-update-slice_fusion.3.refs_0_), channel_id=1, source_target_pairs={{0,4},{4,0},{8,12},{12,8},{16,20},{20,16},{24,28},{28,24},{1,5},{5... | collective-permute-start | bytes 417800 | tf_op jit(solution)/shard_map/ppermute | solution.py:258
  24.0 3.8 %collective-permute-start.13 = (bf16[2,272,128]{2,1,0:T(8,128)(2,1)S(1)}, bf16[2,272,128]{2,1,0:T(8,128)(2,1)S(1)}, u32[]{:S(2)}, u32[]{:S(2)}) collective-permute-start(bf16[2,272,128]{2,1,0:T(8,128)(2,1)S(1)} %collective-permute-done.9.refs_2_), channel_id=1, source_target_pairs={{0,4},{4,0},{8,12},{12,8},{16,20},{20,16},{24,28},{28,24},{1,5},{5... | collective-permute-start | bytes 417800 | tf_op jit(solution)/shard_map/ppermute | solution.py:258
  24.5 3.3 %collective-permute-start.12 = (bf16[2,272,128]{2,1,0:T(8,128)(2,1)S(1)}, bf16[2,272,128]{2,1,0:T(8,128)(2,1)S(1)}, u32[]{:S(2)}, u32[]{:S(2)}) collective-permute-start(bf16[2,272,128]{2,1,0:T(8,128)(2,1)S(1)} %collective-permute-done.8.refs_1_), channel_id=1, source_target_pairs={{0,4},{4,0},{8,12},{12,8},{16,20},{20,16},{24,28},{28,24},{1,5},{5... | collective-permute-start | bytes 417800 | tf_op jit(solution)/shard_map/ppermute | solution.py:258
  25.8 2.8 %collective-permute-start.14 = (bf16[2,272,128]{2,1,0:T(8,128)(2,1)S(1)}, bf16[2,272,128]{2,1,0:T(8,128)(2,1)S(1)}, u32[]{:S(2)}, u32[]{:S(2)}) collective-permute-start(bf16[2,272,128]{2,1,0:T(8,128)(2,1)S(1)} %collective-permute-done.10.refs_3_), channel_id=1, source_target_pairs={{0,4},{4,0},{8,12},{12,8},{16,20},{20,16},{24,28},{28,24},{1,5},{5... | collective-permute-start | bytes 417800 | tf_op jit(solution)/shard_map/ppermute | solution.py:258
  26.7 1.2 %copy-start = (bf16[3,296,296]{2,1,0:T(8,128)(2,1)S(1)}, bf16[3,296,296]{2,1,0:T(8,128)(2,1)}, u32[]{:S(2)}) copy-start(bf16[3,296,296]{2,1,0:T(8,128)(2,1)} %param.10) | copy-start | bytes 1577092

commit v7 on v6

--- a/solution.py
+++ b/solution.py
@@ -92,17 +92,30 @@
             buffer[spot, 128 * full :] = part[full * size : full * size + count, f * tail : (f + 1) * tail]
 
 
-def prep_kernel(flat, block, small, mid, block_out, small_raw, mid_raw, sems):
+def prep_kernel(flat, block, small, flat_out, block_out, raw, sems):
     seg_id = lax.axis_index("morton")
-    jobs = ((small_raw, seg_id, sems.at[0]), (mid_raw, seg_id % 2, sems.at[1]))
-    whole = pltpu.make_async_copy(block, block_out, sems.at[2])
-    for raw, index, sem in jobs:
-        copy_part(flat, raw, raw.shape[0], index, sem, "start")
-    whole.start()
-    for (raw, index, sem), out in zip(jobs, (small, mid)):
-        copy_part(flat, raw, raw.shape[0], index, sem, "wait")
-        pack(out.at[0], raw[...])
-    whole.wait()
+    wholes = [pltpu.make_async_copy(flat, flat_out, sems.at[1]), pltpu.make_async_copy(block, block_out, sems.at[2])]
+    copy_part(flat, raw, raw.shape[0], seg_id, sems.at[0], "start")
+    for whole in wholes:
+        whole.start()
+    copy_part(flat, raw, raw.shape[0], seg_id, sems.at[0], "wait")
+    pack(small.at[0], raw[...])
+    for whole in wholes:
+        whole.wait()
+
+
+def half_kernel(size, flat, mid):
+    rows = flat.shape[0]
+
+    def move(start, count):
+        part = flat[start : start + count, :]
+        if count < size:
+            part = jnp.concatenate([part, jnp.zeros((size - count, flat.shape[1]), flat.dtype)], axis=0)
+        pack(mid.at[0], part)
+
+    core = lax.axis_index("morton") % 2
+    pl.when(core == 0)(lambda: move(0, size))
+    pl.when(core == 1)(lambda: move(size, rows - size))
 
 
 def side_tables(refs, width):
@@ -226,20 +239,21 @@
             cost_estimate=pl.CostEstimate(flops=flops, bytes_accessed=1 << 20, transcendentals=0),
         )(*args)
 
-    small, mid, block_near = call(
+    small, flat_near, block_near = call(
         prep_kernel,
         (
             jax.ShapeDtypeStruct((1, packed_rows(width, eighth), 128), operators.dtype),
-            jax.ShapeDtypeStruct((1, packed_rows(width, quarter), 128), operators.dtype),
+            jax.ShapeDtypeStruct(flat.shape, flat.dtype),
             jax.ShapeDtypeStruct(block.shape, block.dtype),
         ),
-        (pltpu.with_memory_space_constraint(flat, pltpu.HBM), pltpu.with_memory_space_constraint(block, pltpu.HBM)),
-        specs=[hbm, hbm],
-        scratch=[
-            pltpu.VMEM((eighth, width), operators.dtype),
-            pltpu.VMEM((quarter, width), operators.dtype),
-            pltpu.SemaphoreType.DMA((3,)),
-        ],
+        [pltpu.with_memory_space_constraint(x, pltpu.HBM) for x in (flat, block)],
+        specs=[hbm] * 2,
+        scratch=[pltpu.VMEM((eighth, width), operators.dtype), pltpu.SemaphoreType.DMA((3,))],
+    )
+    mid = call(
+        functools.partial(half_kernel, quarter),
+        jax.ShapeDtypeStruct((1, packed_rows(width, quarter), 128), operators.dtype),
+        (flat_near,),
     )
     twin = lax.ppermute(block, "morton", pairs_xor(segs, 1))
     other = lax.ppermute(block, "morton", pairs_odd(segs))
@@ -250,10 +264,13 @@
     close = lax.ppermute(mid, "lane", pairs_xor(lanes, 1))
 
     landed = jnp.concatenate(landed, axis=0)
-    pieces = [landed]
-    while len(pieces) < segs // 2:
-        step = len(pieces)
-        pieces += [lax.ppermute(piece, "morton", pairs_xor(segs, 2 * step)) for piece in pieces]
+    found = {0: landed}
+    step = segs // 4
+    while step:
+        for j, piece in list(found.items()):
+            found[j + step] = lax.ppermute(piece, "morton", pairs_xor(segs, 2 * step))
+        step //= 2
+    pieces = [found[j] for j in range(segs // 2)]
     close_twin = lax.ppermute(close, "morton", pairs_xor(segs, 1))
     twins = [lax.ppermute(piece, "morton", pairs_xor(segs, 1)) for piece in pieces]
 
@@ -281,7 +298,7 @@
     before, buffer_mid = call(
         functools.partial(mid_kernel, len(pieces), quarter, eighth),
         (sums, buffer),
-        (picked, flat, close, close_twin, *pieces, *twins[:early]),
+        (picked, flat_near, close, close_twin, *pieces, *twins[:early]),
         scratch=[pltpu.VMEM((2 * quarter, width), jnp.bfloat16)],
         flops=4 * boxes * rows * width,
     )

time: 30.2 us -> 29.8 us (0.987)
  starting transfers between devices: 12.6 us -> 11 us
  waiting for transfers between devices: 11.9 us -> 13.1 us
    ppermute x1, waiting for transfers between devices: 0.28 us -> 2.08 us  [per_device(): close = lax.ppermute(mid, 'lane', pairs_xor(lanes, 1))]
    ppermute x3, starting transfers between devices: 2.21 us -> 1.1 us  [per_device(): found[j + step] = lax.ppermute(piece, 'morton', pairs_xor(segs, 2 * step))]
    ppermute x1, starting transfers between devices: 1.86 us -> 0.93 us  [per_device(): near = lax.ppermute(column, 'lane', pairs_xor(lanes, 1))]
    ppermute x2, waiting for transfers between devices: 5.75 us -> 5.1 us  [per_device(): lax.ppermute(small, 'lane', pairs_xor(lanes, k))]
    ppermute x1, starting transfers between devices: 0.01 us -> 0.57 us  [per_device(): twin = lax.ppermute(block, 'morton', pairs_xor(segs, 1))]
    ppermute x1, starting transfers between devices: 0.78 us -> 0.3 us  [per_device(): close = lax.ppermute(mid, 'lane', pairs_xor(lanes, 1))]
    ppermute x2, starting transfers between devices: 3.67 us -> 4 us  [per_device(): lax.ppermute(small, 'lane', pairs_xor(lanes, k))]
    pallas_call x5 -> x6, Pallas kernels: 5.29 us -> 5.37 us  [call(): pl.pallas_call(kernel, out_shape=out, in_specs=specs or [vmem] * len(args...]
  transfers between devices with their start and end apart: 15 -> 15, of which waited for: 5 -> 6; matrix products, arithmetic and copies ran while one was open for 0% -> 0% of each run, Pallas kernels for 13% -> 13%
where the time goes in v7:
time: 29.8 us; the launch traced here: 29.7 us
  waiting for transfers between devices  13.1 us (44%)
  starting transfers between devices  11 us (37%)
  Pallas kernels  5.37 us (18%)
    ppermute x3, waiting for transfers between devices, per_device(): found[j + step] = lax.ppermute(piece, 'morton', pairs_xor(segs, 2 * step))  5.87 us
    pallas_call x6, Pallas kernels, call(): pl.pallas_call(kernel, out_shape=out, in_specs=specs or [vmem] * len(args...  5.37 us
    ppermute x2, waiting for transfers between devices, per_device(): lax.ppermute(small, 'lane', pairs_xor(lanes, k))  5.1 us
    ppermute x2, starting transfers between devices, per_device(): lax.ppermute(small, 'lane', pairs_xor(lanes, k))  4 us
    ppermute x1, starting transfers between devices, per_device(): other = lax.ppermute(block, 'morton', pairs_odd(segs))  3.54 us
    ppermute x1, waiting for transfers between devices, per_device(): close = lax.ppermute(mid, 'lane', pairs_xor(lanes, 1))  2.08 us
    ppermute x3, starting transfers between devices, per_device(): found[j + step] = lax.ppermute(piece, 'morton', pairs_xor(segs, 2 * step))  1.1 us
    ppermute x1, starting transfers between devices, per_device(): near = lax.ppermute(column, 'lane', pairs_xor(lanes, 1))  0.93 us
  transfers between devices with their start and end apart: 15, of which 6 were waited for; matrix products, arithmetic and copies ran while one was open for 0% of the time, Pallas kernels for 13%

profile of v7, /device:TPU:0, one launch (start us, length us, event | category | flops | bytes accessed | tf_op | source)
XLA Modules:
  0.0 29.7 jit_solution(5370262740243951935)
XLA Ops:
  0.0 0.0 copy-start.1
  0.0 0.0 copy-start.2
  0.0 0.0 copy-start
  0.0 0.0 copy-start.3
  0.0 0.6 %collective-permute-start = (bf16[296,128]{1,0:T(8,128)(2,1)}, bf16[296,128]{1,0:T(8,128)(2,1)S(1)}, u32[]{:S(2)}, u32[]{:S(2)}) collective-permute-start(bf16[296,128]{1,0:T(8,128)(2,1)} %bitcast.12), channel_id=1, source_target_pairs={{0,4},{4,0},{8,12},{12,8},{16,20},{20,16},{24,28},{28,24},{1,5},{5... | collective-permute-start | bytes 227336 | tf_op jit(solution)/shard_map/ppermute | solution.py:258
  0.6 3.5 %collective-permute-start.1 = (bf16[296,128]{1,0:T(8,128)(2,1)}, bf16[296,128]{1,0:T(8,128)(2,1)S(1)}, u32[]{:S(2)}, u32[]{:S(2)}) collective-permute-start(bf16[296,128]{1,0:T(8,128)(2,1)} %bitcast.13), channel_id=1, source_target_pairs={{0,28},{28,0},{4,8},{8,4},{12,16},{16,12},{20,24},{24,20},{1,29},{... | collective-permute-start | bytes 227336 | tf_op jit(solution)/shard_map/ppermute | solution.py:259
  4.1 1.2 %shard_map.64 = (bf16[1,272,128]{2,1,0:T(8,128)(2,1)S(1)}, bf16[888,296]{1,0:T(8,128)(2,1)S(1)}, bf16[296,128]{1,0:T(8,128)(2,1)S(1)}) custom-call(bf16[888,296]{1,0:T(8,128)(2,1)} %bitcast.11, bf16[296,128]{1,0:T(8,128)(2,1)} %bitcast.14), custom_call_target="tpu_custom_call" | custom-call | bytes 1048576 | tf_op jit(solution)/shard_map/pallas_call | solution.py:231
  5.3 2.7 %collective-permute-start.6 = (bf16[1,272,128]{2,1,0:T(8,128)(2,1)S(1)}, bf16[1,272,128]{2,1,0:T(8,128)(2,1)S(1)}, u32[]{:S(2)}, u32[]{:S(2)}) collective-permute-start(bf16[1,272,128]{2,1,0:T(8,128)(2,1)S(1)} %get-tuple-element.18), channel_id=1, source_target_pairs={{0,2},{1,3},{2,0},{3,1},{4,6},{5,7},{6,4},{7,5},{8,10},{9,11},{10,... | collective-permute-start | bytes 208904 | tf_op jit(solution)/shard_map/ppermute | solution.py:263
  8.0 1.3 %collective-permute-start.7 = (bf16[1,272,128]{2,1,0:T(8,128)(2,1)S(1)}, bf16[1,272,128]{2,1,0:T(8,128)(2,1)S(1)}, u32[]{:S(2)}, u32[]{:S(2)}) collective-permute-start(bf16[1,272,128]{2,1,0:T(8,128)(2,1)S(1)} %get-tuple-element.18), channel_id=1, source_target_pairs={{0,3},{1,2},{2,1},{3,0},{4,7},{5,6},{6,5},{7,4},{8,11},{9,10},{10,... | collective-permute-start | bytes 208904 | tf_op jit(solution)/shard_map/ppermute | solution.py:263
  9.3 0.1 shard_map.67
  9.4 0.3 collective-permute-start.4
  9.7 1.0 %collective-permute-done.6 = bf16[1,272,128]{2,1,0:T(8,128)(2,1)S(1)} collective-permute-done((bf16[1,272,128]{2,1,0:T(8,128)(2,1)S(1)}, bf16[1,272,128]{2,1,0:T(8,128)(2,1)S(1)}, u32[]{:S(2)}, u32[]{:S(2)}) %collective-permute-start.6) | collective-permute-done | bytes 69664 | tf_op jit(solution)/shard_map/ppermute | solution.py:263
  10.8 4.1 %collective-permute-done.7 = bf16[1,272,128]{2,1,0:T(8,128)(2,1)S(1)} collective-permute-done((bf16[1,272,128]{2,1,0:T(8,128)(2,1)S(1)}, bf16[1,272,128]{2,1,0:T(8,128)(2,1)S(1)}, u32[]{:S(2)}, u32[]{:S(2)}) %collective-permute-start.7) | collective-permute-done | bytes 69664 | tf_op jit(solution)/shard_map/ppermute | solution.py:263
  14.9 0.6 %collective-permute-start.9 = (bf16[2,272,128]{2,1,0:T(8,128)(2,1)S(1)}, bf16[2,272,128]{2,1,0:T(8,128)(2,1)S(1)}, u32[]{:S(2)}, u32[]{:S(2)}) collective-permute-start(bf16[2,272,128]{2,1,0:T(8,128)(2,1)S(1)} %constant_dynamic-update-slice_fusion.3.refs_0_), channel_id=1, source_target_pairs={{0,16},{4,20},{8,24},{12,28},{16,0},{20,4},{24,8},{28,12},{1,17},{... | collective-permute-start | bytes 417800 | tf_op jit(solution)/shard_map/ppermute | solution.py:271
  15.4 0.0 collective-permute-done
  15.5 0.0 collective-permute-done.1
  15.5 0.9 %collective-permute-start.2 = (bf16[888,128]{1,0:T(8,128)(2,1)S(1)}, bf16[888,128]{1,0:T(8,128)(2,1)S(1)}, u32[]{:S(2)}, u32[]{:S(2)}) collective-permute-start(bf16[888,128]{1,0:T(8,128)(2,1)S(1)} %constant_dynamic-update-slice_fusion.column), channel_id=1, source_target_pairs={{0,1},{1,0},{2,3},{3,2},{4,5},{5,4},{6,7},{7,6},{8,9},{9,8},{10,11... | collective-permute-start | bytes 681992 | tf_op jit(solution)/shard_map/ppermute | solution.py:261
  16.4 0.0 collective-permute-start.3
  16.4 0.5 %collective-permute-start.8 = (bf16[2,272,128]{2,1,0:T(8,128)(2,1)S(1)}, bf16[2,272,128]{2,1,0:T(8,128)(2,1)S(1)}, u32[]{:S(2)}, u32[]{:S(2)}) collective-permute-start(bf16[2,272,128]{2,1,0:T(8,128)(2,1)S(1)} %constant_dynamic-update-slice_fusion.3.refs_0_), channel_id=1, source_target_pairs={{0,8},{4,12},{8,0},{12,4},{16,24},{20,28},{24,16},{28,20},{1,9},{5... | collective-permute-start | bytes 417800 | tf_op jit(solution)/shard_map/ppermute | solution.py:271
  17.0 2.1 %collective-permute-done.4.close = bf16[1,1056,128]{2,1,0:T(8,128)(2,1)S(1)} collective-permute-done((bf16[1,1056,128]{2,1,0:T(8,128)(2,1)S(1)}, bf16[1,1056,128]{2,1,0:T(8,128)(2,1)S(1)}, u32[]{:S(2)}, u32[]{:S(2)}) %collective-permute-start.4) | collective-permute-done | bytes 270368 | tf_op jit(solution)/shard_map/ppermute | solution.py:264
  19.0 0.0 collective-permute-start.5
  19.0 1.0 %collective-permute-done.9.refs_2_ = bf16[2,272,128]{2,1,0:T(8,128)(2,1)S(1)} collective-permute-done((bf16[2,272,128]{2,1,0:T(8,128)(2,1)S(1)}, bf16[2,272,128]{2,1,0:T(8,128)(2,1)S(1)}, u32[]{:S(2)}, u32[]{:S(2)}) %collective-permute-start.9) | collective-permute-done | bytes 139296 | tf_op jit(solution)/shard_map/ppermute | solution.py:271
  20.0 0.0 collective-permute-start.10
  20.0 2.9 %collective-permute-done.8.refs_1_ = bf16[2,272,128]{2,1,0:T(8,128)(2,1)S(1)} collective-permute-done((bf16[2,272,128]{2,1,0:T(8,128)(2,1)S(1)}, bf16[2,272,128]{2,1,0:T(8,128)(2,1)S(1)}, u32[]{:S(2)}, u32[]{:S(2)}) %collective-permute-start.8) | collective-permute-done | bytes 139296 | tf_op jit(solution)/shard_map/ppermute | solution.py:271
  22.9 0.0 collective-permute-start.11
  22.9 0.0 collective-permute-done.2.near
  22.9 0.5 %collective-permute-start.13 = (bf16[2,272,128]{2,1,0:T(8,128)(2,1)S(1)}, bf16[2,272,128]{2,1,0:T(8,128)(2,1)S(1)}, u32[]{:S(2)}, u32[]{:S(2)}) collective-permute-start(bf16[2,272,128]{2,1,0:T(8,128)(2,1)S(1)} %collective-permute-done.9.refs_2_), channel_id=1, source_target_pairs={{0,4},{4,0},{8,12},{12,8},{16,20},{20,16},{24,28},{28,24},{1,5},{5... | collective-permute-start | bytes 417800 | tf_op jit(solution)/shard_map/ppermute | solution.py:275
  23.4 0.0 collective-permute-done.3.far
  23.4 0.1 collective-permute-start.12
  23.5 2.0 %collective-permute-done.10.refs_3_ = bf16[2,272,128]{2,1,0:T(8,128)(2,1)S(1)} collective-permute-done((bf16[2,272,128]{2,1,0:T(8,128)(2,1)S(1)}, bf16[2,272,128]{2,1,0:T(8,128)(2,1)S(1)}, u32[]{:S(2)}, u32[]{:S(2)}) %collective-permute-start.10) | collective-permute-done | bytes 139296 | tf_op jit(solution)/shard_map/ppermute | solution.py:271
  25.5 0.0 collective-permute-start.14
  25.5 0.0 copy-done.1
  25.5 0.0 copy-done.2
  25.5 0.0 copy-done
  25.5 0.0 copy-done.3
  25.5 0.8 %shard_map.65 = (bf16[12,296,128]{2,1,0:T(8,128)(2,1)S(1)}, s32[12,128]{1,0:T(8,128)S(1)}, bf16[296,296]{1,0:T(8,128)(2,1)S(1)}) custom-call(s32[1,128]{1,0:T(1,128)S(1)} %copy-done.3, s32[12,1,128]{2,1,0:T(1,128)S(1)} %bitcast.9, s32[12,1,128]{2,1,0:T(1,128)S(1)} %bitcast.10, bf16[888,128]{1,0:T(8,128)(2,1)S(1)} %constant_dynamic-update-slice_fusion.column, ...), custom_call_target="tpu_custom_call" | custom-call | flops 349175808 | bytes 1048576 | tf_op jit(solution)/shard_map/pallas_call | solution.py:231
  26.3 1.1 %shard_map.66.picked = bf16[4,128,888]{2,1,0:T(8,128)(2,1)S(1)} custom-call(s32[12,128]{1,0:T(8,128)S(1)} %get-tuple-element.15.index, bf16[12,296,128]{2,1,0:T(8,128)(2,1)S(1)} %get-tuple-element.16.part, bf16[888,128]{1,0:T(8,128)(2,1)S(1)} %collective-permute-done.2.near, bf16[888,128]{1,0:T(8,128)(2,1)S(1)} %collective-permute-done.3.far), custom_call_target="tpu_custom_call" | custom-call | flops 698351616 | bytes 1048576 | tf_op jit(solution)/shard_map/pallas_call | solution.py:231
  27.5 0.0 collective-permute-done.11.refs_4_
  27.5 0.0 collective-permute-done.13.refs_6_
  27.5 0.0 collective-permute-done.12.refs_5_
  27.5 0.0 collective-permute-done.5.close_twin
  27.5 0.7 %shard_map.68 = (f32[128,296]{1,0:T(8,128)S(1)}, bf16[2,896,296]{2,1,0:T(8,128)(2,1)S(1)}) custom-call(bf16[4,128,888]{2,1,0:T(8,128)(2,1)S(1)} %shard_map.66.picked, bf16[888,296]{1,0:T(8,128)(2,1)S(1)} %get-tuple-element.17.flat.own, bf16[1,1056,128]{2,1,0:T(8,128)(2,1)S(1)} %collective-permute-done.4.close, ...), custom_call_target="tpu_custom_call" | custom-call | flops 134578176 | bytes 1048576 | tf_op jit(solution)/shard_map/pallas_call | solution.py:231
  28.2 0.0 collective-permute-done.14.twin
  28.2 1.4 %shard_map.69 = (f32[296,128]{1,0:T(8,128)}, bf16[2,896,296]{2,1,0:T(8,128)(2,1)S(1)}) custom-call(bf16[4,128,888]{2,1,0:T(8,128)(2,1)S(1)} %shard_map.66.picked, f32[128,296]{1,0:T(8,128)S(1)} %get-tuple-element.19.before, bf16[296,296]{1,0:T(8,128)(2,1)S(1)} %get-tuple-element.20.c2e, ...), custom_call_target="tpu_custom_call", output_to_operand_aliasing={{1}: (4, {})} | custom-call | flops 269156352 | bytes 1048576 | tf_op jit(solution)/shard_map/pallas_call | solution.py:231
  (5 shorter events, 0.1 us)
Async XLA Ops:
  0.0 25.5 %copy-start.1 = (s32[1,128,12]{1,0,2:T(1,128)S(1)}, s32[1,128,12]{1,0,2:T(1,128)}, u32[]{:S(2)}) copy-start(s32[1,128,12]{1,0,2:T(1,128)} %param.8) | copy-start | bytes 18436
  0.0 25.5 %copy-start.2 = (s32[1,128,12]{1,0,2:T(1,128)S(1)}, s32[1,128,12]{1,0,2:T(1,128)}, u32[]{:S(2)}) copy-start(s32[1,128,12]{1,0,2:T(1,128)} %param.9) | copy-start | bytes 18436
  0.0 25.5 %copy-start = (bf16[296,296]{1,0:T(8,128)(2,1)S(1)}, bf16[296,296]{1,0:T(8,128)(2,1)}, u32[]{:S(2)}) copy-start(bf16[296,296]{1,0:T(8,128)(2,1)} %c2e.1) | copy-start | bytes 525700
  0.0 25.5 %copy-start.3 = (s32[1,128]{1,0:T(1,128)S(1)}, s32[1,128]{1,0:T(1,128)}, u32[]{:S(2)}) copy-start(s32[1,128]{1,0:T(1,128)} %counts.1) | copy-start | bytes 1540
  0.0 15.4 %collective-permute-start = (bf16[296,128]{1,0:T(8,128)(2,1)}, bf16[296,128]{1,0:T(8,128)(2,1)S(1)}, u32[]{:S(2)}, u32[]{:S(2)}) collective-permute-start(bf16[296,128]{1,0:T(8,128)(2,1)} %bitcast.12), channel_id=1, source_target_pairs={{0,4},{4,0},{8,12},{12,8},{16,20},{20,16},{24,28},{28,24},{1,5},{5... | collective-permute-start | bytes 227336 | tf_op jit(solution)/shard_map/ppermute | solution.py:258
  0.6 14.9 %collective-permute-start.1 = (bf16[296,128]{1,0:T(8,128)(2,1)}, bf16[296,128]{1,0:T(8,128)(2,1)S(1)}, u32[]{:S(2)}, u32[]{:S(2)}) collective-permute-start(bf16[296,128]{1,0:T(8,128)(2,1)} %bitcast.13), channel_id=1, source_target_pairs={{0,28},{28,0},{4,8},{8,4},{12,16},{16,12},{20,24},{24,20},{1,29},{... | collective-permute-start | bytes 227336 | tf_op jit(solution)/shard_map/ppermute | solution.py:259
  5.3 5.4 %collective-permute-start.6 = (bf16[1,272,128]{2,1,0:T(8,128)(2,1)S(1)}, bf16[1,272,128]{2,1,0:T(8,128)(2,1)S(1)}, u32[]{:S(2)}, u32[]{:S(2)}) collective-permute-start(bf16[1,272,128]{2,1,0:T(8,128)(2,1)S(1)} %get-tuple-element.18), channel_id=1, source_target_pairs={{0,2},{1,3},{2,0},{3,1},{4,6},{5,7},{6,4},{7,5},{8,10},{9,11},{10,... | collective-permute-start | bytes 208904 | tf_op jit(solution)/shard_map/ppermute | solution.py:263
  8.0 6.9 %collective-permute-start.7 = (bf16[1,272,128]{2,1,0:T(8,128)(2,1)S(1)}, bf16[1,272,128]{2,1,0:T(8,128)(2,1)S(1)}, u32[]{:S(2)}, u32[]{:S(2)}) collective-permute-start(bf16[1,272,128]{2,1,0:T(8,128)(2,1)S(1)} %get-tuple-element.18), channel_id=1, source_target_pairs={{0,3},{1,2},{2,1},{3,0},{4,7},{5,6},{6,5},{7,4},{8,11},{9,10},{10,... | collective-permute-start | bytes 208904 | tf_op jit(solution)/shard_map/ppermute | solution.py:263
  9.4 9.6 %collective-permute-start.4 = (bf16[1,1056,128]{2,1,0:T(8,128)(2,1)S(1)}, bf16[1,1056,128]{2,1,0:T(8,128)(2,1)S(1)}, u32[]{:S(2)}, u32[]{:S(2)}) collective-permute-start(bf16[1,1056,128]{2,1,0:T(8,128)(2,1)S(1)} %shard_map.67), channel_id=1, source_target_pairs={{0,1},{1,0},{2,3},{3,2},{4,5},{5,4},{6,7},{7,6},{8,9},{9,8},{10,11... | collective-permute-start | bytes 811016 | tf_op jit(solution)/shard_map/ppermute | solution.py:264
  14.9 5.1 %collective-permute-start.9 = (bf16[2,272,128]{2,1,0:T(8,128)(2,1)S(1)}, bf16[2,272,128]{2,1,0:T(8,128)(2,1)S(1)}, u32[]{:S(2)}, u32[]{:S(2)}) collective-permute-start(bf16[2,272,128]{2,1,0:T(8,128)(2,1)S(1)} %constant_dynamic-update-slice_fusion.3.refs_0_), channel_id=1, source_target_pairs={{0,16},{4,20},{8,24},{12,28},{16,0},{20,4},{24,8},{28,12},{1,17},{... | collective-permute-start | bytes 417800 | tf_op jit(solution)/shard_map/ppermute | solution.py:271
  15.5 7.4 %collective-permute-start.2 = (bf16[888,128]{1,0:T(8,128)(2,1)S(1)}, bf16[888,128]{1,0:T(8,128)(2,1)S(1)}, u32[]{:S(2)}, u32[]{:S(2)}) collective-permute-start(bf16[888,128]{1,0:T(8,128)(2,1)S(1)} %constant_dynamic-update-slice_fusion.column), channel_id=1, source_target_pairs={{0,1},{1,0},{2,3},{3,2},{4,5},{5,4},{6,7},{7,6},{8,9},{9,8},{10,11... | collective-permute-start | bytes 681992 | tf_op jit(solution)/shard_map/ppermute | solution.py:261
  16.4 7.0 %collective-permute-start.3 = (bf16[888,128]{1,0:T(8,128)(2,1)S(1)}, bf16[888,128]{1,0:T(8,128)(2,1)S(1)}, u32[]{:S(2)}, u32[]{:S(2)}) collective-permute-start(bf16[888,128]{1,0:T(8,128)(2,1)S(1)} %constant_dynamic-update-slice_fusion.column), channel_id=1, source_target_pairs={{0,4},{3,7},{4,0},{7,3},{8,12},{11,15},{12,8},{15,11},{16,20},{19,... | collective-permute-start | bytes 681992 | tf_op jit(solution)/shard_map/ppermute | solution.py:262
  16.4 6.5 %collective-permute-start.8 = (bf16[2,272,128]{2,1,0:T(8,128)(2,1)S(1)}, bf16[2,272,128]{2,1,0:T(8,128)(2,1)S(1)}, u32[]{:S(2)}, u32[]{:S(2)}) collective-permute-start(bf16[2,272,128]{2,1,0:T(8,128)(2,1)S(1)} %constant_dynamic-update-slice_fusion.3.refs_0_), channel_id=1, source_target_pairs={{0,8},{4,12},{8,0},{12,4},{16,24},{20,28},{24,16},{28,20},{1,9},{5... | collective-permute-start | bytes 417800 | tf_op jit(solution)/shard_map/ppermute | solution.py:271
  19.0 8.5 %collective-permute-start.5 = (bf16[1,1056,128]{2,1,0:T(8,128)(2,1)S(1)}, bf16[1,1056,128]{2,1,0:T(8,128)(2,1)S(1)}, u32[]{:S(2)}, u32[]{:S(2)}) collective-permute-start(bf16[1,1056,128]{2,1,0:T(8,128)(2,1)S(1)} %collective-permute-done.4.close), channel_id=1, source_target_pairs={{0,4},{4,0},{8,12},{12,8},{16,20},{20,16},{24,28},{28,24},{1,5},{5... | collective-permute-start | bytes 811016 | tf_op jit(solution)/shard_map/ppermute | solution.py:274
  20.0 5.5 %collective-permute-start.10 = (bf16[2,272,128]{2,1,0:T(8,128)(2,1)S(1)}, bf16[2,272,128]{2,1,0:T(8,128)(2,1)S(1)}, u32[]{:S(2)}, u32[]{:S(2)}) collective-permute-start(bf16[2,272,128]{2,1,0:T(8,128)(2,1)S(1)} %collective-permute-done.9.refs_2_), channel_id=1, source_target_pairs={{0,8},{4,12},{8,0},{12,4},{16,24},{20,28},{24,16},{28,20},{1,9},{5... | collective-permute-start | bytes 417800 | tf_op jit(solution)/shard_map/ppermute | solution.py:271
  22.9 4.6 %collective-permute-start.11 = (bf16[2,272,128]{2,1,0:T(8,128)(2,1)S(1)}, bf16[2,272,128]{2,1,0:T(8,128)(2,1)S(1)}, u32[]{:S(2)}, u32[]{:S(2)}) collective-permute-start(bf16[2,272,128]{2,1,0:T(8,128)(2,1)S(1)} %constant_dynamic-update-slice_fusion.3.refs_0_), channel_id=1, source_target_pairs={{0,4},{4,0},{8,12},{12,8},{16,20},{20,16},{24,28},{28,24},{1,5},{5... | collective-permute-start | bytes 417800 | tf_op jit(solution)/shard_map/ppermute | solution.py:275
  22.9 4.6 %collective-permute-start.13 = (bf16[2,272,128]{2,1,0:T(8,128)(2,1)S(1)}, bf16[2,272,128]{2,1,0:T(8,128)(2,1)S(1)}, u32[]{:S(2)}, u32[]{:S(2)}) collective-permute-start(bf16[2,272,128]{2,1,0:T(8,128)(2,1)S(1)} %collective-permute-done.9.refs_2_), channel_id=1, source_target_pairs={{0,4},{4,0},{8,12},{12,8},{16,20},{20,16},{24,28},{28,24},{1,5},{5... | collective-permute-start | bytes 417800 | tf_op jit(solution)/shard_map/ppermute | solution.py:275
  23.4 4.1 %collective-permute-start.12 = (bf16[2,272,128]{2,1,0:T(8,128)(2,1)S(1)}, bf16[2,272,128]{2,1,0:T(8,128)(2,1)S(1)}, u32[]{:S(2)}, u32[]{:S(2)}) collective-permute-start(bf16[2,272,128]{2,1,0:T(8,128)(2,1)S(1)} %collective-permute-done.8.refs_1_), channel_id=1, source_target_pairs={{0,4},{4,0},{8,12},{12,8},{16,20},{20,16},{24,28},{28,24},{1,5},{5... | collective-permute-start | bytes 417800 | tf_op jit(solution)/shard_map/ppermute | solution.py:275
  25.5 2.7 %collective-permute-start.14 = (bf16[2,272,128]{2,1,0:T(8,128)(2,1)S(1)}, bf16[2,272,128]{2,1,0:T(8,128)(2,1)S(1)}, u32[]{:S(2)}, u32[]{:S(2)}) collective-permute-start(bf16[2,272,128]{2,1,0:T(8,128)(2,1)S(1)} %collective-permute-done.10.refs_3_), channel_id=1, source_target_pairs={{0,4},{4,0},{8,12},{12,8},{16,20},{20,16},{24,28},{28,24},{1,5},{5... | collective-permute-start | bytes 417800 | tf_op jit(solution)/shard_map/ppermute | solution.py:275
